TPU v7x, 128 devices: a whole 4x4x4 slice. The times are simulated.
128 devices in a mesh: gx: 8 (over x, core), gy: 16 (over y, z).
Axes of the slice: x: 4, y: 4, z: 4, core: 2. Of those that a mesh axis runs over, the one named last changes fastest.
Arguments:
- positions: float32 [3, 32, 32, 32, 16], P(None, None, 'gx', 'gy'), may hold values from 0 to 8
- charges: float32 [32, 32, 32, 16], P(None, 'gx', 'gy'), may hold values from -4 to 4
- types: int32 [32, 32, 32, 16], P(None, 'gx', 'gy'), may hold values from 0 to 63
- counts: int32 [32, 32, 16], P('gx', 'gy'), may hold values from 20 to 32
- eps_type: float32 [64], replicated, may hold values from 0.05 to 0.5
- sig_type: float32 [64], replicated, may hold values from 1.5 to 3
Outputs:
- pair_force: float32 [3, 32, 32, 32, 16], P(None, None, 'gx', 'gy')
- mesh_force: float32 [3, 32, 32, 32, 16], P(None, None, 'gx', 'gy')
All inputs are finite; a program needn't handle non-finite values.
Results may differ from a plain program's by a relative error of at most 0.0003.
Values sent between devices are 32-bit elements; how exact they have to be, the bound alone decides.
No kernel may reach another device: no remote copies, remote signals or barrier semaphores. Data moves between devices by JAX's collectives and lax.ppermute only.
A program may use at most 256 MiB of HBM per device.

v0:
```python
import math

import jax
import jax.numpy as jnp
from jax import lax
from jax.sharding import PartitionSpec as P

CELL = 8


GEWALD = 0.7
HIGHEST = lax.Precision.HIGHEST


def extended(cells, sides, width):
    for axis, dim in sides:
        count = lax.axis_size(axis)
        head = lax.slice_in_dim(cells, 0, width, axis=dim)
        tail = lax.slice_in_dim(cells, cells.shape[dim] - width, cells.shape[dim], axis=dim)
        cells = jnp.concatenate(
            [
                lax.ppermute(tail, axis, [(i, (i + 1) % count) for i in range(count)]),
                cells,
                lax.ppermute(head, axis, [((i + 1) % count, i) for i in range(count)]),
            ],
            axis=dim,
        )
    return cells


def spline_weights(offsets):
    points = jnp.arange(CELL + 4).astype(offsets.dtype) - 2.0
    target_shape = (CELL + 4,) + (1,) * offsets.ndim
    spans = jnp.abs(offsets[None] - points.reshape(target_shape))
    inside_part = (4.0 - 6.0 * spans * spans + 3.0 * spans * spans * spans) / 6.0
    outside_part = (2.0 - spans) * (2.0 - spans) * (2.0 - spans) / 6.0
    return jnp.where(spans < 1.0, inside_part, jnp.where(spans < 2.0, outside_part, 0.0))


def pair_energy(squared, charge_prod, eps_prod, sigma):
    sigma_sq = sigma * sigma
    ratios = sigma_sq / (squared + sigma_sq)
    ratio_cube = ratios * ratios * ratios
    softened = jnp.sqrt(squared + 1.0)
    inside = (
        4.0 * eps_prod * (ratio_cube * ratio_cube - ratio_cube)
        + charge_prod * lax.erfc(GEWALD * softened) / softened
    )
    cutoff_square = float(CELL * CELL)
    fraction = 1.0 - squared / cutoff_square
    switch = jnp.where(squared < cutoff_square, fraction * fraction, 0.0)
    return switch * inside


def pair_slope(squared, charge_prod, eps_prod, sigma):
    return jax.grad(
        lambda squared_in: jnp.sum(pair_energy(squared_in, charge_prod, eps_prod, sigma))
    )(squared)


def cell_forces(padded):
    length_a = padded.shape[2] - 2
    length_b = padded.shape[3] - 2
    length_c = padded.shape[4] - 2
    centre = padded[:, :, 1 : 1 + length_a, 1 : 1 + length_b, 1 : 1 + length_c]
    totals = [jnp.zeros(centre.shape[1:], padded.dtype) for component in range(3)]
    for shift_a in (-1, 0, 1):
        for shift_b in (-1, 0, 1):
            for shift_c in (-1, 0, 1):
                partner = padded[
                    :,
                    :,
                    1 + shift_a : 1 + shift_a + length_a,
                    1 + shift_b : 1 + shift_b + length_b,
                    1 + shift_c : 1 + shift_c + length_c,
                ]
                shifts = (shift_a, shift_b, shift_c)
                separation = [
                    CELL * shifts[component] + partner[component][None] - centre[component][:, None]
                    for component in range(3)
                ]
                squared = (
                    separation[0] * separation[0]
                    + separation[1] * separation[1]
                    + separation[2] * separation[2]
                )
                derivative = pair_slope(
                    squared,
                    centre[3][:, None] * partner[3][None],
                    centre[4][:, None] * partner[4][None],
                    0.5 * (centre[5][:, None] + partner[5][None]),
                )
                totals = [
                    totals[component] + jnp.sum(2.0 * derivative * separation[component], axis=1)
                    for component in range(3)
                ]
    return jnp.stack(totals)


def fold_wrap(blocks):
    cell_count = blocks.shape[-2]
    first_half = blocks[..., :CELL]
    second_half = jnp.pad(blocks[..., CELL:], [(0, 0)] * (blocks.ndim - 1) + [(0, CELL - 4)])
    summed = (first_half + jnp.roll(second_half, 1, axis=-2)).reshape(
        blocks.shape[:-2] + (cell_count * CELL,)
    )
    return jnp.roll(summed, -2, axis=-1)


def fold_open(blocks):
    cell_count = blocks.shape[-2]
    first_half = blocks[..., :CELL]
    second_half = jnp.pad(blocks[..., CELL:], [(0, 0)] * (blocks.ndim - 1) + [(0, CELL - 4)])
    spacer = [(0, 0)] * (blocks.ndim - 2)
    summed = jnp.pad(first_half, spacer + [(0, 1), (0, 0)]) + jnp.pad(
        second_half, spacer + [(1, 0), (0, 0)]
    )
    return summed.reshape(blocks.shape[:-2] + ((cell_count + 1) * CELL,))


def windows_wrap(fields):
    cell_count = fields.shape[-1] // CELL
    leading = jnp.roll(fields, 2, axis=-1).reshape(fields.shape[:-1] + (cell_count, CELL))
    trailing = jnp.roll(leading, -1, axis=-2)[..., :4]
    return jnp.concatenate([leading, trailing], axis=-1)


def windows_open(fields, cell_count):
    leading = fields[..., : cell_count * CELL].reshape(fields.shape[:-1] + (cell_count, CELL))
    trailing = jnp.concatenate(
        [leading[..., 1:, :4], fields[..., cell_count * CELL :][..., None, :]], axis=-2
    )
    return jnp.concatenate([leading, trailing], axis=-1)


def interpolate(windowed, weight_x, weight_y, weight_z):
    reduced = jnp.einsum("dczbyax,xpabc->dzypabc", windowed, weight_x, precision=HIGHEST)
    reduced = jnp.einsum("dzypabc,ypabc->dzpabc", reduced, weight_y, precision=HIGHEST)
    return jnp.einsum("dzpabc,zpabc->dpabc", reduced, weight_z, precision=HIGHEST)


def folded(indices, length):
    return jnp.where(indices < length // 2, indices, indices - length)


def counting(length):
    return jnp.arange(length, dtype=jnp.int32)


def green(mode_x, mode_y, mode_z, length_x, length_y, length_z, normalize):
    freq_x = mode_x.astype(jnp.float32)
    freq_y = mode_y.astype(jnp.float32)
    freq_z = mode_z.astype(jnp.float32)
    wave_x = freq_x * (2.0 * math.pi / length_x)
    wave_y = freq_y * (2.0 * math.pi / length_y)
    wave_z = freq_z * (2.0 * math.pi / length_z)
    norm_sq = wave_x * wave_x + wave_y * wave_y + wave_z * wave_z
    shaped = jnp.sinc(freq_x / length_x) * jnp.sinc(freq_y / length_y) * jnp.sinc(freq_z / length_z)
    shaped = shaped * shaped
    shaped = shaped * shaped
    shaped = shaped * shaped
    safe_sq = jnp.where(norm_sq > 0.0, norm_sq, 1.0)
    values = jnp.where(
        norm_sq > 0.0,
        normalize
        * 4.0
        * math.pi
        * jnp.exp(-norm_sq / (4.0 * GEWALD * GEWALD))
        / (safe_sq * shaped),
        0.0,
    )
    return (values * wave_x, values * wave_y, values * wave_z)


def trig(modes, points, length):
    phases = modes[:, None] * points[None, :] % length
    angles = phases.astype(jnp.float32) * (2.0 * math.pi / length)
    return (jnp.cos(angles), jnp.sin(angles))


def transform(real_part, imag_part, cos_table, sin_table, pattern, direction):
    real_cos = jnp.einsum(pattern, real_part, cos_table, precision=HIGHEST)
    real_sin = jnp.einsum(pattern, real_part, sin_table, precision=HIGHEST)
    imag_cos = jnp.einsum(pattern, imag_part, cos_table, precision=HIGHEST)
    imag_sin = jnp.einsum(pattern, imag_part, sin_table, precision=HIGHEST)
    if direction < 0:
        return (real_cos + imag_sin, imag_cos - real_sin)
    return (real_cos - imag_sin, imag_cos + real_sin)


def field_parts(real_k, imag_k, waves):
    real_e = jnp.stack([component * imag_k for component in waves])
    imag_e = jnp.stack([-component * real_k for component in waves])
    return (real_e, imag_e)


def atom_table(positions, charges, types, counts, eps_type, sig_type):
    slot_count = charges.shape[0]
    occupied = (counting(slot_count)[:, None, None, None] < counts[None]).astype(charges.dtype)
    matches = (types[..., None] == counting(eps_type.shape[0])).astype(eps_type.dtype)
    epsilon = jnp.sum(matches * eps_type, axis=-1)
    sigmas = jnp.sum(matches * sig_type, axis=-1)
    atoms = jnp.concatenate(
        [positions, (charges * occupied)[None], (jnp.sqrt(epsilon) * occupied)[None], sigmas[None]],
        axis=0,
    )
    return (atoms, occupied)


def body(positions, charges, types, counts, eps_type, sig_type):
    atoms, occupied = atom_table(positions, charges, types, counts, eps_type, sig_type)
    slot_count, cells_x, cells_y, cells_z = charges.shape
    ghosted = extended(atoms, (("gx", 2), ("gy", 3)), 1)
    wrapped = jnp.concatenate([ghosted[..., -1:], ghosted, ghosted[..., :1]], axis=4)
    pair_force = cell_forces(wrapped) * occupied[None]
    ghost_x = spline_weights(ghosted[0])
    ghost_y = spline_weights(ghosted[1])
    ghost_z = spline_weights(ghosted[2]) * ghosted[3][None]
    planes = jnp.einsum("ypabc,zpabc->yzpabc", ghost_y, ghost_z, precision=HIGHEST)
    blocks = jnp.einsum("xpabc,yzpabc->xyzabc", ghost_x, planes, precision=HIGHEST)
    along_z = fold_wrap(jnp.moveaxis(blocks, 2, -1))
    along_y = fold_open(jnp.transpose(along_z, (0, 2, 4, 3, 1)))[
        ..., CELL + 2 : CELL + 2 + cells_y * CELL
    ]
    density = fold_open(jnp.transpose(along_y, (2, 3, 1, 0)))[
        ..., CELL + 2 : CELL + 2 + cells_x * CELL
    ]
    width_x = cells_x * CELL
    width_y = cells_y * CELL
    length_z = cells_z * CELL
    count_x = lax.axis_size("gx")
    count_y = lax.axis_size("gy")
    length_x = width_x * count_x
    length_y = width_y * count_y
    index_x = lax.axis_index("gx")
    index_y = lax.axis_index("gy")
    normalize = 1.0 / (length_x * length_y * length_z)
    cos_z, sin_z = trig(counting(length_z), counting(length_z), length_z)
    cos_y, sin_y = trig(counting(length_y), counting(length_y), length_y)
    cos_x, sin_x = trig(counting(length_x), counting(length_x), length_x)
    real_z = jnp.einsum("zyx,zk->kxy", density, cos_z, precision=HIGHEST)
    imag_z = -jnp.einsum("zyx,zk->kxy", density, sin_z, precision=HIGHEST)
    real_r, imag_r = (
        lax.all_to_all(real_z, "gy", split_axis=0, concat_axis=2, tiled=True),
        lax.all_to_all(imag_z, "gy", split_axis=0, concat_axis=2, tiled=True),
    )
    real_y, imag_y = transform(real_r, imag_r, cos_y, sin_y, "zxy,yk->kzx", -1)
    real_c, imag_c = (
        lax.all_to_all(real_y, "gx", split_axis=0, concat_axis=2, tiled=True),
        lax.all_to_all(imag_y, "gx", split_axis=0, concat_axis=2, tiled=True),
    )
    real_k, imag_k = transform(real_c, imag_c, cos_x, sin_x, "kzx,xm->kzm", -1)
    rows_y = length_y // count_x
    rows_z = length_z // count_y
    mode_y = folded(index_x * rows_y + counting(rows_y), length_y)[:, None, None]
    mode_z = folded(index_y * rows_z + counting(rows_z), length_z)[None, :, None]
    mode_x = folded(counting(length_x), length_x)[None, None, :]
    waves = green(mode_x, mode_y, mode_z, length_x, length_y, length_z, normalize)
    real_e, imag_e = field_parts(real_k, imag_k, waves)
    real_b, imag_b = transform(real_e, imag_e, cos_x, sin_x, "dkzm,mx->dkzx", 1)
    real_b, imag_b = (
        lax.all_to_all(real_b, "gx", split_axis=3, concat_axis=1, tiled=True),
        lax.all_to_all(imag_b, "gx", split_axis=3, concat_axis=1, tiled=True),
    )
    real_b, imag_b = transform(real_b, imag_b, cos_y, sin_y, "dkzx,ky->dzxy", 1)
    real_b, imag_b = (
        lax.all_to_all(real_b, "gy", split_axis=3, concat_axis=1, tiled=True),
        lax.all_to_all(imag_b, "gy", split_axis=3, concat_axis=1, tiled=True),
    )
    cos_back, sin_back = (cos_z, sin_z)
    fields = jnp.einsum("dkxy,kz->dxyz", real_b, cos_back, precision=HIGHEST) - jnp.einsum(
        "dkxy,kz->dxyz", imag_b, sin_back, precision=HIGHEST
    )
    rimmed = extended(fields, (("gx", 1), ("gy", 2)), 2)
    z_windows = windows_wrap(rimmed)
    y_windows = windows_open(jnp.transpose(z_windows, (0, 1, 3, 4, 2)), cells_y)
    windowed = windows_open(jnp.transpose(y_windows, (0, 2, 3, 4, 5, 1)), cells_x)
    own_x = spline_weights(atoms[0])
    own_y = spline_weights(atoms[1])
    own_z = spline_weights(atoms[2])
    mesh_force = interpolate(windowed, own_x, own_y, own_z) * atoms[3][None]
    return (pair_force, mesh_force)


def solution(mesh):
    placed = (
        P(None, None, "gx", "gy", None),
        P(None, "gx", "gy", None),
        P(None, "gx", "gy", None),
        P("gx", "gy", None),
        P(),
        P(),
    )
    return jax.shard_map(
        body,
        mesh=mesh,
        in_specs=placed,
        out_specs=(P(None, None, "gx", "gy", None), P(None, None, "gx", "gy", None)),
        check_vma=False,
    )
```

profile of v0, /device:TPU:1, one launch (start us, length us, event | category | flops | bytes accessed | tf_op | source)
XLA Modules:
  0.0 869.6 jit_solution(282952852597244310)
XLA Ops:
  21.0 13.5 %fusion.302 = (f32[32,4,2,16]{3,2,1,0:T(2,128)}, f32[32,4,2,16]{3,2,1,0:T(2,128)}, f32[32,4,2,16]{3,2,1,0:T(2,128)}) fusion(f32[32,4,2,16]{0,3,2,1:T(8,128)S(1)} %get-tuple-element.306, f32[32,4,2,16]{3,2,1,0:T(2,128)S(1)} %copy.998, f32[32,4,2,16]{0,3,2,1:T(8,128)S(1)} %copy.1003, f32[32,4,2,16]{3,2,1,0:T(2,128)S(1)} %get-tuple-element.313, ...), kind=kLoop, calls=%fused_computation.723 | loop fusion | flops 17420288 | bytes 245760 | tf_op jit(solution)/shard_map/reduce_sum | solution.py:94
  34.5 25.4 %fusion.131 = (f32[32,4,2,16]{3,2,1,0:T(2,128)}, f32[32,4,2,16]{3,2,1,0:T(2,128)}, f32[32,4,2,16]{3,2,1,0:T(2,128)}, f32[32,4,2,16]{3,2,1,0:T(2,128)}, f32[32,4,2,16]{3,2,1,0:T(2,128)}, /*index=5*/f32[32,4,2,16]{3,2,1,0:T(2,128)}) fusion(f32[32,4,2,16]{0,3,2,1:T(8,128)S(1)} %get-tuple-element.296, f32[32,4,2,16]{3,2,1,0:T(2,128)S(1)} %copy.998, ...), kind=kLoop, calls=%fused_computation.552 | loop fusion | flops 34840576 | bytes 393216 | tf_op jit(solution)/shard_map/reduce_sum | solution.py:94
  76.0 39.8 %fusion.14 = f32[12,12,6,4,16,12]{0,5,1,4,3,2:T(8,128)} fusion(f32[32,6,4,16,12]{0,4,3,2,1:T(8,128)S(1)} %get-tuple-element.317, f32[32,6,4,16,12]{0,4,3,2,1:T(8,128)S(1)} %get-tuple-element.316, f32[32,6,4,16]{0,3,2,1:T(8,128)S(1)} %get-tuple-element.234, f32[12]{0:T(128)S(1)} %convert_add_fusion), kind=kOutput, calls=%fused_computation.16 | convolution fusion | flops 259227648 | bytes 3883056 | tf_op jit(solution)/shard_map/xpabc,yzpabc->xyzabc/dot_general | solution.py:220
  126.7 12.3 %pad_slice_fusion = f32[12,12,6,4,15,8]{0,5,1,4,3,2:T(8,128)} fusion(f32[12,12,6,4,16,4]{0,5,1,4,3,2:T(4,128)} %copy-done), kind=kLoop, calls=%fused_computation.11 | loop fusion | bytes 2543616 | tf_op jit(solution)/shard_map/jit(_roll_static)/slice | solution.py:104
  138.9 18.5 %slice_add_fusion = f32[12,12,6,4,16,8]{0,5,1,4,3,2:T(8,128)} fusion(f32[12,12,6,4,16,12]{0,5,1,4,3,2:T(8,128)} %fusion.14, f32[12,12,6,4,15,8]{0,5,1,4,3,2:T(8,128)} %pad_slice_fusion, f32[12,12,6,4,1,8]{0,5,1,4,3,2:T(8,128)S(1)} %pad_slice_fusion.1), kind=kLoop, calls=%fused_computation.13 | loop fusion | flops 884736 | bytes 5308416 | tf_op jit(solution)/shard_map/add | solution.py:104
  157.5 38.6 %copy.1004 = f32[12,12,6,4,16,8]{5,4,3,2,1,0:T(8,128)} copy(f32[12,12,6,4,16,8]{0,5,1,4,3,2:T(8,128)} %slice_add_fusion) | data formatting | bytes 3538944 | tf_op jit(solution)/shard_map/add | solution.py:104
  196.1 19.6 %reshape.957 = f32[12,12,6,4,128]{4,3,2,1,0:T(4,128)S(1)} reshape(f32[12,12,6,4,16,8]{5,4,3,2,1,0:T(8,128)} %copy.1004) | data formatting | bytes 3538944 | tf_op jit(solution)/shard_map/reshape | solution.py:104
  231.3 26.5 %fusion.245 = (f32[32,4,2,16]{3,2,1,0:T(2,128)}, f32[32,4,2,16]{3,2,1,0:T(2,128)}, f32[32,4,2,16]{3,2,1,0:T(2,128)}, f32[32,4,2,16]{3,2,1,0:T(2,128)}, f32[32,4,2,16]{3,2,1,0:T(2,128)}, /*index=5*/f32[32,4,2,16]{3,2,1,0:T(2,128)}) fusion(f32[32,4,2,16]{0,3,2,1:T(8,128)} %get-tuple-element.273, f32[32,4,2,16]{3,2,1,0:T(2,128)S(1)} %copy.998, ...), kind=kLoop, calls=%fused_computation.666 | loop fusion | flops 34840576 | bytes 393216 | tf_op jit(solution)/shard_map/reduce_sum | solution.py:94
  257.8 26.3 %fusion.188 = (f32[32,4,2,16]{3,2,1,0:T(2,128)}, f32[32,4,2,16]{3,2,1,0:T(2,128)}, f32[32,4,2,16]{3,2,1,0:T(2,128)}, f32[32,4,2,16]{3,2,1,0:T(2,128)}, f32[32,4,2,16]{3,2,1,0:T(2,128)}, /*index=5*/f32[32,4,2,16]{3,2,1,0:T(2,128)}) fusion(f32[32,4,2,16]{0,3,2,1:T(8,128)S(1)} %copy-done.179, f32[32,4,2,16]{3,2,1,0:T(2,128)S(1)} %copy.998, ...), kind=kLoop, calls=%fused_computation.609 | loop fusion | flops 34840576 | bytes 393216 | tf_op jit(solution)/shard_map/reduce_sum | solution.py:94
  284.3 25.4 %fusion.55 = (f32[32,4,2,16]{3,2,1,0:T(2,128)}, f32[32,4,2,16]{3,2,1,0:T(2,128)}, f32[32,4,2,16]{3,2,1,0:T(2,128)}, f32[32,4,2,16]{3,2,1,0:T(2,128)}, f32[32,4,2,16]{3,2,1,0:T(2,128)}, /*index=5*/f32[32,4,2,16]{3,2,1,0:T(2,128)}) fusion(f32[32,4,2,16]{3,2,1,0:T(2,128)S(1)} %copy.998, f32[32,4,2,16]{0,3,2,1:T(8,128)S(1)} %copy-done.138, ...), kind=kLoop, calls=%fused_computation.476 | loop fusion | flops 34840576 | bytes 393216 | tf_op jit(solution)/shard_map/reduce_sum | solution.py:94
  309.9 25.8 %fusion.93 = (f32[32,4,2,16]{3,2,1,0:T(2,128)}, f32[32,4,2,16]{3,2,1,0:T(2,128)}, f32[32,4,2,16]{3,2,1,0:T(2,128)}, f32[32,4,2,16]{3,2,1,0:T(2,128)}, f32[32,4,2,16]{3,2,1,0:T(2,128)}, /*index=5*/f32[32,4,2,16]{3,2,1,0:T(2,128)}) fusion(f32[32,4,2,16]{0,3,2,1:T(8,128)S(1)} %copy-done.168, f32[32,4,2,16]{3,2,1,0:T(2,128)S(1)} %copy.998, ...), kind=kLoop, calls=%fused_computation.514 | loop fusion | flops 34840576 | bytes 393216 | tf_op jit(solution)/shard_map/reduce_sum | solution.py:94
  335.9 25.4 %fusion.150 = (f32[32,4,2,16]{3,2,1,0:T(2,128)}, f32[32,4,2,16]{3,2,1,0:T(2,128)}, f32[32,4,2,16]{3,2,1,0:T(2,128)}, f32[32,4,2,16]{3,2,1,0:T(2,128)}, f32[32,4,2,16]{3,2,1,0:T(2,128)}, /*index=5*/f32[32,4,2,16]{3,2,1,0:T(2,128)}) fusion(f32[32,4,2,16]{0,3,2,1:T(8,128)S(1)} %copy-done.159, f32[32,4,2,16]{3,2,1,0:T(2,128)S(1)} %copy.998, ...), kind=kLoop, calls=%fused_computation.571 | loop fusion | flops 34840576 | bytes 393216 | tf_op jit(solution)/shard_map/reduce_sum | solution.py:94
  361.4 26.3 %fusion.283 = (f32[32,4,2,16]{3,2,1,0:T(2,128)}, f32[32,4,2,16]{3,2,1,0:T(2,128)}, f32[32,4,2,16]{3,2,1,0:T(2,128)}, f32[32,4,2,16]{3,2,1,0:T(2,128)}, f32[32,4,2,16]{3,2,1,0:T(2,128)}, /*index=5*/f32[32,4,2,16]{3,2,1,0:T(2,128)}) fusion(f32[32,4,2,16]{0,3,2,1:T(8,128)S(1)} %copy-done.109, f32[32,4,2,16]{3,2,1,0:T(2,128)S(1)} %copy.998, ...), kind=kLoop, calls=%fused_computation.704 | loop fusion | flops 34840576 | bytes 393216 | tf_op jit(solution)/shard_map/reduce_sum | solution.py:94
  388.0 25.6 %fusion.207 = (f32[32,4,2,16]{3,2,1,0:T(2,128)}, f32[32,4,2,16]{3,2,1,0:T(2,128)}, f32[32,4,2,16]{3,2,1,0:T(2,128)}, f32[32,4,2,16]{3,2,1,0:T(2,128)}, f32[32,4,2,16]{3,2,1,0:T(2,128)}, /*index=5*/f32[32,4,2,16]{3,2,1,0:T(2,128)}) fusion(f32[32,4,2,16]{0,3,2,1:T(8,128)S(1)} %copy-done.132, f32[32,4,2,16]{3,2,1,0:T(2,128)S(1)} %copy.998, ...), kind=kLoop, calls=%fused_computation.628 | loop fusion | flops 34840576 | bytes 393216 | tf_op jit(solution)/shard_map/reduce_sum | solution.py:94
  413.6 25.4 %fusion.74 = (f32[32,4,2,16]{3,2,1,0:T(2,128)}, f32[32,4,2,16]{3,2,1,0:T(2,128)}, f32[32,4,2,16]{3,2,1,0:T(2,128)}, f32[32,4,2,16]{3,2,1,0:T(2,128)}, f32[32,4,2,16]{3,2,1,0:T(2,128)}, /*index=5*/f32[32,4,2,16]{3,2,1,0:T(2,128)}) fusion(f32[32,4,2,16]{0,3,2,1:T(8,128)S(1)} %copy-done.174, f32[32,4,2,16]{3,2,1,0:T(2,128)S(1)} %copy.998, ...), kind=kLoop, calls=%fused_computation.495 | loop fusion | flops 34840576 | bytes 393216 | tf_op jit(solution)/shard_map/reduce_sum | solution.py:94
  439.1 25.8 %fusion.112 = (f32[32,4,2,16]{3,2,1,0:T(2,128)}, f32[32,4,2,16]{3,2,1,0:T(2,128)}, f32[32,4,2,16]{3,2,1,0:T(2,128)}, f32[32,4,2,16]{3,2,1,0:T(2,128)}, f32[32,4,2,16]{3,2,1,0:T(2,128)}, /*index=5*/f32[32,4,2,16]{3,2,1,0:T(2,128)}) fusion(f32[32,4,2,16]{0,3,2,1:T(8,128)S(1)} %copy-done.104, f32[32,4,2,16]{3,2,1,0:T(2,128)S(1)} %copy.998, ...), kind=kLoop, calls=%fused_computation.533 | loop fusion | flops 34840576 | bytes 393216 | tf_op jit(solution)/shard_map/reduce_sum | solution.py:94
  537.4 26.6 %fusion.169 = (f32[32,4,2,16]{3,2,1,0:T(2,128)}, f32[32,4,2,16]{3,2,1,0:T(2,128)}, f32[32,4,2,16]{3,2,1,0:T(2,128)}, f32[32,4,2,16]{3,2,1,0:T(2,128)}, f32[32,4,2,16]{3,2,1,0:T(2,128)}, /*index=5*/f32[32,4,2,16]{3,2,1,0:T(2,128)}) fusion(f32[32,4,2,16]{0,3,2,1:T(8,128)S(1)} %copy-done.92, f32[32,4,2,16]{3,2,1,0:T(2,128)S(1)} %copy.998, ...), kind=kLoop, calls=%fused_computation.590 | loop fusion | flops 34840576 | bytes 393216 | tf_op jit(solution)/shard_map/reduce_sum | solution.py:94
  578.9 25.4 %fusion.226 = (f32[32,4,2,16]{3,2,1,0:T(2,128)}, f32[32,4,2,16]{3,2,1,0:T(2,128)}, f32[32,4,2,16]{3,2,1,0:T(2,128)}, f32[32,4,2,16]{3,2,1,0:T(2,128)}, f32[32,4,2,16]{3,2,1,0:T(2,128)}, /*index=5*/f32[32,4,2,16]{3,2,1,0:T(2,128)}) fusion(f32[32,4,2,16]{0,3,2,1:T(8,128)S(1)} %copy-done.82, f32[32,4,2,16]{3,2,1,0:T(2,128)S(1)} %copy.998, ...), kind=kLoop, calls=%fused_computation.647 | loop fusion | flops 34840576 | bytes 393216 | tf_op jit(solution)/shard_map/reduce_sum | solution.py:94
  644.8 25.4 %fusion.264 = (f32[32,4,2,16]{3,2,1,0:T(2,128)}, f32[32,4,2,16]{3,2,1,0:T(2,128)}, f32[32,4,2,16]{3,2,1,0:T(2,128)}, f32[32,4,2,16]{3,2,1,0:T(2,128)}, f32[32,4,2,16]{3,2,1,0:T(2,128)}, /*index=5*/f32[32,4,2,16]{3,2,1,0:T(2,128)}) fusion(f32[32,4,2,16]{0,3,2,1:T(8,128)S(1)} %copy-done.88, f32[32,4,2,16]{3,2,1,0:T(2,128)S(1)} %copy.998, ...), kind=kLoop, calls=%fused_computation.685 | loop fusion | flops 34840576 | bytes 393216 | tf_op jit(solution)/shard_map/reduce_sum | solution.py:94
  679.0 7.2 all-to-all-start.7
  749.6 12.1 %copy.1038 = f32[3,16,12,2,12,32]{1,5,4,3,2,0:T(8,128)} copy(f32[3,16,12,2,12,32]{5,4,2,0,1,3:T(8,128)} %bitcast.675) | data formatting | bytes 3538944 | tf_op jit(solution)/shard_map/slice | solution.py:129
  761.7 31.5 %copy.1040 = f32[3,16,12,2,12,4,8]{6,4,2,0,1,3,5:T(8,128)} copy(f32[3,16,12,2,12,4,8]{1,6,5,4,3,2,0:T(8,128)} %bitcast.676) | data formatting | bytes 3538944 | tf_op jit(solution)/shard_map/reshape | solution.py:129
  793.2 20.4 %slice.1256 = f32[3,16,12,2,12,3,4]{6,4,2,0,1,3,5:T(8,128)} slice(f32[3,16,12,2,12,4,8]{6,4,2,0,1,3,5:T(8,128)} %copy.1040), slice={[0:3], [0:16], [0:12], [0:2], [0:12], [1:4], [0:4]} | slice | bytes 1327104 | tf_op jit(solution)/shard_map/slice | solution.py:131
  813.6 53.9 %fusion.6 = f32[32,4,2,16,3,12]{0,5,4,3,2,1:T(8,128)S(1)} fusion(f32[32,4,2,16,12]{0,4,3,2,1:T(8,128)S(1)} %copy-done.3, f32[3,16,12,2,12,1,4]{6,4,2,0,1,3,5:T(8,128)} %slice_bitcast_fusion, f32[3,16,12,2,12,3,4]{6,4,2,0,1,3,5:T(8,128)} %slice.1256, f32[3,16,12,2,12,4,8]{6,4,2,0,1,3,5:T(8,128)} %copy.1040, f32[32,4,2,16]{0,3,2,1:T(8,128)S(1)} %copy-done.10, ...), kind=kOutput, calls=%fused_computation.7 | convolution fusion | flops 260407296 | bytes 3457072 | tf_op jit(solution)/shard_map/dczbyax,xpabc->dzypabc/dot_general | solution.py:137
  (566 shorter events, 263.0 us)
Async XLA Ops:
  7.4 7.1 collective-permute-start
  10.0 4.0 collective-permute-start.1
  10.0 66.0 %copy-start.185 = (f32[12]{0:T(128)}, f32[12]{0:T(128)S(1)}, u32[]{:S(2)}) copy-start(f32[12]{0:T(128)S(1)} %convert_add_fusion) | copy-start | bytes 148
  14.7 48.7 %collective-permute-start.3 = (f32[6,32,6,1,16]{1,4,3,2,0:T(8,128)S(1)}, f32[6,32,6,1,16]{1,4,3,2,0:T(8,128)S(1)}, u32[]{:S(2)}, u32[]{:S(2)}) collective-permute-start(f32[6,32,6,1,16]{1,4,3,2,0:T(8,128)S(1)} %get-tuple-element.284), channel_id=1, source_target_pairs={{1,0},{2,1},{3,2},{4,3},{5,4},{6,5},{7,6},{8,7},{9,8},{10,9},{11,1... | collective-permute-start | bytes 221192 | tf_op jit(solution)/shard_map/ppermute | solution.py:24
  21.0 42.4 %collective-permute-start.2 = (f32[6,32,6,1,16]{1,4,3,2,0:T(8,128)S(1)}, f32[6,32,6,1,16]{1,4,3,2,0:T(8,128)S(1)}, u32[]{:S(2)}, u32[]{:S(2)}) collective-permute-start(f32[6,32,6,1,16]{1,4,3,2,0:T(8,128)S(1)} %get-tuple-element.285), channel_id=1, source_target_pairs={{0,1},{1,2},{2,3},{3,4},{4,5},{5,6},{6,7},{7,8},{8,9},{9,10},{10,1... | collective-permute-start | bytes 221192 | tf_op jit(solution)/shard_map/ppermute | solution.py:22
  224.6 242.7 %all-to-all-start.1 = ((f32[16,1,4096]{2,1,0:T(1,128)}), f32[16,1,4096]{2,1,0:T(1,128)S(1)}, u32[]{:S(2)}, u32[]{:S(2)}) async-start(f32[16,1,4096]{2,1,0:T(1,128)} %reshape.1017), calls=%async_computation.1 | async-start | bytes 524288 | tf_op jit(solution)/shard_map/all_to_all | solution.py:244
  231.2 52.9 %copy-start.133 = (f32[32,4,2,16]{0,3,2,1:T(8,128)S(1)}, f32[32,4,2,16]{0,3,2,1:T(8,128)}, u32[]{:S(2)}) copy-start(f32[32,4,2,16]{0,3,2,1:T(8,128)} %get-tuple-element.228) | copy-start | bytes 49156
  231.2 52.9 %copy-start.134 = (f32[32,4,2,16]{0,3,2,1:T(8,128)S(1)}, f32[32,4,2,16]{0,3,2,1:T(8,128)}, u32[]{:S(2)}) copy-start(f32[32,4,2,16]{0,3,2,1:T(8,128)} %get-tuple-element.229) | copy-start | bytes 49156
  231.2 52.9 %copy-start.135 = (f32[32,4,2,16]{0,3,2,1:T(8,128)S(1)}, f32[32,4,2,16]{0,3,2,1:T(8,128)}, u32[]{:S(2)}) copy-start(f32[32,4,2,16]{0,3,2,1:T(8,128)} %get-tuple-element.230) | copy-start | bytes 49156
  231.2 52.9 %copy-start.136 = (f32[32,4,2,16]{0,3,2,1:T(8,128)S(1)}, f32[32,4,2,16]{0,3,2,1:T(8,128)}, u32[]{:S(2)}) copy-start(f32[32,4,2,16]{0,3,2,1:T(8,128)} %get-tuple-element.231) | copy-start | bytes 49156
  231.2 52.9 %copy-start.137 = (f32[32,4,2,16]{0,3,2,1:T(8,128)S(1)}, f32[32,4,2,16]{0,3,2,1:T(8,128)}, u32[]{:S(2)}) copy-start(f32[32,4,2,16]{0,3,2,1:T(8,128)} %get-tuple-element.232) | copy-start | bytes 49156
  231.2 52.9 %copy-start.138 = (f32[32,4,2,16]{0,3,2,1:T(8,128)S(1)}, f32[32,4,2,16]{0,3,2,1:T(8,128)}, u32[]{:S(2)}) copy-start(f32[32,4,2,16]{0,3,2,1:T(8,128)} %get-tuple-element.233) | copy-start | bytes 49156
  467.3 14.1 %all-to-all-start = ((f32[16,1,4096]{2,1,0:T(1,128)}), f32[16,1,4096]{2,1,0:T(1,128)S(1)}, u32[]{:S(2)}, u32[]{:S(2)}) async-start(f32[16,1,4096]{2,1,0:T(1,128)} %reshape.1015), calls=%async_computation | async-start | bytes 524288 | tf_op jit(solution)/shard_map/all_to_all | solution.py:245
  491.8 12.9 %all-to-all-start.2 = ((f32[8,1,8192]{2,1,0:T(1,128)}), f32[8,1,8192]{2,1,0:T(1,128)S(1)}, u32[]{:S(2)}, u32[]{:S(2)}) async-start(f32[8,1,8192]{2,1,0:T(1,128)} %reshape.1019), calls=%async_computation.2 | async-start | bytes 524288 | tf_op jit(solution)/shard_map/all_to_all | solution.py:250
  504.7 10.9 %all-to-all-start.3 = ((f32[8,1,8192]{2,1,0:T(1,128)}), f32[8,1,8192]{2,1,0:T(1,128)S(1)}, u32[]{:S(2)}, u32[]{:S(2)}) async-start(f32[8,1,8192]{2,1,0:T(1,128)} %reshape.1021), calls=%async_computation.3 | async-start | bytes 524288 | tf_op jit(solution)/shard_map/all_to_all | solution.py:249
  532.9 40.6 %all-to-all-start.5 = ((f32[8,1,24576]{2,1,0:T(1,128)}), f32[8,1,24576]{2,1,0:T(1,128)S(1)}, u32[]{:S(2)}, u32[]{:S(2)}) async-start(f32[8,1,24576]{2,1,0:T(1,128)} %reshape.1025), calls=%async_computation.5 | async-start | bytes 1572864 | tf_op jit(solution)/shard_map/all_to_all | solution.py:263
  573.5 44.0 %all-to-all-start.4 = ((f32[8,1,24576]{2,1,0:T(1,128)}), f32[8,1,24576]{2,1,0:T(1,128)S(1)}, u32[]{:S(2)}, u32[]{:S(2)}) async-start(f32[8,1,24576]{2,1,0:T(1,128)} %reshape.1023), calls=%async_computation.4 | async-start | bytes 1572864 | tf_op jit(solution)/shard_map/all_to_all | solution.py:262
  640.2 38.9 %all-to-all-start.6 = ((f32[16,1,12288]{2,1,0:T(1,128)}), f32[16,1,12288]{2,1,0:T(1,128)}, u32[]{:S(2)}, u32[]{:S(2)}) async-start(f32[16,1,12288]{2,1,0:T(1,128)} %reshape.1027), calls=%async_computation.6 | async-start | bytes 1572864 | tf_op jit(solution)/shard_map/all_to_all | solution.py:267
  679.0 25.2 %all-to-all-start.7 = ((f32[16,1,12288]{2,1,0:T(1,128)}), f32[16,1,12288]{2,1,0:T(1,128)}, u32[]{:S(2)}, u32[]{:S(2)}) async-start(f32[16,1,12288]{2,1,0:T(1,128)} %reshape.1029), calls=%async_computation.7 | async-start | bytes 1572864 | tf_op jit(solution)/shard_map/all_to_all | solution.py:268
  717.2 3.4 collective-permute-start.4
  719.4 3.5 collective-permute-start.5
  723.0 8.3 collective-permute-start.6
  724.8 6.5 collective-permute-start.7
  813.6 53.9 %copy-start.5 = (f32[32,4,2,16,12]{0,3,4,2,1:T(8,128)S(1)}, f32[32,4,2,16,12]{0,3,4,2,1:T(8,128)}, u32[]{:S(2)}) copy-start(f32[32,4,2,16,12]{0,3,4,2,1:T(8,128)} %copy.1074) | copy-start | bytes 589828
  (184 other events, 4278.1 us)
where the time goes:
time: 880 us; the launch traced here: 870 us
  other arithmetic  420 us (48%)
  local copies, waits for them, and re-layouts  240 us (27%)
  matrix products  130 us (15%)
  starting transfers between devices  61.8 us (7%)
  waiting for transfers between devices  12.7 us (1%)
    reduce_sum x14, other arithmetic, cell_forces(): jnp.sum(2.0 * derivative * separation[component], axis=1)  349 us
    dot_general x1, matrix products, interpolate(): jnp.einsum('dczbyax,xpabc->dzypabc', windowed, weight_x, precision=HIGHEST)  53.9 us
    dot_general x1, matrix products, body(): jnp.einsum('xpabc,yzpabc->xyzabc', ghost_x, planes, precision=HIGHEST)  39.8 us
    unnamed x401, local copies, waits for them, and re-layouts  39.8 us
    add x1, local copies, waits for them, and re-layouts, fold_wrap(): first_half + jnp.roll(second_half, 1, axis=-2)  38.6 us
    reshape x2, local copies, waits for them, and re-layouts, windows_open(): fields[..., :cell_count * CELL]  31.9 us
    slice x2, local copies, waits for them, and re-layouts, windows_open(): leading[..., 1:, :4]  20.6 us
    reshape x1, local copies, waits for them, and re-layouts, fold_wrap(): (first_half + jnp.roll(second_half, 1, axis=-2)).reshape(blocks.shape[:-2...  19.6 us
  transfers between devices with their start and end apart: 16, of which 6 were waited for; matrix products, arithmetic and copies ran while one was open for 48% of the time, Pallas kernels for 0%

commit v1 on v0

v1 whole, which is shorter than its diff:
```python
import functools
import math

import jax
import jax.numpy as jnp
import ml_dtypes
import numpy as np
from jax import lax
from jax.experimental import pallas as pl
from jax.experimental.pallas import tpu as pltpu
from jax.sharding import PartitionSpec as P

CELL = 8
GEWALD = 0.7
CUT = 64.0
F32 = jnp.float32
BF16 = jnp.bfloat16

SLOTS = 32
CX, CY, CZ = 4, 2, 16
CELLS = CX * CY * CZ
DX, DY = 8, 16
LX, LY, LZ = 256, 256, 128
BX, BY = CX * CELL + 4, CY * CELL + 4
BLOCK = 768
GROUPS = CELLS // 4
KZ = 48
KX = 48
VMEM = pl.BlockSpec(memory_space=pltpu.VMEM)
SMEM = pl.BlockSpec(memory_space=pltpu.SMEM)


def params(mib=40):
    return pltpu.CompilerParams(vmem_limit_bytes=mib << 20)


def split(array):
    high = array.astype(ml_dtypes.bfloat16)
    low = (array - high.astype(np.float64)).astype(ml_dtypes.bfloat16)
    return high, low


def basis(length):
    half = length // 2
    modes = np.concatenate([np.arange(half + 1), np.arange(1, half)])
    sines = np.arange(length) > half
    return modes, sines


def wave(points, modes, sines, length):
    angle = 2.0 * np.pi * (np.outer(modes, points) % length) / length
    return np.where(sines[:, None], np.sin(angle), np.cos(angle))


def wave_slope(points, modes, sines, length):
    angle = 2.0 * np.pi * (np.outer(modes, points) % length) / length
    k = 2.0 * np.pi * modes / length
    k = np.where(modes == length // 2, 0.0, k)[:, None]
    return np.where(sines[:, None], -k * np.cos(angle), k * np.sin(angle))


def damping(modes, length):
    k = 2.0 * np.pi * modes / length
    return np.exp(-k * k / (4.0 * GEWALD * GEWALD)) / np.sinc(modes / length) ** 8


def norms(modes, length):
    return np.where((modes == 0) | (modes == length // 2), 1.0, 2.0) / length


@functools.cache
def tables():
    mz, sz = basis(LZ)
    tz = np.zeros((4, LZ, KZ))
    for zg in range(4):
        tz[zg, :, :36] = wave(32 * zg - 2 + np.arange(36), mz, sz, LZ)
    mx, sx = basis(LX)
    my, sy = basis(LY)
    tx = np.zeros((DX, KX, LX))
    gain_x = damping(mx, LX) * norms(mx, LX)
    ix = np.zeros((2, LX, DX * BX))
    for gx in range(DX):
        points = gx * CX * CELL - 2 + np.arange(BX)
        tx[gx, :BX] = (wave(points, mx, sx, LX) * gain_x[:, None]).T
        ix[0, :, gx * BX : (gx + 1) * BX] = wave(points, mx, sx, LX)
        ix[1, :, gx * BX : (gx + 1) * BX] = wave_slope(points, mx, sx, LX)
    points = (np.arange(DY)[None, :] * CY * CELL - 2 + np.arange(BY)[:, None]).reshape(-1)
    gain_y = damping(my, LY) * norms(my, LY)
    ty = wave(points, my, sy, LY) * gain_y[:, None]
    iy = np.concatenate([wave(points, my, sy, LY).T, wave_slope(points, my, sy, LY).T])
    kx2 = ((2.0 * np.pi * mx / LX) ** 2).astype(np.float32)[None, :]
    ky2 = ((2.0 * np.pi * my / LY) ** 2).astype(np.float32)[:, None]
    kz = 2.0 * np.pi * mz / LZ
    plane = np.stack([kz * kz, 4.0 * np.pi * damping(mz, LZ) * norms(mz, LZ)], 1)
    half = LZ // 2
    swap = 2.0 * np.pi * np.arange(half) / LZ
    swap = np.concatenate([-swap, swap]).astype(np.float32)[None, :]
    return dict(
        tz=split(tz),
        tx=split(tx),
        ty=split(ty),
        iy=split(iy),
        ix=split(ix),
        kx2=kx2,
        ky2=np.broadcast_to(ky2, (LY, 128)).astype(np.float32),
        plane=plane.astype(np.float32),
        swap=swap,
    )


def halves(value):
    high = value.astype(BF16)
    return high, (value - high.astype(F32)).astype(BF16)


def dot3(left, right, dims=((1,), (0,))):
    dot = lambda a, b: lax.dot_general(a, b, (dims, ((), ())), preferred_element_type=F32)
    return dot(left[0], right[0]) + (dot(left[0], right[1]) + dot(left[1], right[0]))


def table_kernel(pos_ref, charge_ref, type_ref, count_ref, eps_ref, sig_ref, atoms_ref, rows_ref):
    slots = lax.broadcasted_iota(jnp.int32, (SLOTS, CELLS), 0)
    occupied = slots < count_ref[...]
    kinds = type_ref[...].T
    eps = jnp.zeros((SLOTS, CELLS), F32)
    sig = jnp.zeros((SLOTS, CELLS), F32)
    for kind in range(eps_ref.shape[0]):
        match = kinds == kind
        eps = jnp.where(match, eps_ref[kind], eps)
        sig = jnp.where(match, sig_ref[kind], sig)
    charge = jnp.where(occupied, charge_ref[...].T, 0.0)
    for d in range(3):
        atoms_ref[d] = pos_ref[d].T
    atoms_ref[3] = charge
    atoms_ref[4] = jnp.where(occupied, jnp.sqrt(eps), 0.0)
    atoms_ref[5] = sig
    charge = charge.T
    for c in range(4):
        value = pos_ref[c] if c < 3 else charge
        value = value.reshape(GROUPS, 4, SLOTS)
        rows_ref[c] = jnp.concatenate([value[:, s, :] for s in range(4)], axis=1)


def spline(offset):
    span = jnp.abs(offset)
    outer = jnp.maximum(2.0 - span, 0.0)
    inner = jnp.maximum(1.0 - span, 0.0)
    return (outer * outer * outer) * (1.0 / 6.0) - (inner * inner * inner) * (2.0 / 3.0)


def weights(rows_ref, tz_high, tz_low, col, charged):
    point = (lax.broadcasted_iota(jnp.int32, (16, 128), 0) - 2).astype(F32)
    point_z = (lax.broadcasted_iota(jnp.int32, (KZ, 128), 0) - 2).astype(F32)
    shift = ((lax.broadcasted_iota(jnp.int32, (1, 128), 1) // SLOTS) * CELL).astype(F32)
    modes, planes = [], []
    for zg in range(4):
        row = [rows_ref[c, pl.ds(col * 4 + zg, 1), :] for c in range(4)]
        along_x = spline(row[0] - point)
        along_y = spline(row[1] - point)
        if charged:
            along_y = along_y * row[3]
        along_z = spline(row[2] + shift - point_z)
        modes.append(dot3((tz_high[zg], tz_low[zg]), halves(along_z)))
        planes.append((along_y[:12, None, :] * along_x[None, :, :]).reshape(192, 128))
    return jnp.concatenate(modes, axis=1), jnp.concatenate(planes, axis=1)


def spread_kernel(rows_ref, tz_high, tz_low, out_ref, total, packed):
    total[...] = jnp.zeros_like(total)

    def column(col, carry):
        modes, planes = weights(rows_ref, tz_high, tz_low, col, True)
        part = dot3(halves(planes), halves(modes), ((1,), (1,))).reshape(12, 16, LZ)
        y = (col % CY) * CELL
        x = pl.multiple_of((col // CY) * CELL, CELL)
        total[pl.ds(y, 12), pl.ds(x, 16), :] += part
        return carry

    lax.fori_loop(0, CX * CY, column, 0)
    for y in range(BY):
        packed[y * BX : (y + 1) * BX, :] = total[y, :BX, :]
    packed[BX * BY :, :] = jnp.zeros((BLOCK - BX * BY, LZ), F32)
    out_ref[...] = packed[...].T


def plane_kernel(
    plane_ref, in_ref, txh, txl, tyh, tyl, iyh, iyl, ixh, ixl, kx2, ky2, out_ref, stacked
):
    for y in range(BY):
        value = in_ref[:, y * BX : y * BX + KX]
        for gx in range(DX):
            stacked[gx, y * DY : (y + 1) * DY, :KX] = value[gx * DY : (gx + 1) * DY]
    lines = jnp.zeros((BY * DY, LX), F32)
    for gx in range(DX):
        lines = lines + dot3(halves(stacked[gx, :, :KX]), (txh[gx], txl[gx]))
    modes = dot3((tyh[...], tyl[...]), halves(lines))
    k2 = kx2[...] + jnp.concatenate([ky2[...], ky2[...]], axis=1) + plane_ref[0]
    positive = k2 > 0.0
    modes = jnp.where(positive, modes * (plane_ref[1] / jnp.where(positive, k2, 1.0)), 0.0)
    both = dot3((iyh[...], iyl[...]), halves(modes))
    rows = BY * DY
    plain = halves(both[:rows])
    slope = halves(both[rows:])
    fields = (
        dot3(plain, (ixh[1], ixl[1])),
        dot3(slope, (ixh[0], ixl[0])),
        dot3(plain, (ixh[0], ixl[0])),
    )
    for d in range(3):
        out_ref[:, d * BLOCK + BX * BY : (d + 1) * BLOCK] = jnp.zeros(
            (DX * DY, BLOCK - BX * BY), F32
        )
        for gx in range(DX):
            piece = fields[d][:, gx * BX : (gx + 1) * BX]
            for y in range(BY):
                lane = d * BLOCK + y * BX
                out_ref[gx * DY : (gx + 1) * DY, lane : lane + BX] = piece[y * DY : (y + 1) * DY]


def force_kernel(in_ref, rows_ref, tz_high, tz_low, swap_ref, out_ref, packed, padded, rows_out):
    for d in range(3):
        value = in_ref[:, d * BLOCK : (d + 1) * BLOCK].T
        if d == 2:
            value = pltpu.roll(value, LZ // 2, 1) * swap_ref[...]
        packed[...] = value
        for y in range(BY):
            padded[d, y, :BX, :] = packed[y * BX : (y + 1) * BX, :]
            padded[d, y, BX:, :] = jnp.zeros((40 - BX, LZ), F32)

    def column(col, carry):
        modes, planes = weights(rows_ref, tz_high, tz_low, col, False)
        modes = halves(modes)
        y = (col % CY) * CELL
        x = pl.multiple_of((col // CY) * CELL, CELL)
        for d in range(3):
            block = padded[d, pl.ds(y, 12), pl.ds(x, 16), :].reshape(192, LZ)
            along = dot3(halves(block), modes)
            force = jnp.sum(along * planes, axis=0, keepdims=True)
            for zg in range(4):
                at = pl.ds(col * 4 + zg, 1)
                rows_out[d, at, :] = force[:, 128 * zg : 128 * (zg + 1)] * rows_ref[3, at, :]
        return carry

    lax.fori_loop(0, CX * CY, column, 0)
    for d in range(3):
        value = rows_out[d]
        pieces = [value[:, s * SLOTS : (s + 1) * SLOTS][:, None, :] for s in range(4)]
        out_ref[d] = jnp.concatenate(pieces, axis=1).reshape(CELLS, SLOTS)


COULOMB = (
    -0.006157896808528851,
    -0.00037761534771162467,
    0.4246826287075061,
    -0.032594054879277516,
    0.5289809248435148,
    -0.3643412334667553,
    0.147196623703603,
    -0.012411731315994238,
    -0.015640759195296648,
    0.00499632789350256,
)
SCALES = (0.125, 0.125, 0.125, 1.0, 1.0, 0.0625)


def pair_term(own, other):
    dx = other[0] - own[0]
    dy = other[1] - own[1]
    dz = other[2] - own[2]
    r2 = dx * dx + dy * dy + dz * dz
    fade = jnp.maximum(1.0 - r2, 0.0)
    t = lax.rsqrt(r2 + 1.0 / CUT)
    decay = jnp.exp2(r2 * (-0.49 * CUT * math.log2(math.e)))
    scale = -16.0 * math.exp(-0.49)
    terms = [scale * c * 0.125**n for n, c in enumerate(COULOMB)]
    poly = terms[-1] * t + terms[-2]
    for c in terms[-3::-1]:
        poly = poly * t + c
    sigma = own[5] + other[5]
    square = sigma * sigma
    inverse = 1.0 / (r2 + square)
    x = square * inverse
    x3 = x * x * x
    rest = 1.0 - (x3 + x3)
    lj = x3 * (rest * ((fade * inverse) * 3.0 + 1.0) + 1.0)
    w = fade * ((own[4] * other[4]) * lj + (own[3] * other[3]) * (decay * poly))
    return w * dx, w * dy, w * dz


def pair_kernel(*refs, shifts, unroll):
    wide_refs = refs[:-3]
    out_ref, others, own = refs[-3:]
    low = (lax.broadcasted_iota(jnp.int32, (SLOTS, 256), 1) & CZ) == 0
    at_z = lax.broadcasted_iota(jnp.int32, (SLOTS, CELLS), 1) & (CZ - 1)
    for c in range(6):
        wides = []
        for ref in wide_refs:
            value = ref[c] * SCALES[c]
            wides.append(jnp.concatenate([value, jnp.zeros((SLOTS, 64), F32)], axis=1))
        own[c] = wides[0][:, 32:160]
        layers = {0: wides[0]}
        if len(wides) > 1:
            above, below = wides[1:]
            layers[1] = jnp.where(
                low, pltpu.roll(wides[0], 256 - CZ, 1), pltpu.roll(above, CZ, 1)
            )
            layers[-1] = jnp.where(
                low, pltpu.roll(below, 256 - CZ, 1), pltpu.roll(wides[0], CZ, 1)
            )
        for n, (a, b) in enumerate(shifts):
            value = layers[b][:, 32 * (a + 1) : 32 * (a + 1) + CELLS]
            if c == 0:
                value = value + float(a)
            if c == 1:
                value = value + float(b)
            up = jnp.where(
                at_z == CZ - 1, pltpu.roll(value, CZ - 1, 1), pltpu.roll(value, CELLS - 1, 1)
            )
            down = jnp.where(at_z == 0, pltpu.roll(value, CELLS - CZ + 1, 1), pltpu.roll(value, 1, 1))
            if c == 2:
                up = up + 1.0
                down = down - 1.0
            for m, part in enumerate((down, value, up)):
                row = (n * 3 + m) * SLOTS
                others[c, row : row + SLOTS] = part

    def step(n, sums):
        sums = list(sums)
        for jj in range(unroll):
            j = n * unroll + jj
            other = [others[c, pl.ds(j, 8, stride=0), :] for c in range(6)]
            for block in range(4):
                mine = [own[c, 8 * block : 8 * block + 8, :] for c in range(6)]
                force = pair_term(mine, other)
                for d in range(3):
                    sums[block * 3 + d] = sums[block * 3 + d] + force[d]
        return tuple(sums)

    zero = jnp.zeros((8, CELLS), F32)
    steps = len(shifts) * 3 * SLOTS // unroll
    sums = lax.fori_loop(0, steps, step, (zero,) * 12)
    for d in range(3):
        out_ref[d] = jnp.concatenate([sums[block * 3 + d] for block in range(4)], axis=0).T


def pair_forces(wides, shifts, unroll=4):
    rows = len(shifts) * 3 * SLOTS
    pairs = rows * SLOTS * CELLS
    return pl.pallas_call(
        functools.partial(pair_kernel, shifts=tuple(shifts), unroll=unroll),
        out_shape=jax.ShapeDtypeStruct((3, CELLS, SLOTS), F32),
        in_specs=[VMEM] * len(wides),
        out_specs=VMEM,
        scratch_shapes=[pltpu.VMEM((6, rows + 8, CELLS), F32), pltpu.VMEM((6, SLOTS, CELLS), F32)],
        compiler_params=params(),
        cost_estimate=pl.CostEstimate(flops=70 * pairs, bytes_accessed=1 << 20, transcendentals=0),
    )(*wides)


def ring(axis, step):
    count = lax.axis_size(axis)
    return [(i, (i + step) % count) for i in range(count)]


def body(positions, charges, types, counts, eps_type, sig_type):
    tab = tables()
    slot_last = lambda a: jnp.moveaxis(a, -4, -1).reshape(a.shape[:-4] + (CELLS, SLOTS))
    atoms, rows = pl.pallas_call(
        table_kernel,
        out_shape=(
            jax.ShapeDtypeStruct((6, SLOTS, CELLS), F32),
            jax.ShapeDtypeStruct((4, GROUPS, 128), F32),
        ),
        in_specs=[VMEM] * 4 + [SMEM] * 2,
        out_specs=(VMEM, VMEM),
        compiler_params=params(),
    )(
        slot_last(positions),
        slot_last(charges),
        slot_last(types),
        counts.reshape(1, CELLS),
        eps_type,
        sig_type,
    )
    right = lax.ppermute(atoms[:, :, CELLS - 32 :], "gx", ring("gx", 1))
    left = lax.ppermute(atoms[:, :, :32], "gx", ring("gx", -1))

    spread = pl.pallas_call(
        spread_kernel,
        out_shape=jax.ShapeDtypeStruct((LZ, BLOCK), F32),
        in_specs=[VMEM] * 3,
        out_specs=VMEM,
        scratch_shapes=[pltpu.VMEM((BY, 40, LZ), F32), pltpu.VMEM((BLOCK, LZ), F32)],
        compiler_params=params(),
    )(rows, *tab["tz"])
    lines = lax.all_to_all(spread, ("gx", "gy"), split_axis=0, concat_axis=0, tiled=True)

    wide = jnp.concatenate([right, atoms, left], axis=2)
    below = lax.ppermute(wide, "gy", ring("gy", 1))
    above = lax.ppermute(wide, "gy", ring("gy", -1))
    near = pair_forces((wide,), [(a, 0) for a in (-1, 0, 1)])

    index = lax.axis_index("gx") * DY + lax.axis_index("gy")
    plane = lax.dynamic_index_in_dim(jnp.asarray(tab["plane"]), index, 0, keepdims=False)
    fields = pl.pallas_call(
        plane_kernel,
        out_shape=jax.ShapeDtypeStruct((DX * DY, 3 * BLOCK), F32),
        in_specs=[SMEM] + [VMEM] * 11,
        out_specs=VMEM,
        scratch_shapes=[pltpu.VMEM((DX, BY * DY, 128), F32)],
        compiler_params=params(),
    )(plane, lines, *tab["tx"], *tab["ty"], *tab["iy"], *tab["ix"], tab["kx2"], tab["ky2"])
    fields = lax.all_to_all(fields, ("gx", "gy"), split_axis=0, concat_axis=0, tiled=True)
    far = pair_forces((wide, above, below), [(a, b) for b in (-1, 1) for a in (-1, 0, 1)])

    mesh_force = pl.pallas_call(
        force_kernel,
        out_shape=jax.ShapeDtypeStruct((3, CELLS, SLOTS), F32),
        in_specs=[VMEM] * 5,
        out_specs=VMEM,
        scratch_shapes=[
            pltpu.VMEM((BLOCK, LZ), F32),
            pltpu.VMEM((3, BY, 40, LZ), F32),
            pltpu.VMEM((3, GROUPS, 128), F32),
        ],
        compiler_params=params(),
    )(fields, rows, *tab["tz"], tab["swap"])

    slot_first = lambda a: jnp.moveaxis(a.reshape(3, CX, CY, CZ, SLOTS), -1, 1)
    return slot_first(near + far), slot_first(mesh_force)


def solution(mesh):
    placed = (
        P(None, None, "gx", "gy", None),
        P(None, "gx", "gy", None),
        P(None, "gx", "gy", None),
        P("gx", "gy", None),
        P(),
        P(),
    )
    return jax.shard_map(
        body,
        mesh=mesh,
        in_specs=placed,
        out_specs=(P(None, None, "gx", "gy", None), P(None, None, "gx", "gy", None)),
        check_vma=False,
    )
```

time: 880 us -> 119 us (0.14); the launches traced: 870 us -> 118 us
  other arithmetic: 420 us -> 0.84 us
  local copies, waits for them, and re-layouts: 240 us -> 11.7 us
  matrix products: 130 us -> 0 us
  Pallas kernels: 0 us -> 55.3 us
  starting transfers between devices: 61.8 us -> 23.2 us
  waiting for transfers between devices: 12.7 us -> 25.8 us
    reduce_sum x15 -> x0, other arithmetic: 351 us -> none  [the longest x14 349 us: cell_forces(): jnp.sum(2.0 * derivative * separation[component], axis=1)]
    dot_general x20 -> x0, matrix products: 129 us -> none  [the longest x1 53.9 us: interpolate(): jnp.einsum('dczbyax,xpabc->dzypabc', windowed, weight_x, precision=HIGHEST)]
    pallas_call x0 -> x6, Pallas kernels: none -> 55.3 us  [the longest x2 35.5 us: pair_forces(): pl.pallas_call(functools.partial(pair_kernel, shifts=tuple(shifts), unrol...]
    reshape x4 -> x1, local copies, waits for them, and re-layouts: 55.9 us -> 0.77 us  [body(): counts.reshape(1, CELLS)]
    slice x20 -> x1, local copies, waits for them, and re-layouts: 54.9 us -> 0.08 us  [body(): right = lax.ppermute(atoms[:, :, CELLS - 32:], 'gx', ring('gx', 1))]
    add x6 -> x0, local copies, waits for them, and re-layouts: 43.9 us -> none  [the longest x1 38.6 us: fold_wrap(): first_half + jnp.roll(second_half, 1, axis=-2)]
    unnamed x401 -> x42, local copies, waits for them, and re-layouts: 39.8 us -> 6.77 us
    all_to_all x8 -> x2, starting transfers between devices: 45.5 us -> 15.7 us  [the longest x1 11.5 us: body(): lax.all_to_all(spread, ('gx', 'gy'), split_axis=0, concat_axis=0, tiled=T...]
  transfers between devices with their start and end apart: 16 -> 6, of which waited for: 6 -> 3; matrix products, arithmetic and copies ran while one was open for 48% -> 1% of each run, Pallas kernels for 0% -> 30%
where the time goes in v1:
time: 119 us; the launch traced here: 118 us
  Pallas kernels  55.3 us (46%)
  waiting for transfers between devices  25.8 us (22%)
  starting transfers between devices  23.2 us (19%)
  local copies, waits for them, and re-layouts  11.7 us (10%)
    pallas_call x2, Pallas kernels, pair_forces(): pl.pallas_call(functools.partial(pair_kernel, shifts=tuple(shifts), unrol...  35.5 us
    all_to_all x1, waiting for transfers between devices, body(): lax.all_to_all(spread, ('gx', 'gy'), split_axis=0, concat_axis=0, tiled=T...  11.9 us
    ppermute x1, waiting for transfers between devices, body(): right = lax.ppermute(atoms[:, :, CELLS - 32:], 'gx', ring('gx', 1))  11.6 us
    all_to_all x1, starting transfers between devices, body(): lax.all_to_all(spread, ('gx', 'gy'), split_axis=0, concat_axis=0, tiled=T...  11.5 us
    pallas_call x1, Pallas kernels, body(): pl.pallas_call(force_kernel, out_shape=jax.ShapeDtypeStruct((3, CELLS, SL...  8.51 us
    unnamed x42, local copies, waits for them, and re-layouts  6.77 us
    pallas_call x1, Pallas kernels, body(): pl.pallas_call(plane_kernel, out_shape=jax.ShapeDtypeStruct((DX * DY, 3 *...  5.6 us
    pallas_call x1, Pallas kernels, body(): pl.pallas_call(spread_kernel, out_shape=jax.ShapeDtypeStruct((LZ, BLOCK),...  4.71 us
  transfers between devices with their start and end apart: 6, of which 3 were waited for; matrix products, arithmetic and copies ran while one was open for 1% of the time, Pallas kernels for 30%

profile of v1, /device:TPU:1, one launch (start us, length us, event | category | flops | bytes accessed | tf_op | source)
XLA Modules:
  0.0 117.7 jit_solution(9504421364317662804)
XLA Ops:
  0.6 0.8 reshape.29.count_ref
  1.4 0.9 copy-done.12
  2.3 0.8 copy-done.14
  3.2 0.8 copy-done.15
  5.3 1.0 shard_map.203
  6.4 0.9 copy-done
  7.3 0.9 copy-done.2
  8.2 4.7 %shard_map.206 = f32[128,768]{1,0:T(8,128)S(1)} custom-call(f32[4,32,128]{2,1,0:T(8,128)S(1)} %get-tuple-element.5.rows_ref, bf16[4,128,48]{2,1,0:T(8,128)(2,1)S(1)} %copy-done.2, bf16[4,128,48]{2,1,0:T(8,128)(2,1)S(1)} %copy-done), custom_call_target="tpu_custom_call" | custom-call | tf_op jit(solution)/shard_map/pallas_call | solution.py:388
  13.0 1.2 copy.22
  14.2 11.5 %all-to-all-start = ((f32[128,1,768]{2,1,0:T(1,128)}), f32[128,1,768]{2,1,0:T(1,128)S(1)}, u32[]{:S(2)}, u32[]{:S(2)}) async-start(f32[128,1,768]{2,1,0:T(1,128)} %copy.22), calls=%async_computation | async-start | bytes 786432 | tf_op jit(solution)/shard_map/all_to_all | solution.py:396
  26.4 11.9 %all-to-all-done = f32[128,1,768]{2,1,0:T(1,128)S(1)} async-done(((f32[128,1,768]{2,1,0:T(1,128)}), f32[128,1,768]{2,1,0:T(1,128)S(1)}, u32[]{:S(2)}, u32[]{:S(2)}) %all-to-all-start) | async-done | bytes 393248 | tf_op jit(solution)/shard_map/all_to_all | solution.py:396
  38.4 5.6 %shard_map.207 = f32[128,2304]{1,0:T(8,128)S(1)} custom-call(f32[2]{0:T(128)S(1)} %dynamic-slice_bitcast_fusion.plane_ref, f32[128,768]{1,0:T(8,128)S(1)} %bitcast.27, bf16[8,48,256]{2,1,0:T(8,128)(2,1)S(1)} %copy-done.11, bf16[8,48,256]{2,1,0:T(8,128)(2,1)S(1)} %copy-done.10, bf16[256,320]{1,0:T(8,128)(2,1)S(1)} %copy-done.9, ...), custom_call_target="tpu_custom_call" | custom-call | tf_op jit(solution)/shard_map/pallas_call | solution.py:405
  44.0 2.2 %copy.23 = f32[128,1,2304]{2,1,0:T(1,128)} copy(f32[128,1,2304]{2,0,1:T(8,128)S(1)} %bitcast.25) | data formatting | bytes 2359296 | tf_op jit(solution)/shard_map/all_to_all | solution.py:413
  46.2 4.2 %all-to-all-start.1 = ((f32[128,1,2304]{2,1,0:T(1,128)}), f32[128,1,2304]{2,1,0:T(1,128)S(1)}, u32[]{:S(2)}, u32[]{:S(2)}) async-start(f32[128,1,2304]{2,1,0:T(1,128)} %copy.23), calls=%async_computation.1 | async-start | bytes 2359296 | tf_op jit(solution)/shard_map/all_to_all | solution.py:413
  50.5 1.6 %collective-permute-start = (f32[6,32,32]{2,1,0:T(8,128)S(1)}, f32[6,32,32]{2,1,0:T(8,128)S(1)}, u32[]{:S(2)}, u32[]{:S(2)}) collective-permute-start(f32[6,32,32]{2,1,0:T(8,128)S(1)} %get-tuple-element.6), channel_id=1, source_target_pairs={{0,16},{16,32},{32,48},{48,64},{64,80},{80,96},{96,112},{112,0},{1... | collective-permute-start | bytes 73736 | tf_op jit(solution)/shard_map/ppermute | solution.py:385
  52.1 11.6 %collective-permute-done = f32[6,32,32]{2,1,0:T(8,128)S(1)} collective-permute-done((f32[6,32,32]{2,1,0:T(8,128)S(1)}, f32[6,32,32]{2,1,0:T(8,128)S(1)}, u32[]{:S(2)}, u32[]{:S(2)}) %collective-permute-start) | collective-permute-done | bytes 24608 | tf_op jit(solution)/shard_map/ppermute | solution.py:385
  63.7 2.3 %collective-permute-done.1 = f32[6,32,32]{2,1,0:T(8,128)S(1)} collective-permute-done((f32[6,32,32]{2,1,0:T(8,128)S(1)}, f32[6,32,32]{2,1,0:T(8,128)S(1)}, u32[]{:S(2)}, u32[]{:S(2)}) %collective-permute-start.1) | collective-permute-done | bytes 24608 | tf_op jit(solution)/shard_map/ppermute | solution.py:386
  66.2 1.5 %collective-permute-start.3 = (f32[6,32,192]{2,1,0:T(8,128)S(1)}, f32[6,32,192]{2,1,0:T(8,128)S(1)}, u32[]{:S(2)}, u32[]{:S(2)}) collective-permute-start(f32[6,32,192]{2,1,0:T(8,128)S(1)} %pad_maximum_fusion.refs_0_), channel_id=1, source_target_pairs={{0,1},{1,2},{2,3},{3,4},{4,5},{5,6},{6,7},{7,8},{8,9},{9,10},{10,1... | collective-permute-start | bytes 442376 | tf_op jit(solution)/shard_map/ppermute | solution.py:399
  67.7 4.3 %collective-permute-start.2 = (f32[6,32,192]{2,1,0:T(8,128)S(1)}, f32[6,32,192]{2,1,0:T(8,128)S(1)}, u32[]{:S(2)}, u32[]{:S(2)}) collective-permute-start(f32[6,32,192]{2,1,0:T(8,128)S(1)} %pad_maximum_fusion.refs_0_), channel_id=1, source_target_pairs={{0,15},{1,0},{2,1},{3,2},{4,3},{5,4},{6,5},{7,6},{8,7},{9,8},{10,9... | collective-permute-start | bytes 442376 | tf_op jit(solution)/shard_map/ppermute | solution.py:400
  72.0 11.6 %shard_map.204 = f32[3,128,32]{2,1,0:T(8,128)S(1)} custom-call(f32[6,32,192]{2,1,0:T(8,128)S(1)} %pad_maximum_fusion.refs_0_), custom_call_target="tpu_custom_call" | custom-call | flops 82575360 | bytes 1048576 | tf_op jit(solution)/shard_map/pallas_call | solution.py:349
  83.7 23.9 %shard_map.205 = f32[3,128,32]{2,1,0:T(8,128)S(1)} custom-call(f32[6,32,192]{2,1,0:T(8,128)S(1)} %pad_maximum_fusion.refs_0_, f32[6,32,192]{2,1,0:T(8,128)S(1)} %collective-permute-done.2.refs_1_, f32[6,32,192]{2,1,0:T(8,128)S(1)} %collective-permute-done.3.refs_2_), custom_call_target="tpu_custom_call" | custom-call | flops 165150720 | bytes 1048576 | tf_op jit(solution)/shard_map/pallas_call | solution.py:349
  107.6 0.7 add.10
  108.4 0.8 copy-done.1
  109.2 8.5 %shard_map.208 = f32[3,128,32]{2,1,0:T(8,128)} custom-call(f32[128,2304]{1,0:T(8,128)S(1)} %bitcast.26, f32[4,32,128]{2,1,0:T(8,128)S(1)} %get-tuple-element.5.rows_ref, bf16[4,128,48]{2,1,0:T(8,128)(2,1)S(1)} %copy-done.3, bf16[4,128,48]{2,1,0:T(8,128)(2,1)S(1)} %copy-done.1, f32[1,128]{1,0:T(1,128)S(1)} %copy-done.17), custom_call_target="tpu_custom_call" | custom-call | tf_op jit(solution)/shard_map/pallas_call | solution.py:416
  (43 shorter events, 2.5 us)
Async XLA Ops:
  1.4 0.9 copy-start.12
  2.3 0.8 copy-start.14
  3.2 0.8 copy-start.15
  6.3 0.9 copy-start
  7.3 0.9 copy-start.2
  12.9 25.4 %copy-start.4 = (bf16[2,256,288]{2,1,0:T(8,128)(2,1)S(1)}, bf16[2,256,288]{2,1,0:T(8,128)(2,1)}, u32[]{:S(2)}) copy-start(bf16[2,256,288]{2,1,0:T(8,128)(2,1)} %constant.55.clone.ixl) | copy-start | bytes 884740
  12.9 25.4 %copy-start.5 = (bf16[2,256,288]{2,1,0:T(8,128)(2,1)S(1)}, bf16[2,256,288]{2,1,0:T(8,128)(2,1)}, u32[]{:S(2)}) copy-start(bf16[2,256,288]{2,1,0:T(8,128)(2,1)} %constant.54.clone.ixh) | copy-start | bytes 884740
  12.9 25.4 %copy-start.6 = (bf16[640,256]{1,0:T(8,128)(2,1)S(1)}, bf16[640,256]{1,0:T(8,128)(2,1)}, u32[]{:S(2)}) copy-start(bf16[640,256]{1,0:T(8,128)(2,1)} %constant.53.clone.iyl) | copy-start | bytes 983044
  12.9 25.4 %copy-start.7 = (bf16[640,256]{1,0:T(8,128)(2,1)S(1)}, bf16[640,256]{1,0:T(8,128)(2,1)}, u32[]{:S(2)}) copy-start(bf16[640,256]{1,0:T(8,128)(2,1)} %constant.52.clone.iyh) | copy-start | bytes 983044
  12.9 25.4 %copy-start.8 = (bf16[256,320]{1,0:T(8,128)(2,1)S(1)}, bf16[256,320]{1,0:T(8,128)(2,1)}, u32[]{:S(2)}) copy-start(bf16[256,320]{1,0:T(8,128)(2,1)} %constant.51.clone.tyl) | copy-start | bytes 491524
  12.9 25.4 %copy-start.9 = (bf16[256,320]{1,0:T(8,128)(2,1)S(1)}, bf16[256,320]{1,0:T(8,128)(2,1)}, u32[]{:S(2)}) copy-start(bf16[256,320]{1,0:T(8,128)(2,1)} %constant.50.clone.tyh) | copy-start | bytes 491524
  13.0 25.4 %copy-start.10 = (bf16[8,48,256]{2,1,0:T(8,128)(2,1)S(1)}, bf16[8,48,256]{2,1,0:T(8,128)(2,1)}, u32[]{:S(2)}) copy-start(bf16[8,48,256]{2,1,0:T(8,128)(2,1)} %constant.49.clone.txl) | copy-start | bytes 589828
  13.0 25.4 %copy-start.11 = (bf16[8,48,256]{2,1,0:T(8,128)(2,1)S(1)}, bf16[8,48,256]{2,1,0:T(8,128)(2,1)}, u32[]{:S(2)}) copy-start(bf16[8,48,256]{2,1,0:T(8,128)(2,1)} %constant.48.clone.txh) | copy-start | bytes 589828
  13.0 25.4 %copy-start.13 = (f32[256,128]{1,0:T(8,128)S(1)}, f32[256,128]{1,0:T(8,128)}, u32[]{:S(2)}) copy-start(f32[256,128]{1,0:T(8,128)} %constant.57.clone.ky2) | copy-start | bytes 393220
  13.0 25.4 %copy-start.16 = (f32[1,256]{1,0:T(1,128)S(1)}, f32[1,256]{1,0:T(1,128)}, u32[]{:S(2)}) copy-start(f32[1,256]{1,0:T(1,128)} %constant.56.clone.kx2) | copy-start | bytes 3076
  14.2 24.1 %all-to-all-start = ((f32[128,1,768]{2,1,0:T(1,128)}), f32[128,1,768]{2,1,0:T(1,128)S(1)}, u32[]{:S(2)}, u32[]{:S(2)}) async-start(f32[128,1,768]{2,1,0:T(1,128)} %copy.22), calls=%async_computation | async-start | bytes 786432 | tf_op jit(solution)/shard_map/all_to_all | solution.py:396
  46.2 62.1 %all-to-all-start.1 = ((f32[128,1,2304]{2,1,0:T(1,128)}), f32[128,1,2304]{2,1,0:T(1,128)S(1)}, u32[]{:S(2)}, u32[]{:S(2)}) async-start(f32[128,1,2304]{2,1,0:T(1,128)} %copy.23), calls=%async_computation.1 | async-start | bytes 2359296 | tf_op jit(solution)/shard_map/all_to_all | solution.py:413
  50.5 13.2 %collective-permute-start = (f32[6,32,32]{2,1,0:T(8,128)S(1)}, f32[6,32,32]{2,1,0:T(8,128)S(1)}, u32[]{:S(2)}, u32[]{:S(2)}) collective-permute-start(f32[6,32,32]{2,1,0:T(8,128)S(1)} %get-tuple-element.6), channel_id=1, source_target_pairs={{0,16},{16,32},{32,48},{48,64},{64,80},{80,96},{96,112},{112,0},{1... | collective-permute-start | bytes 73736 | tf_op jit(solution)/shard_map/ppermute | solution.py:385
  52.1 13.9 %collective-permute-start.1 = (f32[6,32,32]{2,1,0:T(8,128)S(1)}, f32[6,32,32]{2,1,0:T(8,128)S(1)}, u32[]{:S(2)}, u32[]{:S(2)}) collective-permute-start(f32[6,32,32]{2,1,0:T(8,128)S(1)} %get-tuple-element.7), channel_id=1, source_target_pairs={{0,112},{16,0},{32,16},{48,32},{64,48},{80,64},{96,80},{112,96},{1... | collective-permute-start | bytes 73736 | tf_op jit(solution)/shard_map/ppermute | solution.py:386
  66.2 17.5 %collective-permute-start.3 = (f32[6,32,192]{2,1,0:T(8,128)S(1)}, f32[6,32,192]{2,1,0:T(8,128)S(1)}, u32[]{:S(2)}, u32[]{:S(2)}) collective-permute-start(f32[6,32,192]{2,1,0:T(8,128)S(1)} %pad_maximum_fusion.refs_0_), channel_id=1, source_target_pairs={{0,1},{1,2},{2,3},{3,4},{4,5},{5,6},{6,7},{7,8},{8,9},{9,10},{10,1... | collective-permute-start | bytes 442376 | tf_op jit(solution)/shard_map/ppermute | solution.py:399
  67.7 16.0 %collective-permute-start.2 = (f32[6,32,192]{2,1,0:T(8,128)S(1)}, f32[6,32,192]{2,1,0:T(8,128)S(1)}, u32[]{:S(2)}, u32[]{:S(2)}) collective-permute-start(f32[6,32,192]{2,1,0:T(8,128)S(1)} %pad_maximum_fusion.refs_0_), channel_id=1, source_target_pairs={{0,15},{1,0},{2,1},{3,2},{4,3},{5,4},{6,5},{7,6},{8,7},{9,8},{10,9... | collective-permute-start | bytes 442376 | tf_op jit(solution)/shard_map/ppermute | solution.py:400
  108.3 0.9 copy-start.1
  108.3 1.0 copy-start.3
  108.3 1.0 copy-start.17
  (2 other events, 1.3 us)

commit v2 on v1

--- a/solution.py
+++ b/solution.py
@@ -25,9 +25,10 @@
 BLOCK = 768
 GROUPS = CELLS // 4
 KZ = 48
-KX = 48
+KX = 64
 VMEM = pl.BlockSpec(memory_space=pltpu.VMEM)
 SMEM = pl.BlockSpec(memory_space=pltpu.SMEM)
+ANY = pl.BlockSpec(memory_space=pl.ANY)
 
 
 def params(mib=40):
@@ -38,6 +39,16 @@
     high = array.astype(ml_dtypes.bfloat16)
     low = (array - high.astype(np.float64)).astype(ml_dtypes.bfloat16)
     return high, low
+
+
+def left_parts(array):
+    high, low = split(array)
+    return np.concatenate([high, high, low], axis=-1)
+
+
+def right_parts(array):
+    high, low = split(array)
+    return np.concatenate([high, low, high], axis=-2)
 
 
 def basis(length):
@@ -76,12 +87,13 @@
         tz[zg, :, :36] = wave(32 * zg - 2 + np.arange(36), mz, sz, LZ)
     mx, sx = basis(LX)
     my, sy = basis(LY)
-    tx = np.zeros((DX, KX, LX))
+    tx = np.zeros((DX // 2, 128, LX))
     gain_x = damping(mx, LX) * norms(mx, LX)
     ix = np.zeros((2, LX, DX * BX))
     for gx in range(DX):
         points = gx * CX * CELL - 2 + np.arange(BX)
-        tx[gx, :BX] = (wave(points, mx, sx, LX) * gain_x[:, None]).T
+        at = KX * (gx % 2)
+        tx[gx // 2, at : at + BX] = (wave(points, mx, sx, LX) * gain_x[:, None]).T
         ix[0, :, gx * BX : (gx + 1) * BX] = wave(points, mx, sx, LX)
         ix[1, :, gx * BX : (gx + 1) * BX] = wave_slope(points, mx, sx, LX)
     points = (np.arange(DY)[None, :] * CY * CELL - 2 + np.arange(BY)[:, None]).reshape(-1)
@@ -96,11 +108,11 @@
     swap = 2.0 * np.pi * np.arange(half) / LZ
     swap = np.concatenate([-swap, swap]).astype(np.float32)[None, :]
     return dict(
-        tz=split(tz),
-        tx=split(tx),
-        ty=split(ty),
-        iy=split(iy),
-        ix=split(ix),
+        tz=left_parts(tz),
+        tx=right_parts(tx).reshape(-1, LX),
+        ty=left_parts(ty),
+        iy=left_parts(iy),
+        ix=right_parts(np.concatenate([ix[0], ix[1]], axis=1)),
         kx2=kx2,
         ky2=np.broadcast_to(ky2, (LY, 128)).astype(np.float32),
         plane=plane.astype(np.float32),
@@ -113,14 +125,64 @@
     return high, (value - high.astype(F32)).astype(BF16)
 
 
-def dot3(left, right, dims=((1,), (0,))):
-    dot = lambda a, b: lax.dot_general(a, b, (dims, ((), ())), preferred_element_type=F32)
-    return dot(left[0], right[0]) + (dot(left[0], right[1]) + dot(left[1], right[0]))
-
-
-def table_kernel(pos_ref, charge_ref, type_ref, count_ref, eps_ref, sig_ref, atoms_ref, rows_ref):
+def left_split(value):
+    high, low = halves(value)
+    return jnp.concatenate([high, high, low], axis=1)
+
+
+def right_split(value, axis=0):
+    high, low = halves(value)
+    return jnp.concatenate([high, low, high], axis=axis)
+
+
+def dot(left, right, dims=((1,), (0,))):
+    return lax.dot_general(left, right, (dims, ((), ())), preferred_element_type=F32)
+
+
+def spline(offset):
+    span = jnp.abs(offset)
+    outer = jnp.maximum(2.0 - span, 0.0)
+    inner = jnp.maximum(1.0 - span, 0.0)
+    return (outer * outer * outer) * (1.0 / 6.0) - (inner * inner * inner) * (2.0 / 3.0)
+
+
+def weights(rows_ref, tz_ref, col):
+    point = (lax.broadcasted_iota(jnp.int32, (16, 128), 0) - 2).astype(F32)
+    point_z = (lax.broadcasted_iota(jnp.int32, (KZ, 128), 0) - 2).astype(F32)
+    shift = ((lax.broadcasted_iota(jnp.int32, (1, 128), 1) // SLOTS) * CELL).astype(F32)
+    modes, edges = [], []
+    for zg in range(4):
+        row = [rows_ref[c, pl.ds(col * 4 + zg, 1), :] for c in range(4)]
+        along_x = spline(row[0] - point)
+        along_y = spline(row[1] - point) * row[3]
+        along_z = spline(row[2] + shift - point_z)
+        modes.append(dot(tz_ref[zg], right_split(along_z)))
+        edges.append(jnp.concatenate([along_x, along_y], axis=0))
+    return jnp.concatenate(modes, axis=1), jnp.concatenate(edges, axis=1)
+
+
+def products(edges):
+    return (edges[16:28][:, None, :] * edges[:16][None, :, :]).reshape(192, edges.shape[1])
+
+
+def started(*copies):
+    copies = [pltpu.make_async_copy(*copy) for copy in copies]
+    for copy in copies:
+        copy.start()
+    return copies
+
+
+def spread_kernel(*refs):
+    sources, (atoms_out, spread_out, modes_out, edges_out) = refs[:7], refs[7:11]
+    pos_ref, charge_ref, type_ref, count_ref, eps_ref, sig_ref, tz_ref = refs[11:18]
+    atoms_ref, rows_ref, modes_ref, edges_ref, total, packed, turned, sems = refs[18:]
+    incoming = started(*((s, t, sems.at[n]) for n, (s, t) in enumerate(zip(sources, refs[11:18]))))
+    total[...] = jnp.zeros_like(total)
+    for copy in incoming[:-1]:
+        copy.wait()
     slots = lax.broadcasted_iota(jnp.int32, (SLOTS, CELLS), 0)
-    occupied = slots < count_ref[...]
+    counts = [count_ref[cx, cy : cy + 1, :] for cx in range(CX) for cy in range(CY)]
+    occupied = slots < jnp.concatenate(counts, axis=1)
     kinds = type_ref[...].T
     eps = jnp.zeros((SLOTS, CELLS), F32)
     sig = jnp.zeros((SLOTS, CELLS), F32)
@@ -134,114 +196,117 @@
     atoms_ref[3] = charge
     atoms_ref[4] = jnp.where(occupied, jnp.sqrt(eps), 0.0)
     atoms_ref[5] = sig
+    outgoing = started((atoms_ref, atoms_out, sems.at[7]))
     charge = charge.T
     for c in range(4):
         value = pos_ref[c] if c < 3 else charge
         value = value.reshape(GROUPS, 4, SLOTS)
         rows_ref[c] = jnp.concatenate([value[:, s, :] for s in range(4)], axis=1)
-
-
-def spline(offset):
-    span = jnp.abs(offset)
-    outer = jnp.maximum(2.0 - span, 0.0)
-    inner = jnp.maximum(1.0 - span, 0.0)
-    return (outer * outer * outer) * (1.0 / 6.0) - (inner * inner * inner) * (2.0 / 3.0)
-
-
-def weights(rows_ref, tz_high, tz_low, col, charged):
-    point = (lax.broadcasted_iota(jnp.int32, (16, 128), 0) - 2).astype(F32)
-    point_z = (lax.broadcasted_iota(jnp.int32, (KZ, 128), 0) - 2).astype(F32)
-    shift = ((lax.broadcasted_iota(jnp.int32, (1, 128), 1) // SLOTS) * CELL).astype(F32)
-    modes, planes = [], []
-    for zg in range(4):
-        row = [rows_ref[c, pl.ds(col * 4 + zg, 1), :] for c in range(4)]
-        along_x = spline(row[0] - point)
-        along_y = spline(row[1] - point)
-        if charged:
-            along_y = along_y * row[3]
-        along_z = spline(row[2] + shift - point_z)
-        modes.append(dot3((tz_high[zg], tz_low[zg]), halves(along_z)))
-        planes.append((along_y[:12, None, :] * along_x[None, :, :]).reshape(192, 128))
-    return jnp.concatenate(modes, axis=1), jnp.concatenate(planes, axis=1)
-
-
-def spread_kernel(rows_ref, tz_high, tz_low, out_ref, total, packed):
-    total[...] = jnp.zeros_like(total)
+    incoming[-1].wait()
 
     def column(col, carry):
-        modes, planes = weights(rows_ref, tz_high, tz_low, col, True)
-        part = dot3(halves(planes), halves(modes), ((1,), (1,))).reshape(12, 16, LZ)
+        modes, edges = weights(rows_ref, tz_ref, col)
+        edges_ref[col] = edges
+        high, low = halves(modes)
+        modes_ref[col] = jnp.concatenate([high, low, high], axis=0)
+        started((modes_ref.at[col], modes_out.at[col], sems.at[10 + col]))
+        modes = jnp.concatenate([high, low, high], axis=1)
+        part = dot(left_split(products(edges)), modes, ((1,), (1,))).reshape(12, 16, LZ)
         y = (col % CY) * CELL
         x = pl.multiple_of((col // CY) * CELL, CELL)
         total[pl.ds(y, 12), pl.ds(x, 16), :] += part
         return carry
 
-    lax.fori_loop(0, CX * CY, column, 0)
+    lax.fori_loop(0, CX * CY, column, 0, unroll=2)
+    outgoing += started((edges_ref, edges_out, sems.at[8]))
     for y in range(BY):
         packed[y * BX : (y + 1) * BX, :] = total[y, :BX, :]
     packed[BX * BY :, :] = jnp.zeros((BLOCK - BX * BY, LZ), F32)
-    out_ref[...] = packed[...].T
-
-
-def plane_kernel(
-    plane_ref, in_ref, txh, txl, tyh, tyl, iyh, iyl, ixh, ixl, kx2, ky2, out_ref, stacked
-):
+    turned[...] = packed[...].T
+    outgoing += started((turned, spread_out.at[:, 0, :], sems.at[9]))
+    for copy in outgoing:
+        copy.wait()
+    for col in range(CX * CY):
+        pltpu.make_async_copy(modes_ref.at[col], modes_out.at[col], sems.at[10 + col]).wait()
+
+
+def plane_kernel(plane_ref, in_ref, *refs):
+    sources, out_ref, held = refs[:6], refs[6], refs[7:13]
+    lines, stacked, turned, sems = refs[13:]
+    tx, ty, iy, ix, kx2, ky2 = held
+    (arrival,) = started((in_ref.at[:, 0, :], lines, sems.at[3]))
+    constants = started(*((s, t, sems.at[4 + n]) for n, (s, t) in enumerate(zip(sources, held))))
+    arrival.wait()
     for y in range(BY):
-        value = in_ref[:, y * BX : y * BX + KX]
+        value = lines[:, y * BX : y * BX + KX]
         for gx in range(DX):
-            stacked[gx, y * DY : (y + 1) * DY, :KX] = value[gx * DY : (gx + 1) * DY]
-    lines = jnp.zeros((BY * DY, LX), F32)
-    for gx in range(DX):
-        lines = lines + dot3(halves(stacked[gx, :, :KX]), (txh[gx], txl[gx]))
-    modes = dot3((tyh[...], tyl[...]), halves(lines))
+            at = KX * (gx % 2)
+            stacked[gx // 2, y * DY : (y + 1) * DY, at : at + KX] = value[gx * DY : (gx + 1) * DY]
+    pairs = jnp.concatenate([left_split(stacked[n]) for n in range(DX // 2)], axis=1)
+    for copy in constants:
+        copy.wait()
+    modes = dot(ty[...], right_split(dot(pairs, tx[...])))
     k2 = kx2[...] + jnp.concatenate([ky2[...], ky2[...]], axis=1) + plane_ref[0]
     positive = k2 > 0.0
     modes = jnp.where(positive, modes * (plane_ref[1] / jnp.where(positive, k2, 1.0)), 0.0)
-    both = dot3((iyh[...], iyl[...]), halves(modes))
+    both = dot(iy[...], right_split(modes))
     rows = BY * DY
-    plain = halves(both[:rows])
-    slope = halves(both[rows:])
-    fields = (
-        dot3(plain, (ixh[1], ixl[1])),
-        dot3(slope, (ixh[0], ixl[0])),
-        dot3(plain, (ixh[0], ixl[0])),
-    )
+    width = DX * BX
+    plain = dot(left_split(both[:rows]), ix[...])
+    slope = dot(left_split(both[rows:]), ix[:, :width])
+    fields = (plain[:, width:], slope, plain[:, :width])
+    outgoing = []
     for d in range(3):
-        out_ref[:, d * BLOCK + BX * BY : (d + 1) * BLOCK] = jnp.zeros(
-            (DX * DY, BLOCK - BX * BY), F32
-        )
+        turned[d, :, BX * BY :] = jnp.zeros((DX * DY, BLOCK - BX * BY), F32)
         for gx in range(DX):
             piece = fields[d][:, gx * BX : (gx + 1) * BX]
             for y in range(BY):
-                lane = d * BLOCK + y * BX
-                out_ref[gx * DY : (gx + 1) * DY, lane : lane + BX] = piece[y * DY : (y + 1) * DY]
-
-
-def force_kernel(in_ref, rows_ref, tz_high, tz_low, swap_ref, out_ref, packed, padded, rows_out):
+                lane = y * BX
+                turned[d, gx * DY : (gx + 1) * DY, lane : lane + BX] = piece[y * DY : (y + 1) * DY]
+        outgoing += started(
+            (turned.at[d], out_ref.at[:, 0, d * BLOCK : (d + 1) * BLOCK], sems.at[d])
+        )
+    for copy in outgoing:
+        copy.wait()
+
+
+def force_kernel(in_ref, *refs):
+    sources, out_ref, held = refs[:3], refs[3], refs[4:7]
+    turned, packed, padded, rows_out, sems = refs[7:]
+    modes_ref, edges_ref, swap_ref = held
+    incoming = started(
+        *(
+            (in_ref.at[:, 0, d * BLOCK : (d + 1) * BLOCK], turned.at[d], sems.at[d])
+            for d in range(3)
+        )
+    )
+    kept = started(*((s, t, sems.at[3 + n]) for n, (s, t) in enumerate(zip(sources, held))))
+    kept[2].wait()
     for d in range(3):
-        value = in_ref[:, d * BLOCK : (d + 1) * BLOCK].T
+        incoming[d].wait()
+        value = turned[d].T
         if d == 2:
             value = pltpu.roll(value, LZ // 2, 1) * swap_ref[...]
         packed[...] = value
         for y in range(BY):
             padded[d, y, :BX, :] = packed[y * BX : (y + 1) * BX, :]
             padded[d, y, BX:, :] = jnp.zeros((40 - BX, LZ), F32)
+    kept[0].wait()
+    kept[1].wait()
 
     def column(col, carry):
-        modes, planes = weights(rows_ref, tz_high, tz_low, col, False)
-        modes = halves(modes)
         y = (col % CY) * CELL
         x = pl.multiple_of((col // CY) * CELL, CELL)
+        planes = products(edges_ref[col])
         for d in range(3):
             block = padded[d, pl.ds(y, 12), pl.ds(x, 16), :].reshape(192, LZ)
-            along = dot3(halves(block), modes)
+            along = dot(left_split(block), modes_ref[col])
             force = jnp.sum(along * planes, axis=0, keepdims=True)
             for zg in range(4):
-                at = pl.ds(col * 4 + zg, 1)
-                rows_out[d, at, :] = force[:, 128 * zg : 128 * (zg + 1)] * rows_ref[3, at, :]
+                rows_out[d, pl.ds(col * 4 + zg, 1), :] = force[:, 128 * zg : 128 * (zg + 1)]
         return carry
 
-    lax.fori_loop(0, CX * CY, column, 0)
+    lax.fori_loop(0, CX * CY, column, 0, unroll=2)
     for d in range(3):
         value = rows_out[d]
         pieces = [value[:, s * SLOTS : (s + 1) * SLOTS][:, None, :] for s in range(4)]
@@ -287,8 +352,8 @@
     return w * dx, w * dy, w * dz
 
 
-def pair_kernel(*refs, shifts, unroll):
-    wide_refs = refs[:-3]
+def pair_kernel(*refs, shifts, unroll, begun):
+    wide_refs = refs[begun:-3]
     out_ref, others, own = refs[-3:]
     low = (lax.broadcasted_iota(jnp.int32, (SLOTS, 256), 1) & CZ) == 0
     at_z = lax.broadcasted_iota(jnp.int32, (SLOTS, CELLS), 1) & (CZ - 1)
@@ -340,21 +405,22 @@
     steps = len(shifts) * 3 * SLOTS // unroll
     sums = lax.fori_loop(0, steps, step, (zero,) * 12)
     for d in range(3):
-        out_ref[d] = jnp.concatenate([sums[block * 3 + d] for block in range(4)], axis=0).T
-
-
-def pair_forces(wides, shifts, unroll=4):
+        force = jnp.concatenate([sums[block * 3 + d] for block in range(4)], axis=0).T
+        out_ref[d] = refs[0][d] + force if begun else force
+
+
+def pair_forces(wides, shifts, start=(), unroll=4):
     rows = len(shifts) * 3 * SLOTS
     pairs = rows * SLOTS * CELLS
     return pl.pallas_call(
-        functools.partial(pair_kernel, shifts=tuple(shifts), unroll=unroll),
+        functools.partial(pair_kernel, shifts=tuple(shifts), unroll=unroll, begun=len(start)),
         out_shape=jax.ShapeDtypeStruct((3, CELLS, SLOTS), F32),
-        in_specs=[VMEM] * len(wides),
+        in_specs=[VMEM] * (len(start) + len(wides)),
         out_specs=VMEM,
         scratch_shapes=[pltpu.VMEM((6, rows + 8, CELLS), F32), pltpu.VMEM((6, SLOTS, CELLS), F32)],
-        compiler_params=params(),
+        compiler_params=params(8),
         cost_estimate=pl.CostEstimate(flops=70 * pairs, bytes_accessed=1 << 20, transcendentals=0),
-    )(*wides)
+    )(*start, *wides)
 
 
 def ring(axis, step):
@@ -365,69 +431,96 @@
 def body(positions, charges, types, counts, eps_type, sig_type):
     tab = tables()
     slot_last = lambda a: jnp.moveaxis(a, -4, -1).reshape(a.shape[:-4] + (CELLS, SLOTS))
-    atoms, rows = pl.pallas_call(
-        table_kernel,
+    atoms, spread, modes, edges = pl.pallas_call(
+        spread_kernel,
         out_shape=(
             jax.ShapeDtypeStruct((6, SLOTS, CELLS), F32),
-            jax.ShapeDtypeStruct((4, GROUPS, 128), F32),
+            jax.ShapeDtypeStruct((LZ, 1, BLOCK), F32),
+            jax.ShapeDtypeStruct((CX * CY, 3 * LZ, 512), BF16),
+            jax.ShapeDtypeStruct((CX * CY, 32, 512), F32),
         ),
-        in_specs=[VMEM] * 4 + [SMEM] * 2,
-        out_specs=(VMEM, VMEM),
-        compiler_params=params(),
+        in_specs=[ANY] * 7,
+        out_specs=(ANY,) * 4,
+        scratch_shapes=[
+            pltpu.VMEM((3, CELLS, SLOTS), F32),
+            pltpu.VMEM((CELLS, SLOTS), F32),
+            pltpu.VMEM((CELLS, SLOTS), jnp.int32),
+            pltpu.VMEM((CX, CY, CZ), jnp.int32),
+            pltpu.SMEM(eps_type.shape, F32),
+            pltpu.SMEM(sig_type.shape, F32),
+            pltpu.VMEM(tab["tz"].shape, BF16),
+            pltpu.VMEM((6, SLOTS, CELLS), F32),
+            pltpu.VMEM((4, GROUPS, 128), F32),
+            pltpu.VMEM((CX * CY, 3 * LZ, 512), BF16),
+            pltpu.VMEM((CX * CY, 32, 512), F32),
+            pltpu.VMEM((BY, 40, LZ), F32),
+            pltpu.VMEM((BLOCK, LZ), F32),
+            pltpu.VMEM((LZ, BLOCK), F32),
+            pltpu.SemaphoreType.DMA((10 + CX * CY,)),
+        ],
+        compiler_params=params(56),
     )(
         slot_last(positions),
         slot_last(charges),
         slot_last(types),
-        counts.reshape(1, CELLS),
+        counts,
         eps_type,
         sig_type,
+        tab["tz"],
     )
-    right = lax.ppermute(atoms[:, :, CELLS - 32 :], "gx", ring("gx", 1))
-    left = lax.ppermute(atoms[:, :, :32], "gx", ring("gx", -1))
-
-    spread = pl.pallas_call(
-        spread_kernel,
-        out_shape=jax.ShapeDtypeStruct((LZ, BLOCK), F32),
-        in_specs=[VMEM] * 3,
-        out_specs=VMEM,
-        scratch_shapes=[pltpu.VMEM((BY, 40, LZ), F32), pltpu.VMEM((BLOCK, LZ), F32)],
-        compiler_params=params(),
-    )(rows, *tab["tz"])
+    before = lax.ppermute(atoms[:, :, CELLS - 32 :], "gx", ring("gx", 1))
+    after = lax.ppermute(atoms[:, :, :32], "gx", ring("gx", -1))
     lines = lax.all_to_all(spread, ("gx", "gy"), split_axis=0, concat_axis=0, tiled=True)
 
-    wide = jnp.concatenate([right, atoms, left], axis=2)
+    wide = jnp.concatenate([before, atoms, after], axis=2)
     below = lax.ppermute(wide, "gy", ring("gy", 1))
     above = lax.ppermute(wide, "gy", ring("gy", -1))
     near = pair_forces((wide,), [(a, 0) for a in (-1, 0, 1)])
+    lines, near, below, above = lax.optimization_barrier((lines, near, below, above))
 
     index = lax.axis_index("gx") * DY + lax.axis_index("gy")
     plane = lax.dynamic_index_in_dim(jnp.asarray(tab["plane"]), index, 0, keepdims=False)
     fields = pl.pallas_call(
         plane_kernel,
-        out_shape=jax.ShapeDtypeStruct((DX * DY, 3 * BLOCK), F32),
-        in_specs=[SMEM] + [VMEM] * 11,
-        out_specs=VMEM,
-        scratch_shapes=[pltpu.VMEM((DX, BY * DY, 128), F32)],
-        compiler_params=params(),
-    )(plane, lines, *tab["tx"], *tab["ty"], *tab["iy"], *tab["ix"], tab["kx2"], tab["ky2"])
+        out_shape=jax.ShapeDtypeStruct((DX * DY, 1, 3 * BLOCK), F32),
+        in_specs=[SMEM] + [ANY] * 7,
+        out_specs=ANY,
+        scratch_shapes=[
+            *(pltpu.VMEM(tab[name].shape, BF16) for name in ("tx", "ty", "iy", "ix")),
+            *(pltpu.VMEM(tab[name].shape, F32) for name in ("kx2", "ky2")),
+            pltpu.VMEM((DX * DY, BLOCK), F32),
+            pltpu.VMEM((DX // 2, BY * DY, 128), F32),
+            pltpu.VMEM((3, DX * DY, BLOCK), F32),
+            pltpu.SemaphoreType.DMA((10,)),
+        ],
+        compiler_params=params(56),
+    )(plane, lines, tab["tx"], tab["ty"], tab["iy"], tab["ix"], tab["kx2"], tab["ky2"])
     fields = lax.all_to_all(fields, ("gx", "gy"), split_axis=0, concat_axis=0, tiled=True)
-    far = pair_forces((wide, above, below), [(a, b) for b in (-1, 1) for a in (-1, 0, 1)])
+    far = pair_forces(
+        (wide, above, below), [(a, b) for b in (-1, 1) for a in (-1, 0, 1)], (near,)
+    )
+    fields, far = lax.optimization_barrier((fields, far))
 
     mesh_force = pl.pallas_call(
         force_kernel,
         out_shape=jax.ShapeDtypeStruct((3, CELLS, SLOTS), F32),
-        in_specs=[VMEM] * 5,
+        in_specs=[ANY] * 4,
         out_specs=VMEM,
         scratch_shapes=[
+            pltpu.VMEM((CX * CY, 3 * LZ, 512), BF16),
+            pltpu.VMEM((CX * CY, 32, 512), F32),
+            pltpu.VMEM((1, LZ), F32),
+            pltpu.VMEM((3, LZ, BLOCK), F32),
             pltpu.VMEM((BLOCK, LZ), F32),
             pltpu.VMEM((3, BY, 40, LZ), F32),
             pltpu.VMEM((3, GROUPS, 128), F32),
+            pltpu.SemaphoreType.DMA((6,)),
         ],
-        compiler_params=params(),
-    )(fields, rows, *tab["tz"], tab["swap"])
+        compiler_params=params(56),
+    )(fields, modes, edges, tab["swap"])
 
     slot_first = lambda a: jnp.moveaxis(a.reshape(3, CX, CY, CZ, SLOTS), -1, 1)
-    return slot_first(near + far), slot_first(mesh_force)
+    return slot_first(far), slot_first(mesh_force)
 
 
 def solution(mesh):

time: 119 us -> 93 us (0.78)
  waiting for transfers between devices: 25.8 us -> 4.54 us
  local copies, waits for them, and re-layouts: 11.7 us -> 4.03 us
  starting transfers between devices: 23.2 us -> 27 us
    all_to_all x1, waiting for transfers between devices: 11.9 us -> 0.01 us  [body(): lax.all_to_all(spread, ('gx', 'gy'), split_axis=0, concat_axis=0, tiled=T...]
    ppermute x2, waiting for transfers between devices: 13.9 us -> 4.53 us  [the longest x1 2.41 us: body(): before = lax.ppermute(atoms[:, :, CELLS - 32:], 'gx', ring('gx', 1))]
    unnamed x42 -> x6, local copies, waits for them, and re-layouts: 6.77 us -> 1.78 us
    all_to_all x1, starting transfers between devices: 4.18 us -> 8.43 us  [body(): lax.all_to_all(fields, ('gx', 'gy'), split_axis=0, concat_axis=0, tiled=T...]
    all_to_all x2 -> x0, local copies, waits for them, and re-layouts: 3.4 us -> none  [the longest x1 2.24 us: body(): lax.all_to_all(fields, ('gx', 'gy'), split_axis=0, concat_axis=0, tiled=T...]
    ppermute x1, starting transfers between devices: 1.52 us -> 0.01 us  [body(): below = lax.ppermute(wide, 'gy', ring('gy', 1))]
    pallas_call x3 -> x2, Pallas kernels: 11.3 us -> 12.8 us  [the longest x1 6.79 us: body(): pl.pallas_call(plane_kernel, out_shape=jax.ShapeDtypeStruct((DX * DY, 1,...]
    pallas_call x1, Pallas kernels: 8.51 us -> 7.23 us  [body(): pl.pallas_call(force_kernel, out_shape=jax.ShapeDtypeStruct((3, CELLS, SL...]
  transfers between devices with their start and end apart: 6 -> 6, of which waited for: 3 -> 2; matrix products, arithmetic and copies ran while one was open for 1% -> 3% of each run, Pallas kernels for 30% -> 39%
where the time goes in v2:
time: 93 us; the launch traced here: 92.7 us
  Pallas kernels  56.2 us (60%)
  starting transfers between devices  27 us (29%)
  waiting for transfers between devices  4.54 us (5%)
  local copies, waits for them, and re-layouts  4.03 us (4%)
    pallas_call x2, Pallas kernels, pair_forces(): pl.pallas_call(functools.partial(pair_kernel, shifts=tuple(shifts), unrol...  36.2 us
    all_to_all x1, starting transfers between devices, body(): lax.all_to_all(spread, ('gx', 'gy'), split_axis=0, concat_axis=0, tiled=T...  11.5 us
    all_to_all x1, starting transfers between devices, body(): lax.all_to_all(fields, ('gx', 'gy'), split_axis=0, concat_axis=0, tiled=T...  8.43 us
    pallas_call x1, Pallas kernels, body(): pl.pallas_call(force_kernel, out_shape=jax.ShapeDtypeStruct((3, CELLS, SL...  7.23 us
    pallas_call x1, Pallas kernels, body(): pl.pallas_call(plane_kernel, out_shape=jax.ShapeDtypeStruct((DX * DY, 1,...  6.79 us
    pallas_call x1, Pallas kernels, body(): pl.pallas_call(spread_kernel, out_shape=(jax.ShapeDtypeStruct((6, SLOTS,...  6.04 us
    ppermute x1, starting transfers between devices, body(): above = lax.ppermute(wide, 'gy', ring('gy', -1))  5.45 us
    ppermute x1, waiting for transfers between devices, body(): before = lax.ppermute(atoms[:, :, CELLS - 32:], 'gx', ring('gx', 1))  2.41 us
  transfers between devices with their start and end apart: 6, of which 2 were waited for; matrix products, arithmetic and copies ran while one was open for 3% of the time, Pallas kernels for 39%

profile of v2, /device:TPU:1, one launch (start us, length us, event | category | flops | bytes accessed | tf_op | source)
XLA Modules:
  0.0 92.7 jit_solution(17641827483140686170)
XLA Ops:
  0.6 6.0 %shard_map.158 = (f32[6,32,128]{2,1,0:T(8,128)}, f32[128,1,768]{2,1,0:T(1,128)}, bf16[8,384,512]{2,1,0:T(8,128)(2,1)}, f32[8,32,512]{2,1,0:T(8,128)}) custom-call(f32[3,128,32]{2,1,0:T(8,128)} %bitcast.17, f32[128,32]{1,0:T(8,128)} %bitcast.20, s32[128,32]{1,0:T(8,128)} %bitcast.21, s32[4,2,16]{2,1,0:T(2,128)} %refs_3_.2, f32[64]{0:T(128)} %refs_4_.2, ...), custom_call_target="tpu_custom_call" | custom-call | tf_op jit(solution)/shard_map/pallas_call | solution.py:434
  6.7 0.0 copy-start.2
  6.7 11.5 %all-to-all-start = ((f32[128,1,768]{2,1,0:T(1,128)}), f32[128,1,768]{2,1,0:T(1,128)S(1)}, u32[]{:S(2)}, u32[]{:S(2)}) async-start(f32[128,1,768]{2,1,0:T(1,128)} %get-tuple-element.12), calls=%async_computation | async-start | bytes 786432 | tf_op jit(solution)/shard_map/all_to_all | solution.py:473
  18.2 1.1 %fusion = (f32[6,32,32]{2,1,0:T(8,128)S(1)}, f32[6,32,32]{2,1,0:T(8,128)S(1)}) fusion(f32[6,32,128]{2,1,0:T(8,128)} %get-tuple-element.13), kind=kLoop, calls=%fused_computation.2 | loop fusion | bytes 98304 | tf_op jit(solution)/shard_map/slice | solution.py:471
  19.3 1.6 %collective-permute-start = (f32[6,32,32]{2,1,0:T(8,128)S(1)}, f32[6,32,32]{2,1,0:T(8,128)S(1)}, u32[]{:S(2)}, u32[]{:S(2)}) collective-permute-start(f32[6,32,32]{2,1,0:T(8,128)S(1)} %get-tuple-element.22), channel_id=1, source_target_pairs={{0,16},{16,32},{32,48},{48,64},{64,80},{80,96},{96,112},{112,0},{1... | collective-permute-start | bytes 73736 | tf_op jit(solution)/shard_map/ppermute | solution.py:471
  20.9 0.0 collective-permute-start.1
  20.9 2.4 %collective-permute-done = f32[6,32,32]{2,1,0:T(8,128)S(1)} collective-permute-done((f32[6,32,32]{2,1,0:T(8,128)S(1)}, f32[6,32,32]{2,1,0:T(8,128)S(1)}, u32[]{:S(2)}, u32[]{:S(2)}) %collective-permute-start) | collective-permute-done | bytes 24608 | tf_op jit(solution)/shard_map/ppermute | solution.py:471
  23.3 2.1 %collective-permute-done.1 = f32[6,32,32]{2,1,0:T(8,128)S(1)} collective-permute-done((f32[6,32,32]{2,1,0:T(8,128)S(1)}, f32[6,32,32]{2,1,0:T(8,128)S(1)}, u32[]{:S(2)}, u32[]{:S(2)}) %collective-permute-start.1) | collective-permute-done | bytes 24608 | tf_op jit(solution)/shard_map/ppermute | solution.py:472
  25.4 0.0 copy-done.2
  25.4 0.1 pad_maximum_fusion.refs_0_.refs_1_
  25.6 5.5 %collective-permute-start.3 = (f32[6,32,192]{2,1,0:T(8,128)S(1)}, f32[6,32,192]{2,1,0:T(8,128)S(1)}, u32[]{:S(2)}, u32[]{:S(2)}) collective-permute-start(f32[6,32,192]{2,1,0:T(8,128)S(1)} %pad_maximum_fusion.refs_0_.refs_1_), channel_id=1, source_target_pairs={{0,15},{1,0},{2,1},{3,2},{4,3},{5,4},{6,5},{7,6},{8,7},{9,8},{10,9... | collective-permute-start | bytes 442376 | tf_op jit(solution)/shard_map/ppermute | solution.py:477
  31.0 0.0 collective-permute-start.2
  31.0 1.2 %dynamic-slice_bitcast_fusion.plane_ref = f32[2]{0:T(128)} fusion(f32[128,2]{1,0:T(8,128)} %constant.36.clone, s32[]{:T(128)S(6)} %select_n.4), kind=kLoop, calls=%fused_computation.1 | loop fusion | bytes 20 | tf_op jit(solution)/shard_map/jit(dynamic_index_in_dim)/squeeze | solution.py:482
  32.2 11.6 %shard_map.159.refs_0_ = f32[3,128,32]{2,1,0:T(8,128)S(1)} custom-call(f32[6,32,192]{2,1,0:T(8,128)S(1)} %pad_maximum_fusion.refs_0_.refs_1_), custom_call_target="tpu_custom_call" | custom-call | flops 82575360 | bytes 1048576 | tf_op jit(solution)/shard_map/pallas_call | solution.py:415
  43.9 0.0 collective-permute-done.3.refs_2_
  43.9 0.0 collective-permute-done.2.refs_3_
  43.9 0.0 all-to-all-done.in_ref
  43.9 0.7 copy-done.1
  44.6 6.8 %shard_map.160 = f32[128,1,2304]{2,1,0:T(1,128)} custom-call(f32[2]{0:T(128)} %dynamic-slice_bitcast_fusion.plane_ref, f32[128,1,768]{2,1,0:T(1,128)} %copy-done.1, bf16[1536,256]{1,0:T(8,128)(2,1)} %constant.37.clone.refs_0_, bf16[256,960]{1,0:T(8,128)(2,1)} %constant.38.clone.refs_1_, bf16[640,768]{1,0:T(8,128)(2,1)} %constant.39.clone.refs_2_, ...), custom_call_target="tpu_custom_call" | custom-call | tf_op jit(solution)/shard_map/pallas_call | solution.py:483
  51.4 8.4 %all-to-all-start.1 = ((f32[128,1,2304]{2,1,0:T(1,128)}), f32[128,1,2304]{2,1,0:T(1,128)S(1)}, u32[]{:S(2)}, u32[]{:S(2)}) async-start(f32[128,1,2304]{2,1,0:T(1,128)} %shard_map.160), calls=%async_computation.1 | async-start | bytes 2359296 | tf_op jit(solution)/shard_map/all_to_all | solution.py:498
  59.9 24.6 %shard_map.161 = f32[3,128,32]{2,1,0:T(8,128)} custom-call(f32[3,128,32]{2,1,0:T(8,128)S(1)} %shard_map.159.refs_0_, f32[6,32,192]{2,1,0:T(8,128)S(1)} %pad_maximum_fusion.refs_0_.refs_1_, f32[6,32,192]{2,1,0:T(8,128)S(1)} %collective-permute-done.3.refs_2_, f32[6,32,192]{2,1,0:T(8,128)S(1)} %collective-permute-done.2.refs_3_), custom_call_target="tpu_custom_call" | custom-call | flops 165150720 | bytes 1048576 | tf_op jit(solution)/shard_map/pallas_call | solution.py:415
  84.4 0.0 all-to-all-done.1.in_ref
  84.4 1.0 %copy-done = f32[128,1,2304]{2,1,0:T(1,128)} copy-done((f32[128,1,2304]{2,1,0:T(1,128)}, f32[128,1,2304]{2,1,0:T(1,128)S(1)}, u32[]{:S(2)}) %copy-start) | copy-done | bytes 1179672
  85.5 7.2 %shard_map.162 = f32[3,128,32]{2,1,0:T(8,128)} custom-call(f32[128,1,2304]{2,1,0:T(1,128)} %copy-done, bf16[8,384,512]{2,1,0:T(8,128)(2,1)} %get-tuple-element.20.refs_0_, f32[8,32,512]{2,1,0:T(8,128)} %get-tuple-element.21.refs_1_, f32[1,128]{1,0:T(1,128)} %constant.43.clone.refs_2_), custom_call_target="tpu_custom_call" | custom-call | tf_op jit(solution)/shard_map/pallas_call | solution.py:504
  (2 shorter events, 0.0 us)
Async XLA Ops:
  6.7 18.8 %copy-start.2 = (f32[6,32,128]{2,1,0:T(8,128)S(1)}, f32[6,32,128]{2,1,0:T(8,128)}, u32[]{:S(2)}) copy-start(f32[6,32,128]{2,1,0:T(8,128)} %get-tuple-element.13) | copy-start | bytes 294916
  6.7 37.2 %all-to-all-start = ((f32[128,1,768]{2,1,0:T(1,128)}), f32[128,1,768]{2,1,0:T(1,128)S(1)}, u32[]{:S(2)}, u32[]{:S(2)}) async-start(f32[128,1,768]{2,1,0:T(1,128)} %get-tuple-element.12), calls=%async_computation | async-start | bytes 786432 | tf_op jit(solution)/shard_map/all_to_all | solution.py:473
  19.3 4.1 %collective-permute-start = (f32[6,32,32]{2,1,0:T(8,128)S(1)}, f32[6,32,32]{2,1,0:T(8,128)S(1)}, u32[]{:S(2)}, u32[]{:S(2)}) collective-permute-start(f32[6,32,32]{2,1,0:T(8,128)S(1)} %get-tuple-element.22), channel_id=1, source_target_pairs={{0,16},{16,32},{32,48},{48,64},{64,80},{80,96},{96,112},{112,0},{1... | collective-permute-start | bytes 73736 | tf_op jit(solution)/shard_map/ppermute | solution.py:471
  20.9 4.5 %collective-permute-start.1 = (f32[6,32,32]{2,1,0:T(8,128)S(1)}, f32[6,32,32]{2,1,0:T(8,128)S(1)}, u32[]{:S(2)}, u32[]{:S(2)}) collective-permute-start(f32[6,32,32]{2,1,0:T(8,128)S(1)} %get-tuple-element.23), channel_id=1, source_target_pairs={{0,112},{16,0},{32,16},{48,32},{64,48},{80,64},{96,80},{112,96},{1... | collective-permute-start | bytes 73736 | tf_op jit(solution)/shard_map/ppermute | solution.py:472
  25.6 18.3 %collective-permute-start.3 = (f32[6,32,192]{2,1,0:T(8,128)S(1)}, f32[6,32,192]{2,1,0:T(8,128)S(1)}, u32[]{:S(2)}, u32[]{:S(2)}) collective-permute-start(f32[6,32,192]{2,1,0:T(8,128)S(1)} %pad_maximum_fusion.refs_0_.refs_1_), channel_id=1, source_target_pairs={{0,15},{1,0},{2,1},{3,2},{4,3},{5,4},{6,5},{7,6},{8,7},{9,8},{10,9... | collective-permute-start | bytes 442376 | tf_op jit(solution)/shard_map/ppermute | solution.py:477
  31.0 12.8 %collective-permute-start.2 = (f32[6,32,192]{2,1,0:T(8,128)S(1)}, f32[6,32,192]{2,1,0:T(8,128)S(1)}, u32[]{:S(2)}, u32[]{:S(2)}) collective-permute-start(f32[6,32,192]{2,1,0:T(8,128)S(1)} %pad_maximum_fusion.refs_0_.refs_1_), channel_id=1, source_target_pairs={{0,1},{1,2},{2,3},{3,4},{4,5},{5,6},{6,7},{7,8},{8,9},{9,10},{10,1... | collective-permute-start | bytes 442376 | tf_op jit(solution)/shard_map/ppermute | solution.py:476
  43.9 0.7 copy-start.1
  51.4 33.0 %all-to-all-start.1 = ((f32[128,1,2304]{2,1,0:T(1,128)}), f32[128,1,2304]{2,1,0:T(1,128)S(1)}, u32[]{:S(2)}, u32[]{:S(2)}) async-start(f32[128,1,2304]{2,1,0:T(1,128)} %shard_map.160), calls=%async_computation.1 | async-start | bytes 2359296 | tf_op jit(solution)/shard_map/all_to_all | solution.py:498
  84.4 1.0 %copy-start = (f32[128,1,2304]{2,1,0:T(1,128)}, f32[128,1,2304]{2,1,0:T(1,128)S(1)}, u32[]{:S(2)}) copy-start(f32[128,1,2304]{2,1,0:T(1,128)S(1)} %all-to-all-done.1.in_ref) | copy-start | bytes 3538948

commit v3 on v2

--- a/solution.py
+++ b/solution.py
@@ -19,6 +19,7 @@
 SLOTS = 32
 CX, CY, CZ = 4, 2, 16
 CELLS = CX * CY * CZ
+COLUMNS = CY * CZ
 DX, DY = 8, 16
 LX, LY, LZ = 256, 256, 128
 BX, BY = CX * CELL + 4, CY * CELL + 4
@@ -26,6 +27,9 @@
 GROUPS = CELLS // 4
 KZ = 48
 KX = 64
+LENGTH = math.sqrt(GEWALD * GEWALD * math.log2(math.e))
+FAR = CUT * LENGTH * LENGTH
+SCALES = (LENGTH, LENGTH, LENGTH, 1.0, 1.0 / math.sqrt(8.0 * FAR * LENGTH), 0.5 * LENGTH)
 VMEM = pl.BlockSpec(memory_space=pltpu.VMEM)
 SMEM = pl.BlockSpec(memory_space=pltpu.SMEM)
 ANY = pl.BlockSpec(memory_space=pl.ANY)
@@ -172,12 +176,11 @@
     return copies
 
 
-def spread_kernel(*refs):
-    sources, (atoms_out, spread_out, modes_out, edges_out) = refs[:7], refs[7:11]
-    pos_ref, charge_ref, type_ref, count_ref, eps_ref, sig_ref, tz_ref = refs[11:18]
-    atoms_ref, rows_ref, modes_ref, edges_ref, total, packed, turned, sems = refs[18:]
-    incoming = started(*((s, t, sems.at[n]) for n, (s, t) in enumerate(zip(sources, refs[11:18]))))
-    total[...] = jnp.zeros_like(total)
+def table_kernel(*refs):
+    sources, (atoms_ref, first_ref, last_ref, rows_ref, tz_ref) = refs[:7], refs[7:12]
+    pos_ref, charge_ref, type_ref, count_ref, eps_ref, sig_ref, sems = refs[12:]
+    targets = refs[12:18] + (tz_ref,)
+    incoming = started(*((s, t, sems.at[n]) for n, (s, t) in enumerate(zip(sources, targets))))
     for copy in incoming[:-1]:
         copy.wait()
     slots = lax.broadcasted_iota(jnp.int32, (SLOTS, CELLS), 0)
@@ -191,12 +194,12 @@
         eps = jnp.where(match, eps_ref[kind], eps)
         sig = jnp.where(match, sig_ref[kind], sig)
     charge = jnp.where(occupied, charge_ref[...].T, 0.0)
-    for d in range(3):
-        atoms_ref[d] = pos_ref[d].T
-    atoms_ref[3] = charge
-    atoms_ref[4] = jnp.where(occupied, jnp.sqrt(eps), 0.0)
-    atoms_ref[5] = sig
-    outgoing = started((atoms_ref, atoms_out, sems.at[7]))
+    root = jnp.where(occupied, jnp.sqrt(eps), 0.0)
+    for c, value in enumerate([pos_ref[d].T for d in range(3)] + [charge, root, sig]):
+        value = value * SCALES[c]
+        atoms_ref[c] = value
+        first_ref[c] = value[:, :COLUMNS]
+        last_ref[c] = value[:, CELLS - COLUMNS :]
     charge = charge.T
     for c in range(4):
         value = pos_ref[c] if c < 3 else charge
@@ -204,12 +207,17 @@
         rows_ref[c] = jnp.concatenate([value[:, s, :] for s in range(4)], axis=1)
     incoming[-1].wait()
 
+
+def spread_kernel(
+    rows_ref, tz_ref, spread_out, modes_ref, edges_out, total, packed, turned, edges_ref, sems
+):
+    total[...] = jnp.zeros_like(total)
+
     def column(col, carry):
         modes, edges = weights(rows_ref, tz_ref, col)
         edges_ref[col] = edges
         high, low = halves(modes)
         modes_ref[col] = jnp.concatenate([high, low, high], axis=0)
-        started((modes_ref.at[col], modes_out.at[col], sems.at[10 + col]))
         modes = jnp.concatenate([high, low, high], axis=1)
         part = dot(left_split(products(edges)), modes, ((1,), (1,))).reshape(12, 16, LZ)
         y = (col % CY) * CELL
@@ -218,16 +226,14 @@
         return carry
 
     lax.fori_loop(0, CX * CY, column, 0, unroll=2)
-    outgoing += started((edges_ref, edges_out, sems.at[8]))
+    outgoing = started((edges_ref, edges_out, sems.at[0]))
     for y in range(BY):
         packed[y * BX : (y + 1) * BX, :] = total[y, :BX, :]
     packed[BX * BY :, :] = jnp.zeros((BLOCK - BX * BY, LZ), F32)
     turned[...] = packed[...].T
-    outgoing += started((turned, spread_out.at[:, 0, :], sems.at[9]))
+    outgoing += started((turned, spread_out.at[:, 0, :], sems.at[1]))
     for copy in outgoing:
         copy.wait()
-    for col in range(CX * CY):
-        pltpu.make_async_copy(modes_ref.at[col], modes_out.at[col], sems.at[10 + col]).wait()
 
 
 def plane_kernel(plane_ref, in_ref, *refs):
@@ -270,18 +276,16 @@
         copy.wait()
 
 
-def force_kernel(in_ref, *refs):
-    sources, out_ref, held = refs[:3], refs[3], refs[4:7]
-    turned, packed, padded, rows_out, sems = refs[7:]
-    modes_ref, edges_ref, swap_ref = held
+def force_kernel(
+    in_ref, modes_ref, edges, swap_ref, out_ref, turned, packed, padded, rows_out, edges_ref, sems
+):
+    (kept,) = started((edges, edges_ref, sems.at[3]))
     incoming = started(
         *(
             (in_ref.at[:, 0, d * BLOCK : (d + 1) * BLOCK], turned.at[d], sems.at[d])
             for d in range(3)
         )
     )
-    kept = started(*((s, t, sems.at[3 + n]) for n, (s, t) in enumerate(zip(sources, held))))
-    kept[2].wait()
     for d in range(3):
         incoming[d].wait()
         value = turned[d].T
@@ -291,8 +295,7 @@
         for y in range(BY):
             padded[d, y, :BX, :] = packed[y * BX : (y + 1) * BX, :]
             padded[d, y, BX:, :] = jnp.zeros((40 - BX, LZ), F32)
-    kept[0].wait()
-    kept[1].wait()
+    kept.wait()
 
     def column(col, carry):
         y = (col % CY) * CELL
@@ -314,18 +317,16 @@
 
 
 COULOMB = (
-    -0.006157896808528851,
-    -0.00037761534771162467,
-    0.4246826287075061,
-    -0.032594054879277516,
-    0.5289809248435148,
-    -0.3643412334667553,
-    0.147196623703603,
-    -0.012411731315994238,
-    -0.015640759195296648,
-    0.00499632789350256,
+    -0.006156452396320011,
+    -0.0004198503476764426,
+    0.4251962050951751,
+    -0.035971568956237085,
+    0.5422242920959217,
+    -0.3965913855606964,
+    0.1962617265017834,
+    -0.05766279059061346,
+    0.007452967624700701,
 )
-SCALES = (0.125, 0.125, 0.125, 1.0, 1.0, 0.0625)
 
 
 def pair_term(own, other):
@@ -333,11 +334,11 @@
     dy = other[1] - own[1]
     dz = other[2] - own[2]
     r2 = dx * dx + dy * dy + dz * dz
-    fade = jnp.maximum(1.0 - r2, 0.0)
-    t = lax.rsqrt(r2 + 1.0 / CUT)
-    decay = jnp.exp2(r2 * (-0.49 * CUT * math.log2(math.e)))
-    scale = -16.0 * math.exp(-0.49)
-    terms = [scale * c * 0.125**n for n, c in enumerate(COULOMB)]
+    gap = FAR - r2
+    fade = jnp.maximum(gap, 0.0)
+    t = lax.rsqrt(r2 + LENGTH * LENGTH)
+    scale = -2.0 * math.exp(-GEWALD * GEWALD) * 2.0**-FAR / (FAR * LENGTH)
+    terms = [scale * c * LENGTH**n for n, c in enumerate(COULOMB)]
     poly = terms[-1] * t + terms[-2]
     for c in terms[-3::-1]:
         poly = poly * t + c
@@ -348,99 +349,153 @@
     x3 = x * x * x
     rest = 1.0 - (x3 + x3)
     lj = x3 * (rest * ((fade * inverse) * 3.0 + 1.0) + 1.0)
-    w = fade * ((own[4] * other[4]) * lj + (own[3] * other[3]) * (decay * poly))
+    w = fade * ((own[4] * other[4]) * lj + (own[3] * other[3]) * (jnp.exp2(gap) * poly))
     return w * dx, w * dy, w * dz
 
 
-def pair_kernel(*refs, shifts, unroll, begun):
-    wide_refs = refs[begun:-3]
-    out_ref, others, own = refs[-3:]
+def shifted_z(value, at_z, step):
+    if step == 0:
+        return value
+    if step > 0:
+        return jnp.where(
+            at_z == CZ - 1, pltpu.roll(value, CZ - 1, 1), pltpu.roll(value, CELLS - 1, 1)
+        )
+    return jnp.where(at_z == 0, pltpu.roll(value, CELLS - CZ + 1, 1), pltpu.roll(value, 1, 1))
+
+
+def pair_kernel(*refs, passes, single, sources, unroll):
+    blocks, outs = refs[:sources], refs[sources:-3]
+    others, own, back = refs[-3:]
     low = (lax.broadcasted_iota(jnp.int32, (SLOTS, 256), 1) & CZ) == 0
     at_z = lax.broadcasted_iota(jnp.int32, (SLOTS, CELLS), 1) & (CZ - 1)
+    empty = jnp.zeros((SLOTS, 64), F32)
     for c in range(6):
-        wides = []
-        for ref in wide_refs:
-            value = ref[c] * SCALES[c]
-            wides.append(jnp.concatenate([value, jnp.zeros((SLOTS, 64), F32)], axis=1))
-        own[c] = wides[0][:, 32:160]
-        layers = {0: wides[0]}
-        if len(wides) > 1:
-            above, below = wides[1:]
-            layers[1] = jnp.where(
-                low, pltpu.roll(wides[0], 256 - CZ, 1), pltpu.roll(above, CZ, 1)
+        wide = jnp.concatenate([blocks[1][c], blocks[0][c], blocks[2][c], empty], axis=1)
+        own[c] = blocks[0][c]
+        layers = {0: wide}
+        if sources > 3:
+            above = jnp.concatenate([blocks[4][c], blocks[3][c], blocks[5][c], empty], axis=1)
+            layers[1] = jnp.where(low, pltpu.roll(wide, 256 - CZ, 1), pltpu.roll(above, CZ, 1))
+        for n, offset in enumerate(passes):
+            at = COLUMNS * (offset[0] + 1)
+            value = layers[offset[1]][:, at : at + CELLS]
+            value = shifted_z(value, at_z, offset[2])
+            others[c, n * SLOTS : (n + 1) * SLOTS] = (
+                value + offset[c] * CELL * LENGTH if c < 3 else value
             )
-            layers[-1] = jnp.where(
-                low, pltpu.roll(below, 256 - CZ, 1), pltpu.roll(wides[0], CZ, 1)
-            )
-        for n, (a, b) in enumerate(shifts):
-            value = layers[b][:, 32 * (a + 1) : 32 * (a + 1) + CELLS]
-            if c == 0:
-                value = value + float(a)
-            if c == 1:
-                value = value + float(b)
-            up = jnp.where(
-                at_z == CZ - 1, pltpu.roll(value, CZ - 1, 1), pltpu.roll(value, CELLS - 1, 1)
-            )
-            down = jnp.where(at_z == 0, pltpu.roll(value, CELLS - CZ + 1, 1), pltpu.roll(value, 1, 1))
-            if c == 2:
-                up = up + 1.0
-                down = down - 1.0
-            for m, part in enumerate((down, value, up)):
-                row = (n * 3 + m) * SLOTS
-                others[c, row : row + SLOTS] = part
-
-    def step(n, sums):
+
+    def step(n, sums, reverse):
         sums = list(sums)
         for jj in range(unroll):
             j = n * unroll + jj
             other = [others[c, pl.ds(j, 8, stride=0), :] for c in range(6)]
+            total = [None] * 3
             for block in range(4):
                 mine = [own[c, 8 * block : 8 * block + 8, :] for c in range(6)]
                 force = pair_term(mine, other)
                 for d in range(3):
                     sums[block * 3 + d] = sums[block * 3 + d] + force[d]
+                    total[d] = force[d] if block == 0 else total[d] + force[d]
+            if reverse:
+                for d in range(3):
+                    back[d, pl.ds(pl.multiple_of((j - single * SLOTS) * 8, 8), 8), :] = total[d]
         return tuple(sums)
 
-    zero = jnp.zeros((8, CELLS), F32)
-    steps = len(shifts) * 3 * SLOTS // unroll
-    sums = lax.fori_loop(0, steps, step, (zero,) * 12)
+    per = SLOTS // unroll
+    sums = (jnp.zeros((8, CELLS), F32),) * 12
+    sums = lax.fori_loop(0, single * per, functools.partial(step, reverse=False), sums)
+    sums = lax.fori_loop(
+        single * per, len(passes) * per, functools.partial(step, reverse=True), sums
+    )
+    nothing = jnp.zeros((SLOTS, 128), F32)
     for d in range(3):
-        force = jnp.concatenate([sums[block * 3 + d] for block in range(4)], axis=0).T
-        out_ref[d] = refs[0][d] + force if begun else force
-
-
-def pair_forces(wides, shifts, start=(), unroll=4):
-    rows = len(shifts) * 3 * SLOTS
+        force = jnp.concatenate([sums[block * 3 + d] for block in range(4)], axis=0)
+        here = pltpu.roll(jnp.concatenate([force, nothing], axis=1), COLUMNS, 1)
+        there = jnp.zeros((SLOTS, 256), F32)
+        for n, offset in enumerate(passes):
+            if n < single:
+                continue
+            base = (n - single) * SLOTS * 8
+            value = back[d, pl.ds(base, SLOTS, stride=8), :]
+            for s in range(1, 8):
+                value = value + back[d, pl.ds(base + s, SLOTS, stride=8), :]
+            value = shifted_z(value, at_z, -offset[2])
+            value = jnp.concatenate([value, nothing], axis=1)
+            at = COLUMNS * (offset[0] + 1)
+            if offset[1]:
+                here = here - pltpu.roll(jnp.where(low, value, 0.0), at + CZ, 1)
+                there = there - pltpu.roll(jnp.where(low, 0.0, value), (at - CZ) % 256, 1)
+            else:
+                here = here - pltpu.roll(value, at, 1)
+        if len(outs) == 1:
+            outs[0][d] = here[:, COLUMNS : COLUMNS + CELLS]
+            continue
+        for at, total in ((0, here), (3, there)):
+            outs[at][d] = total[:, COLUMNS : COLUMNS + CELLS]
+            outs[at + 1][d] = total[:, :COLUMNS]
+            outs[at + 2][d] = total[:, COLUMNS + CELLS : 2 * COLUMNS + CELLS]
+
+
+def pair_forces(blocks, passes, single, unroll=4):
+    rows = len(passes) * SLOTS
     pairs = rows * SLOTS * CELLS
+    widths = (CELLS, COLUMNS, COLUMNS) * 2 if len(blocks) > 3 else (CELLS,)
     return pl.pallas_call(
-        functools.partial(pair_kernel, shifts=tuple(shifts), unroll=unroll, begun=len(start)),
-        out_shape=jax.ShapeDtypeStruct((3, CELLS, SLOTS), F32),
-        in_specs=[VMEM] * (len(start) + len(wides)),
-        out_specs=VMEM,
-        scratch_shapes=[pltpu.VMEM((6, rows + 8, CELLS), F32), pltpu.VMEM((6, SLOTS, CELLS), F32)],
+        functools.partial(
+            pair_kernel,
+            passes=tuple(passes),
+            single=single,
+            sources=len(blocks),
+            unroll=unroll,
+        ),
+        out_shape=[jax.ShapeDtypeStruct((3, SLOTS, width), F32) for width in widths],
+        in_specs=[VMEM] * len(blocks),
+        out_specs=[VMEM] * len(widths),
+        scratch_shapes=[
+            pltpu.VMEM((6, rows + 8, CELLS), F32),
+            pltpu.VMEM((6, SLOTS, CELLS), F32),
+            pltpu.VMEM((3, (rows - single * SLOTS) * 8, CELLS), F32),
+        ],
         compiler_params=params(8),
         cost_estimate=pl.CostEstimate(flops=70 * pairs, bytes_accessed=1 << 20, transcendentals=0),
-    )(*start, *wides)
-
-
-def ring(axis, step):
-    count = lax.axis_size(axis)
-    return [(i, (i + step) % count) for i in range(count)]
+    )(*blocks)
+
+
+def join_kernel(near_ref, here_ref, down_ref, first_a, first_b, last_a, last_b, out_ref):
+    middle = jnp.zeros((SLOTS, CELLS - 2 * COLUMNS), F32)
+    for d in range(3):
+        sides = [first_a[d] + first_b[d], middle, last_a[d] + last_b[d]]
+        out_ref[d] = (near_ref[d] + here_ref[d] + down_ref[d] + jnp.concatenate(sides, axis=1)).T
+
+
+def hbm(array):
+    return pltpu.with_memory_space_constraint(jnp.asarray(array), pltpu.HBM)
+
+
+def send(value, step_x, step_y):
+    route = [
+        (x * DY + y, (x + step_x) % DX * DY + (y + step_y) % DY)
+        for x in range(DX)
+        for y in range(DY)
+    ]
+    return lax.ppermute(value, ("gx", "gy"), route)
 
 
 def body(positions, charges, types, counts, eps_type, sig_type):
     tab = tables()
     slot_last = lambda a: jnp.moveaxis(a, -4, -1).reshape(a.shape[:-4] + (CELLS, SLOTS))
-    atoms, spread, modes, edges = pl.pallas_call(
-        spread_kernel,
+    side = jax.ShapeDtypeStruct((6, SLOTS, COLUMNS), F32)
+    atoms, first, last, rows, tz = pl.pallas_call(
+        table_kernel,
         out_shape=(
             jax.ShapeDtypeStruct((6, SLOTS, CELLS), F32),
-            jax.ShapeDtypeStruct((LZ, 1, BLOCK), F32),
-            jax.ShapeDtypeStruct((CX * CY, 3 * LZ, 512), BF16),
-            jax.ShapeDtypeStruct((CX * CY, 32, 512), F32),
+            side,
+            side,
+            jax.ShapeDtypeStruct((4, GROUPS, 128), F32),
+            jax.ShapeDtypeStruct(tab["tz"].shape, BF16),
         ),
         in_specs=[ANY] * 7,
-        out_specs=(ANY,) * 4,
+        out_specs=(VMEM,) * 5,
         scratch_shapes=[
             pltpu.VMEM((3, CELLS, SLOTS), F32),
             pltpu.VMEM((CELLS, SLOTS), F32),
@@ -448,38 +503,65 @@
             pltpu.VMEM((CX, CY, CZ), jnp.int32),
             pltpu.SMEM(eps_type.shape, F32),
             pltpu.SMEM(sig_type.shape, F32),
-            pltpu.VMEM(tab["tz"].shape, BF16),
-            pltpu.VMEM((6, SLOTS, CELLS), F32),
-            pltpu.VMEM((4, GROUPS, 128), F32),
-            pltpu.VMEM((CX * CY, 3 * LZ, 512), BF16),
-            pltpu.VMEM((CX * CY, 32, 512), F32),
+            pltpu.SemaphoreType.DMA((7,)),
+        ],
+        compiler_params=params(8),
+    )(
+        hbm(slot_last(positions)),
+        hbm(slot_last(charges)),
+        hbm(slot_last(types)),
+        hbm(counts),
+        hbm(eps_type),
+        hbm(sig_type),
+        hbm(tab["tz"]),
+    )
+    after = send(first, -1, 0)
+    before = send(last, 1, 0)
+    above = send(atoms, 0, -1)
+    above_after = send(first, -1, -1)
+    above_before = send(last, 1, -1)
+
+    spread, modes, edges = pl.pallas_call(
+        spread_kernel,
+        out_shape=(
+            jax.ShapeDtypeStruct((LZ, 1, BLOCK), F32),
+            jax.ShapeDtypeStruct((CX * CY, 3 * LZ, 512), BF16),
+            jax.ShapeDtypeStruct((CX * CY, 32, 512), F32),
+        ),
+        in_specs=[VMEM] * 2,
+        out_specs=(ANY, VMEM, ANY),
+        scratch_shapes=[
             pltpu.VMEM((BY, 40, LZ), F32),
             pltpu.VMEM((BLOCK, LZ), F32),
             pltpu.VMEM((LZ, BLOCK), F32),
-            pltpu.SemaphoreType.DMA((10 + CX * CY,)),
+            pltpu.VMEM((CX * CY, 32, 512), F32),
+            pltpu.SemaphoreType.DMA((2,)),
         ],
-        compiler_params=params(56),
-    )(
-        slot_last(positions),
-        slot_last(charges),
-        slot_last(types),
-        counts,
-        eps_type,
-        sig_type,
-        tab["tz"],
-    )
-    before = lax.ppermute(atoms[:, :, CELLS - 32 :], "gx", ring("gx", 1))
-    after = lax.ppermute(atoms[:, :, :32], "gx", ring("gx", -1))
-    lines = lax.all_to_all(spread, ("gx", "gy"), split_axis=0, concat_axis=0, tiled=True)
-
-    wide = jnp.concatenate([before, atoms, after], axis=2)
-    below = lax.ppermute(wide, "gy", ring("gy", 1))
-    above = lax.ppermute(wide, "gy", ring("gy", -1))
-    near = pair_forces((wide,), [(a, 0) for a in (-1, 0, 1)])
-    lines, near, below, above = lax.optimization_barrier((lines, near, below, above))
+        compiler_params=params(16),
+    )(rows, tz)
+    spread, after, before, above, above_after, above_before = lax.optimization_barrier(
+        (spread, after, before, above, above_after, above_before)
+    )
+    lines = lax.all_to_all(hbm(spread), ("gx", "gy"), split_axis=0, concat_axis=0, tiled=True)
+    here, to_before, to_after, up, up_before, up_after = pair_forces(
+        (atoms, before, after, above, above_before, above_after),
+        [(a, 1, c) for a in (-1, 0, 1) for c in (-1, 0, 1)],
+        0,
+    )
+    lines, here, to_before, to_after, up, up_before, up_after = lax.optimization_barrier(
+        (lines, here, to_before, to_after, up, up_before, up_after)
+    )
+    sides = (
+        send(up, 0, 1),
+        send(to_after, 1, 0),
+        send(up_after, 1, 1),
+        send(to_before, -1, 0),
+        send(up_before, -1, 1),
+    )
 
     index = lax.axis_index("gx") * DY + lax.axis_index("gy")
     plane = lax.dynamic_index_in_dim(jnp.asarray(tab["plane"]), index, 0, keepdims=False)
+    constants = [hbm(tab[name]) for name in ("tx", "ty", "iy", "ix", "kx2", "ky2")]
     fields = pl.pallas_call(
         plane_kernel,
         out_shape=jax.ShapeDtypeStruct((DX * DY, 1, 3 * BLOCK), F32),
@@ -493,34 +575,37 @@
             pltpu.VMEM((3, DX * DY, BLOCK), F32),
             pltpu.SemaphoreType.DMA((10,)),
         ],
-        compiler_params=params(56),
-    )(plane, lines, tab["tx"], tab["ty"], tab["iy"], tab["ix"], tab["kx2"], tab["ky2"])
-    fields = lax.all_to_all(fields, ("gx", "gy"), split_axis=0, concat_axis=0, tiled=True)
-    far = pair_forces(
-        (wide, above, below), [(a, b) for b in (-1, 1) for a in (-1, 0, 1)], (near,)
-    )
-    fields, far = lax.optimization_barrier((fields, far))
+        compiler_params=params(20),
+    )(plane, lines, *constants)
+    fields = lax.all_to_all(hbm(fields), ("gx", "gy"), split_axis=0, concat_axis=0, tiled=True)
+    beside = [(a, 0, c) for a in (-1, 1) for c in (-1, 0, 1)]
+    (near,) = pair_forces((atoms, before, after), [(0, 0, 0), *beside, (0, 0, 1)], 7)
+    pair_force = pl.pallas_call(
+        join_kernel,
+        out_shape=jax.ShapeDtypeStruct((3, CELLS, SLOTS), F32),
+        in_specs=[VMEM] * 7,
+        out_specs=VMEM,
+        compiler_params=params(4),
+    )(near, here, *sides)
+    fields, pair_force = lax.optimization_barrier((fields, pair_force))
 
     mesh_force = pl.pallas_call(
         force_kernel,
         out_shape=jax.ShapeDtypeStruct((3, CELLS, SLOTS), F32),
-        in_specs=[ANY] * 4,
+        in_specs=[ANY, VMEM, ANY, VMEM],
         out_specs=VMEM,
         scratch_shapes=[
-            pltpu.VMEM((CX * CY, 3 * LZ, 512), BF16),
-            pltpu.VMEM((CX * CY, 32, 512), F32),
-            pltpu.VMEM((1, LZ), F32),
             pltpu.VMEM((3, LZ, BLOCK), F32),
             pltpu.VMEM((BLOCK, LZ), F32),
             pltpu.VMEM((3, BY, 40, LZ), F32),
             pltpu.VMEM((3, GROUPS, 128), F32),
-            pltpu.SemaphoreType.DMA((6,)),
+            pltpu.VMEM((CX * CY, 32, 512), F32),
+            pltpu.SemaphoreType.DMA((4,)),
         ],
-        compiler_params=params(56),
-    )(fields, modes, edges, tab["swap"])
-
+        compiler_params=params(20),
+    )(fields, modes, hbm(edges), tab["swap"])
     slot_first = lambda a: jnp.moveaxis(a.reshape(3, CX, CY, CZ, SLOTS), -1, 1)
-    return slot_first(far), slot_first(mesh_force)
+    return slot_first(pair_force), slot_first(mesh_force)
 
 
 def solution(mesh):

time: 93 us -> 93.3 us (level)
  Pallas kernels: 56.2 us -> 44 us
  starting transfers between devices: 27 us -> 35.9 us
  local copies, waits for them, and re-layouts: 4.03 us -> 8.26 us
    pallas_call x3 -> x5, Pallas kernels: 42.2 us -> 31.1 us  [the longest x2 24.1 us: pair_forces(): pl.pallas_call(functools.partial(pair_kernel, passes=tuple(passes), singl...]
    ppermute x4 -> x10, starting transfers between devices: 7.1 us -> 17.2 us  [send(): return lax.ppermute(value, ('gx', 'gy'), route)]
    unnamed x6 -> x28, local copies, waits for them, and re-layouts: 1.78 us -> 7.56 us
    all_to_all x2, starting transfers between devices: 19.9 us -> 18.6 us  [the longest x1 10.2 us: body(): lax.all_to_all(hbm(fields), ('gx', 'gy'), split_axis=0, concat_axis=0, ti...]
    slice x1 -> x0, local copies, waits for them, and re-layouts: 1.05 us -> none  [body(): before = lax.ppermute(atoms[:, :, CELLS - 32:], 'gx', ring('gx', 1))]
    pallas_call x1, Pallas kernels: 7.23 us -> 6.21 us  [body(): pl.pallas_call(force_kernel, out_shape=jax.ShapeDtypeStruct((3, CELLS, SL...]
    ppermute x4 -> x10, waiting for transfers between devices: 4.53 us -> 3.9 us  [send(): return lax.ppermute(value, ('gx', 'gy'), route)]
  transfers between devices with their start and end apart: 6 -> 12, of which waited for: 2 -> 1; matrix products, arithmetic and copies ran while one was open for 3% -> 1% of each run, Pallas kernels for 39% -> 32%
where the time goes in v3:
time: 93.3 us; the launch traced here: 92.9 us
  Pallas kernels  44 us (47%)
  starting transfers between devices  35.9 us (38%)
  local copies, waits for them, and re-layouts  8.26 us (9%)
  waiting for transfers between devices  3.91 us (4%)
  between operations  0.95 us (1%)
    pallas_call x2, Pallas kernels, pair_forces(): pl.pallas_call(functools.partial(pair_kernel, passes=tuple(passes), singl...  24.1 us
    ppermute x10, starting transfers between devices, send(): return lax.ppermute(value, ('gx', 'gy'), route)  17.2 us
    all_to_all x1, starting transfers between devices, body(): lax.all_to_all(hbm(fields), ('gx', 'gy'), split_axis=0, concat_axis=0, ti...  10.2 us
    all_to_all x1, starting transfers between devices, body(): lax.all_to_all(hbm(spread), ('gx', 'gy'), split_axis=0, concat_axis=0, ti...  8.48 us
    unnamed x28, local copies, waits for them, and re-layouts  7.56 us
    pallas_call x1, Pallas kernels, body(): pl.pallas_call(plane_kernel, out_shape=jax.ShapeDtypeStruct((DX * DY, 1,...  6.67 us
    pallas_call x1, Pallas kernels, body(): pl.pallas_call(force_kernel, out_shape=jax.ShapeDtypeStruct((3, CELLS, SL...  6.21 us
    pallas_call x1, Pallas kernels, body(): pl.pallas_call(spread_kernel, out_shape=(jax.ShapeDtypeStruct((LZ, 1, BLO...  4.53 us
  transfers between devices with their start and end apart: 12, of which 1 were waited for; matrix products, arithmetic and copies ran while one was open for 1% of the time, Pallas kernels for 32%

profile of v3, /device:TPU:1, one launch (start us, length us, event | category | flops | bytes accessed | tf_op | source)
XLA Modules:
  0.0 92.9 jit_solution(7640556680948771079)
XLA Ops:
  0.6 1.6 %shard_map.158 = (f32[6,32,128]{2,1,0:T(8,128)S(1)}, f32[6,32,32]{2,1,0:T(8,128)S(1)}, f32[6,32,32]{2,1,0:T(8,128)S(1)}, f32[4,32,128]{2,1,0:T(8,128)S(1)}, bf16[4,128,144]{2,1,0:T(8,128)(2,1)S(1)}) custom-call(f32[3,128,32]{2,1,0:T(8,128)} %bitcast.18, f32[128,32]{1,0:T(8,128)} %bitcast.20, s32[128,32]{1,0:T(8,128)} %bitcast.21, s32[4,2,16]{2,1,0:T(2,128)} %refs_3_.2, ...), custom_call_target="tpu_custom_call" | custom-call | tf_op jit(solution)/shard_map/pallas_call | solution.py:488
  2.3 7.1 %collective-permute-start.2 = (f32[6,32,128]{2,1,0:T(8,128)S(1)}, f32[6,32,128]{2,1,0:T(8,128)S(1)}, u32[]{:S(2)}, u32[]{:S(2)}) collective-permute-start(f32[6,32,128]{2,1,0:T(8,128)S(1)} %get-tuple-element.36.refs_0_), channel_id=1, source_target_pairs={{0,15},{1,0},{2,1},{3,2},{4,3},{5,4},{6,5},{7,6},{8,7},{9,8},{10,9... | collective-permute-start | bytes 294920 | tf_op jit(solution)/shard_map/ppermute | solution.py:481
  9.4 1.0 %collective-permute-start.3 = (f32[6,32,32]{2,1,0:T(8,128)S(1)}, f32[6,32,32]{2,1,0:T(8,128)S(1)}, u32[]{:S(2)}, u32[]{:S(2)}) collective-permute-start(f32[6,32,32]{2,1,0:T(8,128)S(1)} %get-tuple-element.34), channel_id=1, source_target_pairs={{0,127},{1,112},{2,113},{3,114},{4,115},{5,116},{6,117},{7,118},{8... | collective-permute-start | bytes 73736 | tf_op jit(solution)/shard_map/ppermute | solution.py:481
  10.3 1.7 %collective-permute-start = (f32[6,32,32]{2,1,0:T(8,128)S(1)}, f32[6,32,32]{2,1,0:T(8,128)S(1)}, u32[]{:S(2)}, u32[]{:S(2)}) collective-permute-start(f32[6,32,32]{2,1,0:T(8,128)S(1)} %get-tuple-element.34), channel_id=1, source_target_pairs={{0,112},{1,113},{2,114},{3,115},{4,116},{5,117},{6,118},{7,119},{8... | collective-permute-start | bytes 73736 | tf_op jit(solution)/shard_map/ppermute | solution.py:481
  12.1 4.5 %shard_map.159 = (f32[128,1,768]{2,1,0:T(1,128)}, bf16[8,384,512]{2,1,0:T(8,128)(2,1)S(1)}, f32[8,32,512]{2,1,0:T(8,128)S(1)}) custom-call(f32[4,32,128]{2,1,0:T(8,128)S(1)} %get-tuple-element.31.rows_ref, bf16[4,128,144]{2,1,0:T(8,128)(2,1)S(1)} %get-tuple-element.32.tz_ref), custom_call_target="tpu_custom_call" | custom-call | tf_op jit(solution)/shard_map/pallas_call | solution.py:524
  16.6 0.8 copy-done
  17.4 0.6 copy-done.1
  18.1 0.6 copy-done.3
  18.7 8.5 %all-to-all-start = ((f32[128,1,768]{2,1,0:T(1,128)}), f32[128,1,768]{2,1,0:T(1,128)}, u32[]{:S(2)}, u32[]{:S(2)}) async-start(f32[128,1,768]{2,1,0:T(1,128)} %get-tuple-element.37), calls=%async_computation | async-start | bytes 786432 | tf_op jit(solution)/shard_map/all_to_all | solution.py:545
  27.2 0.7 dynamic-slice_bitcast_fusion.plane_ref
  27.9 0.9 copy-done.2
  28.8 0.9 copy-done.4
  29.7 13.7 %shard_map.160 = (f32[3,32,128]{2,1,0:T(8,128)S(1)}, f32[3,32,32]{2,1,0:T(8,128)S(1)}, f32[3,32,32]{2,1,0:T(8,128)S(1)}, f32[3,32,128]{2,1,0:T(8,128)S(1)}, f32[...) custom-call(f32[6,32,128]{2,1,0:T(8,128)S(1)} %get-tuple-element.36.refs_0_, ...), custom_call_target="tpu_custom_call" | custom-call | flops 82575360 | bytes 1048576 | tf_op jit(solution)/shard_map/pallas_call | solution.py:443
  47.2 6.7 %shard_map.161 = f32[128,1,2304]{2,1,0:T(1,128)} custom-call(f32[2]{0:T(128)S(1)} %dynamic-slice_bitcast_fusion.plane_ref, f32[128,1,768]{2,1,0:T(1,128)} %all-to-all-done.in_ref, bf16[1536,256]{1,0:T(8,128)(2,1)} %constant.37.clone.refs_0_, bf16[256,960]{1,0:T(8,128)(2,1)} %constant.38.clone.refs_1_, bf16[640,768]{1,0:T(8,128)(2,1)} %constant.39.clone.refs_2_, ...), custom_call_target="tpu_custom_call" | custom-call | tf_op jit(solution)/shard_map/pallas_call | solution.py:565
  53.9 10.2 %all-to-all-start.1 = ((f32[128,1,2304]{2,1,0:T(1,128)}), f32[128,1,2304]{2,1,0:T(1,128)}, u32[]{:S(2)}, u32[]{:S(2)}) async-start(f32[128,1,2304]{2,1,0:T(1,128)} %shard_map.161), calls=%async_computation.1 | async-start | bytes 2359296 | tf_op jit(solution)/shard_map/all_to_all | solution.py:580
  64.1 1.6 %collective-permute-start.5 = (f32[3,32,128]{2,1,0:T(8,128)S(1)}, f32[3,32,128]{2,1,0:T(8,128)S(1)}, u32[]{:S(2)}, u32[]{:S(2)}) collective-permute-start(f32[3,32,128]{2,1,0:T(8,128)S(1)} %copy-done.9), channel_id=1, source_target_pairs={{0,1},{1,2},{2,3},{3,4},{4,5},{5,6},{6,7},{7,8},{8,9},{9,10},{10,1... | collective-permute-start | bytes 147464 | tf_op jit(solution)/shard_map/ppermute | solution.py:481
  65.6 1.7 %collective-permute-start.6 = (f32[3,32,32]{2,1,0:T(8,128)}, f32[3,32,32]{2,1,0:T(8,128)S(1)}, u32[]{:S(2)}, u32[]{:S(2)}) collective-permute-start(f32[3,32,32]{2,1,0:T(8,128)} %copy-done.13), channel_id=1, source_target_pairs={{0,16},{1,17},{2,18},{3,19},{4,20},{5,21},{6,22},{7,23},{8,24},{9,... | collective-permute-start | bytes 36872 | tf_op jit(solution)/shard_map/ppermute | solution.py:481
  67.4 1.2 %collective-permute-start.7 = (f32[3,32,32]{2,1,0:T(8,128)}, f32[3,32,32]{2,1,0:T(8,128)S(1)}, u32[]{:S(2)}, u32[]{:S(2)}) collective-permute-start(f32[3,32,32]{2,1,0:T(8,128)} %copy-done.12), channel_id=1, source_target_pairs={{0,17},{1,18},{2,19},{3,20},{4,21},{5,22},{6,23},{7,24},{8,25},{9,... | collective-permute-start | bytes 36872 | tf_op jit(solution)/shard_map/ppermute | solution.py:481
  68.5 0.7 collective-permute-start.8
  69.2 2.2 %collective-permute-start.9 = (f32[3,32,32]{2,1,0:T(8,128)}, f32[3,32,32]{2,1,0:T(8,128)S(1)}, u32[]{:S(2)}, u32[]{:S(2)}) collective-permute-start(f32[3,32,32]{2,1,0:T(8,128)} %copy-done.10), channel_id=1, source_target_pairs={{0,113},{1,114},{2,115},{3,116},{4,117},{5,118},{6,119},{7,120},{8... | collective-permute-start | bytes 36872 | tf_op jit(solution)/shard_map/ppermute | solution.py:481
  71.4 10.3 %shard_map.162.near_ref = f32[3,32,128]{2,1,0:T(8,128)S(1)} custom-call(f32[6,32,128]{2,1,0:T(8,128)S(1)} %get-tuple-element.36.refs_0_, f32[6,32,32]{2,1,0:T(8,128)S(1)} %collective-permute-done.1.refs_1_, f32[6,32,32]{2,1,0:T(8,128)S(1)} %collective-permute-done.refs_2_), custom_call_target="tpu_custom_call" | custom-call | flops 73400320 | bytes 1048576 | tf_op jit(solution)/shard_map/pallas_call | solution.py:443
  81.8 3.9 %collective-permute-done.7.first_b = f32[3,32,32]{2,1,0:T(8,128)S(1)} collective-permute-done((f32[3,32,32]{2,1,0:T(8,128)}, f32[3,32,32]{2,1,0:T(8,128)S(1)}, u32[]{:S(2)}, u32[]{:S(2)}) %collective-permute-start.7) | collective-permute-done | bytes 12320 | tf_op jit(solution)/shard_map/ppermute | solution.py:481
  85.7 0.9 shard_map.163
  86.6 6.2 %shard_map.164 = f32[3,128,32]{2,1,0:T(8,128)} custom-call(f32[128,1,2304]{2,1,0:T(1,128)} %all-to-all-done.1.in_ref, bf16[8,384,512]{2,1,0:T(8,128)(2,1)S(1)} %get-tuple-element.58.modes_ref, f32[8,32,512]{2,1,0:T(8,128)} %copy-done, f32[1,128]{1,0:T(1,128)S(1)} %copy-done.7), custom_call_target="tpu_custom_call" | custom-call | tf_op jit(solution)/shard_map/pallas_call | solution.py:592
  (36 shorter events, 3.7 us)
Async XLA Ops:
  2.3 16.5 %collective-permute-start.2 = (f32[6,32,128]{2,1,0:T(8,128)S(1)}, f32[6,32,128]{2,1,0:T(8,128)S(1)}, u32[]{:S(2)}, u32[]{:S(2)}) collective-permute-start(f32[6,32,128]{2,1,0:T(8,128)S(1)} %get-tuple-element.36.refs_0_), channel_id=1, source_target_pairs={{0,15},{1,0},{2,1},{3,2},{4,3},{5,4},{6,5},{7,6},{8,7},{9,8},{10,9... | collective-permute-start | bytes 294920 | tf_op jit(solution)/shard_map/ppermute | solution.py:481
  9.4 8.1 %collective-permute-start.3 = (f32[6,32,32]{2,1,0:T(8,128)S(1)}, f32[6,32,32]{2,1,0:T(8,128)S(1)}, u32[]{:S(2)}, u32[]{:S(2)}) collective-permute-start(f32[6,32,32]{2,1,0:T(8,128)S(1)} %get-tuple-element.34), channel_id=1, source_target_pairs={{0,127},{1,112},{2,113},{3,114},{4,115},{5,116},{6,117},{7,118},{8... | collective-permute-start | bytes 73736 | tf_op jit(solution)/shard_map/ppermute | solution.py:481
  10.3 7.7 %collective-permute-start = (f32[6,32,32]{2,1,0:T(8,128)S(1)}, f32[6,32,32]{2,1,0:T(8,128)S(1)}, u32[]{:S(2)}, u32[]{:S(2)}) collective-permute-start(f32[6,32,32]{2,1,0:T(8,128)S(1)} %get-tuple-element.34), channel_id=1, source_target_pairs={{0,112},{1,113},{2,114},{3,115},{4,116},{5,117},{6,118},{7,119},{8... | collective-permute-start | bytes 73736 | tf_op jit(solution)/shard_map/ppermute | solution.py:481
  12.1 6.0 %collective-permute-start.4 = (f32[6,32,32]{2,1,0:T(8,128)S(1)}, f32[6,32,32]{2,1,0:T(8,128)S(1)}, u32[]{:S(2)}, u32[]{:S(2)}) collective-permute-start(f32[6,32,32]{2,1,0:T(8,128)S(1)} %get-tuple-element.35), channel_id=1, source_target_pairs={{0,31},{1,16},{2,17},{3,18},{4,19},{5,20},{6,21},{7,22},{8,23},{9,... | collective-permute-start | bytes 73736 | tf_op jit(solution)/shard_map/ppermute | solution.py:481
  12.1 6.6 %collective-permute-start.1 = (f32[6,32,32]{2,1,0:T(8,128)S(1)}, f32[6,32,32]{2,1,0:T(8,128)S(1)}, u32[]{:S(2)}, u32[]{:S(2)}) collective-permute-start(f32[6,32,32]{2,1,0:T(8,128)S(1)} %get-tuple-element.35), channel_id=1, source_target_pairs={{0,16},{1,17},{2,18},{3,19},{4,20},{5,21},{6,22},{7,23},{8,24},{9,... | collective-permute-start | bytes 73736 | tf_op jit(solution)/shard_map/ppermute | solution.py:481
  16.6 0.8 copy-start
  17.4 0.6 copy-start.1
  18.1 0.6 copy-start.3
  18.7 28.4 %all-to-all-start = ((f32[128,1,768]{2,1,0:T(1,128)}), f32[128,1,768]{2,1,0:T(1,128)}, u32[]{:S(2)}, u32[]{:S(2)}) async-start(f32[128,1,768]{2,1,0:T(1,128)} %get-tuple-element.37), calls=%async_computation | async-start | bytes 786432 | tf_op jit(solution)/shard_map/all_to_all | solution.py:545
  27.9 0.9 copy-start.2
  28.8 0.9 copy-start.4
  43.5 0.6 copy-start.5
  44.1 0.6 copy-start.8
  45.3 0.6 copy-start.11
  45.9 0.6 copy-start.12
  53.8 10.2 %copy-start.9 = (f32[3,32,128]{2,1,0:T(8,128)S(1)}, f32[3,32,128]{2,1,0:T(8,128)}, u32[]{:S(2)}) copy-start(f32[3,32,128]{2,1,0:T(8,128)} %copy-done.8) | copy-start | bytes 147460
  53.8 31.8 %copy-start.6 = (f32[3,32,128]{2,1,0:T(8,128)S(1)}, f32[3,32,128]{2,1,0:T(8,128)}, u32[]{:S(2)}) copy-start(f32[3,32,128]{2,1,0:T(8,128)} %copy-done.5) | copy-start | bytes 147460
  53.9 32.7 %copy-start.7 = (f32[1,128]{1,0:T(1,128)S(1)}, f32[1,128]{1,0:T(1,128)}, u32[]{:S(2)}) copy-start(f32[1,128]{1,0:T(1,128)} %constant.43.clone.swap_ref) | copy-start | bytes 1540
  53.9 32.7 %all-to-all-start.1 = ((f32[128,1,2304]{2,1,0:T(1,128)}), f32[128,1,2304]{2,1,0:T(1,128)}, u32[]{:S(2)}, u32[]{:S(2)}) async-start(f32[128,1,2304]{2,1,0:T(1,128)} %shard_map.161), calls=%async_computation.1 | async-start | bytes 2359296 | tf_op jit(solution)/shard_map/all_to_all | solution.py:580
  64.1 21.6 %collective-permute-start.5 = (f32[3,32,128]{2,1,0:T(8,128)S(1)}, f32[3,32,128]{2,1,0:T(8,128)S(1)}, u32[]{:S(2)}, u32[]{:S(2)}) collective-permute-start(f32[3,32,128]{2,1,0:T(8,128)S(1)} %copy-done.9), channel_id=1, source_target_pairs={{0,1},{1,2},{2,3},{3,4},{4,5},{5,6},{6,7},{7,8},{8,9},{9,10},{10,1... | collective-permute-start | bytes 147464 | tf_op jit(solution)/shard_map/ppermute | solution.py:481
  65.6 16.1 %collective-permute-start.6 = (f32[3,32,32]{2,1,0:T(8,128)}, f32[3,32,32]{2,1,0:T(8,128)S(1)}, u32[]{:S(2)}, u32[]{:S(2)}) collective-permute-start(f32[3,32,32]{2,1,0:T(8,128)} %copy-done.13), channel_id=1, source_target_pairs={{0,16},{1,17},{2,18},{3,19},{4,20},{5,21},{6,22},{7,23},{8,24},{9,... | collective-permute-start | bytes 36872 | tf_op jit(solution)/shard_map/ppermute | solution.py:481
  67.4 18.3 %collective-permute-start.7 = (f32[3,32,32]{2,1,0:T(8,128)}, f32[3,32,32]{2,1,0:T(8,128)S(1)}, u32[]{:S(2)}, u32[]{:S(2)}) collective-permute-start(f32[3,32,32]{2,1,0:T(8,128)} %copy-done.12), channel_id=1, source_target_pairs={{0,17},{1,18},{2,19},{3,20},{4,21},{5,22},{6,23},{7,24},{8,25},{9,... | collective-permute-start | bytes 36872 | tf_op jit(solution)/shard_map/ppermute | solution.py:481
  68.5 17.1 %collective-permute-start.8 = (f32[3,32,32]{2,1,0:T(8,128)}, f32[3,32,32]{2,1,0:T(8,128)S(1)}, u32[]{:S(2)}, u32[]{:S(2)}) collective-permute-start(f32[3,32,32]{2,1,0:T(8,128)} %copy-done.11), channel_id=1, source_target_pairs={{0,112},{1,113},{2,114},{3,115},{4,116},{5,117},{6,118},{7,119},{8... | collective-permute-start | bytes 36872 | tf_op jit(solution)/shard_map/ppermute | solution.py:481
  69.2 16.4 %collective-permute-start.9 = (f32[3,32,32]{2,1,0:T(8,128)}, f32[3,32,32]{2,1,0:T(8,128)S(1)}, u32[]{:S(2)}, u32[]{:S(2)}) collective-permute-start(f32[3,32,32]{2,1,0:T(8,128)} %copy-done.10), channel_id=1, source_target_pairs={{0,113},{1,114},{2,115},{3,116},{4,117},{5,118},{6,119},{7,120},{8... | collective-permute-start | bytes 36872 | tf_op jit(solution)/shard_map/ppermute | solution.py:481
  (2 other events, 1.2 us)

commit v4 on v3

--- a/solution.py
+++ b/solution.py
@@ -208,41 +208,46 @@
     incoming[-1].wait()
 
 
-def spread_kernel(
-    rows_ref, tz_ref, spread_out, modes_ref, edges_out, total, packed, turned, edges_ref, sems
-):
+def spread_kernel(rows_ref, tz_ref, spread_out, total, packed, turned, sems):
     total[...] = jnp.zeros_like(total)
 
     def column(col, carry):
         modes, edges = weights(rows_ref, tz_ref, col)
-        edges_ref[col] = edges
-        high, low = halves(modes)
-        modes_ref[col] = jnp.concatenate([high, low, high], axis=0)
-        modes = jnp.concatenate([high, low, high], axis=1)
-        part = dot(left_split(products(edges)), modes, ((1,), (1,))).reshape(12, 16, LZ)
+        part = dot(left_split(products(edges)), right_split(modes, 1), ((1,), (1,)))
         y = (col % CY) * CELL
         x = pl.multiple_of((col // CY) * CELL, CELL)
-        total[pl.ds(y, 12), pl.ds(x, 16), :] += part
+        total[pl.ds(y, 12), pl.ds(x, 16), :] += part.reshape(12, 16, LZ)
         return carry
 
     lax.fori_loop(0, CX * CY, column, 0, unroll=2)
-    outgoing = started((edges_ref, edges_out, sems.at[0]))
     for y in range(BY):
         packed[y * BX : (y + 1) * BX, :] = total[y, :BX, :]
     packed[BX * BY :, :] = jnp.zeros((BLOCK - BX * BY, LZ), F32)
     turned[...] = packed[...].T
-    outgoing += started((turned, spread_out.at[:, 0, :], sems.at[1]))
+    outgoing = started(
+        *(
+            (turned.at[gx * DY : (gx + 1) * DY, :], spread_out.at[:, gx, :], sems.at[gx])
+            for gx in range(DX)
+        )
+    )
     for copy in outgoing:
         copy.wait()
 
 
-def plane_kernel(plane_ref, in_ref, *refs):
+def weight_kernel(rows_ref, tz_ref, modes_ref, edges_ref):
+    def column(col, carry):
+        modes, edges_ref[col] = weights(rows_ref, tz_ref, col)
+        modes_ref[col] = jnp.concatenate(halves(modes), axis=0)
+        return carry
+
+    lax.fori_loop(0, CX * CY, column, 0, unroll=2)
+
+
+def plane_kernel(plane_ref, lines, *refs):
     sources, out_ref, held = refs[:6], refs[6], refs[7:13]
-    lines, stacked, turned, sems = refs[13:]
+    stacked, turned, sems = refs[13:]
     tx, ty, iy, ix, kx2, ky2 = held
-    (arrival,) = started((in_ref.at[:, 0, :], lines, sems.at[3]))
     constants = started(*((s, t, sems.at[4 + n]) for n, (s, t) in enumerate(zip(sources, held))))
-    arrival.wait()
     for y in range(BY):
         value = lines[:, y * BX : y * BX + KX]
         for gx in range(DX):
@@ -277,9 +282,8 @@
 
 
 def force_kernel(
-    in_ref, modes_ref, edges, swap_ref, out_ref, turned, packed, padded, rows_out, edges_ref, sems
+    in_ref, modes_ref, edges_ref, swap_ref, out_ref, turned, packed, padded, rows_out, sems
 ):
-    (kept,) = started((edges, edges_ref, sems.at[3]))
     incoming = started(
         *(
             (in_ref.at[:, 0, d * BLOCK : (d + 1) * BLOCK], turned.at[d], sems.at[d])
@@ -295,15 +299,16 @@
         for y in range(BY):
             padded[d, y, :BX, :] = packed[y * BX : (y + 1) * BX, :]
             padded[d, y, BX:, :] = jnp.zeros((40 - BX, LZ), F32)
-    kept.wait()
 
     def column(col, carry):
         y = (col % CY) * CELL
         x = pl.multiple_of((col // CY) * CELL, CELL)
         planes = products(edges_ref[col])
+        modes = modes_ref[col]
+        modes = jnp.concatenate([modes, modes[:LZ]], axis=0)
         for d in range(3):
             block = padded[d, pl.ds(y, 12), pl.ds(x, 16), :].reshape(192, LZ)
-            along = dot(left_split(block), modes_ref[col])
+            along = dot(left_split(block), modes)
             force = jnp.sum(along * planes, axis=0, keepdims=True)
             for zg in range(4):
                 rows_out[d, pl.ds(col * 4 + zg, 1), :] = force[:, 128 * zg : 128 * (zg + 1)]
@@ -363,8 +368,8 @@
     return jnp.where(at_z == 0, pltpu.roll(value, CELLS - CZ + 1, 1), pltpu.roll(value, 1, 1))
 
 
-def pair_kernel(*refs, passes, single, sources, unroll):
-    blocks, outs = refs[:sources], refs[sources:-3]
+def pair_kernel(*refs, passes, single, sources, begun, unroll):
+    blocks, start, outs = refs[:sources], refs[sources : sources + begun], refs[sources + begun : -3]
     others, own, back = refs[-3:]
     low = (lax.broadcasted_iota(jnp.int32, (SLOTS, 256), 1) & CZ) == 0
     at_z = lax.broadcasted_iota(jnp.int32, (SLOTS, CELLS), 1) & (CZ - 1)
@@ -427,29 +432,33 @@
                 there = there - pltpu.roll(jnp.where(low, 0.0, value), (at - CZ) % 256, 1)
             else:
                 here = here - pltpu.roll(value, at, 1)
-        if len(outs) == 1:
-            outs[0][d] = here[:, COLUMNS : COLUMNS + CELLS]
+        if not begun:
+            outs[0][d] = here
+            outs[1][d] = there
             continue
+        here = here + start[0][d]
+        there = there + start[1][d]
         for at, total in ((0, here), (3, there)):
             outs[at][d] = total[:, COLUMNS : COLUMNS + CELLS]
             outs[at + 1][d] = total[:, :COLUMNS]
             outs[at + 2][d] = total[:, COLUMNS + CELLS : 2 * COLUMNS + CELLS]
 
 
-def pair_forces(blocks, passes, single, unroll=4):
+def pair_forces(blocks, passes, single=0, start=(), unroll=4):
     rows = len(passes) * SLOTS
     pairs = rows * SLOTS * CELLS
-    widths = (CELLS, COLUMNS, COLUMNS) * 2 if len(blocks) > 3 else (CELLS,)
+    widths = (CELLS, COLUMNS, COLUMNS) * 2 if start else (256, 256)
     return pl.pallas_call(
         functools.partial(
             pair_kernel,
             passes=tuple(passes),
             single=single,
             sources=len(blocks),
+            begun=len(start),
             unroll=unroll,
         ),
         out_shape=[jax.ShapeDtypeStruct((3, SLOTS, width), F32) for width in widths],
-        in_specs=[VMEM] * len(blocks),
+        in_specs=[VMEM] * (len(blocks) + len(start)),
         out_specs=[VMEM] * len(widths),
         scratch_shapes=[
             pltpu.VMEM((6, rows + 8, CELLS), F32),
@@ -458,14 +467,14 @@
         ],
         compiler_params=params(8),
         cost_estimate=pl.CostEstimate(flops=70 * pairs, bytes_accessed=1 << 20, transcendentals=0),
-    )(*blocks)
-
-
-def join_kernel(near_ref, here_ref, down_ref, first_a, first_b, last_a, last_b, out_ref):
+    )(*blocks, *start)
+
+
+def join_kernel(here_ref, down_ref, first_a, first_b, last_a, last_b, out_ref):
     middle = jnp.zeros((SLOTS, CELLS - 2 * COLUMNS), F32)
     for d in range(3):
         sides = [first_a[d] + first_b[d], middle, last_a[d] + last_b[d]]
-        out_ref[d] = (near_ref[d] + here_ref[d] + down_ref[d] + jnp.concatenate(sides, axis=1)).T
+        out_ref[d] = (here_ref[d] + down_ref[d] + jnp.concatenate(sides, axis=1)).T
 
 
 def hbm(array):
@@ -521,36 +530,39 @@
     above_after = send(first, -1, -1)
     above_before = send(last, 1, -1)
 
-    spread, modes, edges = pl.pallas_call(
+    spread = pl.pallas_call(
         spread_kernel,
-        out_shape=(
-            jax.ShapeDtypeStruct((LZ, 1, BLOCK), F32),
-            jax.ShapeDtypeStruct((CX * CY, 3 * LZ, 512), BF16),
-            jax.ShapeDtypeStruct((CX * CY, 32, 512), F32),
-        ),
+        out_shape=jax.ShapeDtypeStruct((DY, DX, BLOCK), F32),
         in_specs=[VMEM] * 2,
-        out_specs=(ANY, VMEM, ANY),
+        out_specs=ANY,
         scratch_shapes=[
             pltpu.VMEM((BY, 40, LZ), F32),
             pltpu.VMEM((BLOCK, LZ), F32),
             pltpu.VMEM((LZ, BLOCK), F32),
-            pltpu.VMEM((CX * CY, 32, 512), F32),
-            pltpu.SemaphoreType.DMA((2,)),
+            pltpu.SemaphoreType.DMA((DX,)),
         ],
         compiler_params=params(16),
     )(rows, tz)
     spread, after, before, above, above_after, above_before = lax.optimization_barrier(
         (spread, after, before, above, above_after, above_before)
     )
-    lines = lax.all_to_all(hbm(spread), ("gx", "gy"), split_axis=0, concat_axis=0, tiled=True)
+    blocks = (atoms, before, after, above, above_before, above_after)
+    lines = lax.all_to_all(spread, "gy", split_axis=0, concat_axis=0, tiled=True)
+    sums = pair_forces(
+        blocks,
+        [(0, 0, 0), (0, 0, 1)] + [(a, 1 - a, c) for a in (0, 1) for c in (-1, 0, 1)],
+        single=1,
+    )
+    lines, *sums = lax.optimization_barrier((lines, *sums))
+    lines = jnp.transpose(lines, (1, 0, 2))
+    lines = lax.all_to_all(lines, "gx", split_axis=0, concat_axis=0, tiled=True)
     here, to_before, to_after, up, up_before, up_after = pair_forces(
-        (atoms, before, after, above, above_before, above_after),
-        [(a, 1, c) for a in (-1, 0, 1) for c in (-1, 0, 1)],
-        0,
+        blocks, [(a, 1, c) for a in (-1, 1) for c in (-1, 0, 1)], start=sums
     )
     lines, here, to_before, to_after, up, up_before, up_after = lax.optimization_barrier(
         (lines, here, to_before, to_after, up, up_before, up_after)
     )
+    lines = lines.reshape(DX * DY, BLOCK)
     sides = (
         send(up, 0, 1),
         send(to_after, 1, 0),
@@ -565,12 +577,11 @@
     fields = pl.pallas_call(
         plane_kernel,
         out_shape=jax.ShapeDtypeStruct((DX * DY, 1, 3 * BLOCK), F32),
-        in_specs=[SMEM] + [ANY] * 7,
+        in_specs=[SMEM, VMEM] + [ANY] * 6,
         out_specs=ANY,
         scratch_shapes=[
             *(pltpu.VMEM(tab[name].shape, BF16) for name in ("tx", "ty", "iy", "ix")),
             *(pltpu.VMEM(tab[name].shape, F32) for name in ("kx2", "ky2")),
-            pltpu.VMEM((DX * DY, BLOCK), F32),
             pltpu.VMEM((DX // 2, BY * DY, 128), F32),
             pltpu.VMEM((3, DX * DY, BLOCK), F32),
             pltpu.SemaphoreType.DMA((10,)),
@@ -578,32 +589,42 @@
         compiler_params=params(20),
     )(plane, lines, *constants)
     fields = lax.all_to_all(hbm(fields), ("gx", "gy"), split_axis=0, concat_axis=0, tiled=True)
-    beside = [(a, 0, c) for a in (-1, 1) for c in (-1, 0, 1)]
-    (near,) = pair_forces((atoms, before, after), [(0, 0, 0), *beside, (0, 0, 1)], 7)
     pair_force = pl.pallas_call(
         join_kernel,
         out_shape=jax.ShapeDtypeStruct((3, CELLS, SLOTS), F32),
-        in_specs=[VMEM] * 7,
+        in_specs=[VMEM] * 6,
         out_specs=VMEM,
         compiler_params=params(4),
-    )(near, here, *sides)
-    fields, pair_force = lax.optimization_barrier((fields, pair_force))
+    )(here, *sides)
+    modes, edges = pl.pallas_call(
+        weight_kernel,
+        out_shape=(
+            jax.ShapeDtypeStruct((CX * CY, 2 * LZ, 512), BF16),
+            jax.ShapeDtypeStruct((CX * CY, 32, 512), F32),
+        ),
+        in_specs=[VMEM] * 2,
+        out_specs=(VMEM, VMEM),
+        compiler_params=params(8),
+        cost_estimate=pl.CostEstimate(flops=1 << 28, bytes_accessed=1 << 20, transcendentals=0),
+    )(rows, tz)
+    fields, pair_force, modes, edges = lax.optimization_barrier(
+        (fields, pair_force, modes, edges)
+    )
 
     mesh_force = pl.pallas_call(
         force_kernel,
         out_shape=jax.ShapeDtypeStruct((3, CELLS, SLOTS), F32),
-        in_specs=[ANY, VMEM, ANY, VMEM],
+        in_specs=[ANY, VMEM, VMEM, VMEM],
         out_specs=VMEM,
         scratch_shapes=[
             pltpu.VMEM((3, LZ, BLOCK), F32),
             pltpu.VMEM((BLOCK, LZ), F32),
             pltpu.VMEM((3, BY, 40, LZ), F32),
             pltpu.VMEM((3, GROUPS, 128), F32),
-            pltpu.VMEM((CX * CY, 32, 512), F32),
-            pltpu.SemaphoreType.DMA((4,)),
+            pltpu.SemaphoreType.DMA((3,)),
         ],
         compiler_params=params(20),
-    )(fields, modes, hbm(edges), tab["swap"])
+    )(fields, modes, edges, tab["swap"])
     slot_first = lambda a: jnp.moveaxis(a.reshape(3, CX, CY, CZ, SLOTS), -1, 1)
     return slot_first(pair_force), slot_first(mesh_force)
 

time: 93.3 us -> 96.5 us (1.034)
  waiting for transfers between devices: 3.91 us -> 12.7 us
  local copies, waits for them, and re-layouts: 8.26 us -> 1.57 us
  starting transfers between devices: 35.9 us -> 38.1 us
  Pallas kernels: 44 us -> 43 us
    ppermute x10, waiting for transfers between devices: 3.9 us -> 12.7 us  [send(): return lax.ppermute(value, ('gx', 'gy'), route)]
    unnamed x28 -> x2, local copies, waits for them, and re-layouts: 7.56 us -> 0.01 us
    pallas_call x2, Pallas kernels: 24.1 us -> 21.1 us  [pair_forces(): pl.pallas_call(functools.partial(pair_kernel, passes=tuple(passes), singl...]
    all_to_all x1 -> x2, starting transfers between devices: 8.48 us -> 10.7 us  [the longest x1 5.8 us: body(): lines = lax.all_to_all(lines, 'gx', split_axis=0, concat_axis=0, tiled=True)]
    pallas_call x1 -> x2, Pallas kernels: 4.53 us -> 6.21 us  [the longest x1 4.66 us: body(): pl.pallas_call(spread_kernel, out_shape=jax.ShapeDtypeStruct((DY, DX, BLO...]
  transfers between devices with their start and end apart: 12 -> 13, of which waited for: 1 -> 2; matrix products, arithmetic and copies ran while one was open for 1% -> 1% of each run, Pallas kernels for 32% -> 29%
where the time goes in v4:
time: 96.5 us; the launch traced here: 96.1 us
  Pallas kernels  43 us (45%)
  starting transfers between devices  38.1 us (39%)
  waiting for transfers between devices  12.7 us (13%)
  local copies, waits for them, and re-layouts  1.57 us (2%)
    pallas_call x2, Pallas kernels, pair_forces(): pl.pallas_call(functools.partial(pair_kernel, passes=tuple(passes), singl...  21.1 us
    ppermute x10, starting transfers between devices, send(): return lax.ppermute(value, ('gx', 'gy'), route)  17.2 us
    ppermute x10, waiting for transfers between devices, send(): return lax.ppermute(value, ('gx', 'gy'), route)  12.7 us
    all_to_all x1, starting transfers between devices, body(): lax.all_to_all(hbm(fields), ('gx', 'gy'), split_axis=0, concat_axis=0, ti...  10.1 us
    pallas_call x1, Pallas kernels, body(): pl.pallas_call(plane_kernel, out_shape=jax.ShapeDtypeStruct((DX * DY, 1,...  7.12 us
    pallas_call x1, Pallas kernels, body(): pl.pallas_call(force_kernel, out_shape=jax.ShapeDtypeStruct((3, CELLS, SL...  6.06 us
    all_to_all x1, starting transfers between devices, body(): lines = lax.all_to_all(lines, 'gx', split_axis=0, concat_axis=0, tiled=True)  5.8 us
    all_to_all x1, starting transfers between devices, body(): lax.all_to_all(spread, 'gy', split_axis=0, concat_axis=0, tiled=True)  4.95 us
  transfers between devices with their start and end apart: 13, of which 2 were waited for; matrix products, arithmetic and copies ran while one was open for 1% of the time, Pallas kernels for 29%

profile of v4, /device:TPU:1, one launch (start us, length us, event | category | flops | bytes accessed | tf_op | source)
XLA Modules:
  0.0 96.1 jit_solution(680183152561135678)
XLA Ops:
  0.6 1.6 %shard_map.158 = (f32[6,32,128]{2,1,0:T(8,128)S(1)}, f32[6,32,32]{2,1,0:T(8,128)S(1)}, f32[6,32,32]{2,1,0:T(8,128)S(1)}, f32[4,32,128]{2,1,0:T(8,128)S(1)}, bf16[4,128,144]{2,1,0:T(8,128)(2,1)S(1)}) custom-call(f32[3,128,32]{2,1,0:T(8,128)} %bitcast.22, f32[128,32]{1,0:T(8,128)} %bitcast.24, s32[128,32]{1,0:T(8,128)} %bitcast.25, s32[4,2,16]{2,1,0:T(2,128)} %refs_3_.2, ...), custom_call_target="tpu_custom_call" | custom-call | tf_op jit(solution)/shard_map/pallas_call | solution.py:497
  2.3 7.1 %collective-permute-start.2 = (f32[6,32,128]{2,1,0:T(8,128)S(1)}, f32[6,32,128]{2,1,0:T(8,128)S(1)}, u32[]{:S(2)}, u32[]{:S(2)}) collective-permute-start(f32[6,32,128]{2,1,0:T(8,128)S(1)} %get-tuple-element.41.refs_0_), channel_id=1, source_target_pairs={{0,15},{1,0},{2,1},{3,2},{4,3},{5,4},{6,5},{7,6},{8,7},{9,8},{10,9... | collective-permute-start | bytes 294920 | tf_op jit(solution)/shard_map/ppermute | solution.py:490
  9.4 1.0 %collective-permute-start.3 = (f32[6,32,32]{2,1,0:T(8,128)S(1)}, f32[6,32,32]{2,1,0:T(8,128)S(1)}, u32[]{:S(2)}, u32[]{:S(2)}) collective-permute-start(f32[6,32,32]{2,1,0:T(8,128)S(1)} %get-tuple-element.39), channel_id=1, source_target_pairs={{0,127},{1,112},{2,113},{3,114},{4,115},{5,116},{6,117},{7,118},{8... | collective-permute-start | bytes 73736 | tf_op jit(solution)/shard_map/ppermute | solution.py:490
  10.3 1.7 %collective-permute-start = (f32[6,32,32]{2,1,0:T(8,128)S(1)}, f32[6,32,32]{2,1,0:T(8,128)S(1)}, u32[]{:S(2)}, u32[]{:S(2)}) collective-permute-start(f32[6,32,32]{2,1,0:T(8,128)S(1)} %get-tuple-element.39), channel_id=1, source_target_pairs={{0,112},{1,113},{2,114},{3,115},{4,116},{5,117},{6,118},{7,119},{8... | collective-permute-start | bytes 73736 | tf_op jit(solution)/shard_map/ppermute | solution.py:490
  12.1 4.7 %shard_map.159 = f32[16,8,768]{2,1,0:T(8,128)} custom-call(f32[4,32,128]{2,1,0:T(8,128)S(1)} %get-tuple-element.37.rows_ref, bf16[4,128,144]{2,1,0:T(8,128)(2,1)S(1)} %get-tuple-element.38.tz_ref), custom_call_target="tpu_custom_call" | custom-call | tf_op jit(solution)/shard_map/pallas_call | solution.py:533
  16.8 4.9 %all-to-all-start = ((f32[16,8,768]{2,1,0:T(8,128)}), f32[16,8,768]{2,1,0:T(8,128)S(1)}, u32[]{:S(2)}, u32[]{:S(2)}) async-start(f32[16,8,768]{2,1,0:T(8,128)} %shard_map.159), calls=%async_computation | async-start | bytes 786432 | tf_op jit(solution)/shard_map/all_to_all | solution.py:550
  21.8 12.0 %shard_map.160 = (f32[3,32,256]{2,1,0:T(8,128)S(1)}, f32[3,32,256]{2,1,0:T(8,128)S(1)}) custom-call(f32[6,32,128]{2,1,0:T(8,128)S(1)} %get-tuple-element.41.refs_0_, f32[6,32,32]{2,1,0:T(8,128)S(1)} %collective-permute-done.1.refs_1_, f32[6,32,32]{2,1,0:T(8,128)S(1)} %collective-permute-done.refs_2_, f32[6,32,128]{2,1,0:T(8,128)S(1)} %collective-permute-done.2.refs_3_, ...), custom_call_target="tpu_custom_call" | custom-call | flops 73400320 | bytes 1048576 | tf_op jit(solution)/shard_map/pallas_call | solution.py:451
  33.8 0.9 copy.18
  34.6 5.8 %all-to-all-start.1 = ((f32[8,16,768]{2,1,0:T(8,128)}), f32[8,16,768]{2,1,0:T(8,128)S(1)}, u32[]{:S(2)}, u32[]{:S(2)}) async-start(f32[8,16,768]{2,1,0:T(8,128)} %copy.18), calls=%async_computation.1 | async-start | bytes 786432 | tf_op jit(solution)/shard_map/all_to_all | solution.py:558
  40.4 0.7 dynamic-slice_bitcast_fusion.plane_ref
  41.1 9.1 %shard_map.161 = (f32[3,32,128]{2,1,0:T(8,128)S(1)}, f32[3,32,32]{2,1,0:T(8,128)S(1)}, f32[3,32,32]{2,1,0:T(8,128)S(1)}, f32[3,32,128]{2,1,0:T(8,128)S(1)}, f32[...) custom-call(f32[6,32,128]{2,1,0:T(8,128)S(1)} %get-tuple-element.41.refs_0_, ...), custom_call_target="tpu_custom_call" | custom-call | flops 55050240 | bytes 1048576 | tf_op jit(solution)/shard_map/pallas_call | solution.py:451
  50.3 7.1 %shard_map.162 = f32[128,1,2304]{2,1,0:T(1,128)} custom-call(f32[2]{0:T(128)S(1)} %dynamic-slice_bitcast_fusion.plane_ref, f32[128,768]{1,0:T(8,128)S(1)} %bitcast.19, bf16[1536,256]{1,0:T(8,128)(2,1)} %constant.37.clone.refs_0_, bf16[256,960]{1,0:T(8,128)(2,1)} %constant.38.clone.refs_1_, bf16[640,768]{1,0:T(8,128)(2,1)} %constant.39.clone.refs_2_, ...), custom_call_target="tpu_custom_call" | custom-call | tf_op jit(solution)/shard_map/pallas_call | solution.py:577
  57.4 10.1 %all-to-all-start.2 = ((f32[128,1,2304]{2,1,0:T(1,128)}), f32[128,1,2304]{2,1,0:T(1,128)}, u32[]{:S(2)}, u32[]{:S(2)}) async-start(f32[128,1,2304]{2,1,0:T(1,128)} %shard_map.162), calls=%async_computation.2 | async-start | bytes 2359296 | tf_op jit(solution)/shard_map/all_to_all | solution.py:591
  67.5 0.0 copy-start
  67.5 1.6 %collective-permute-start.5 = (f32[3,32,128]{2,1,0:T(8,128)S(1)}, f32[3,32,128]{2,1,0:T(8,128)S(1)}, u32[]{:S(2)}, u32[]{:S(2)}) collective-permute-start(f32[3,32,128]{2,1,0:T(8,128)S(1)} %get-tuple-element.61), channel_id=1, source_target_pairs={{0,1},{1,2},{2,3},{3,4},{4,5},{5,6},{6,7},{7,8},{8,9},{9,10},{10,1... | collective-permute-start | bytes 147464 | tf_op jit(solution)/shard_map/ppermute | solution.py:490
  69.1 1.7 %collective-permute-start.6 = (f32[3,32,32]{2,1,0:T(8,128)S(1)}, f32[3,32,32]{2,1,0:T(8,128)S(1)}, u32[]{:S(2)}, u32[]{:S(2)}) collective-permute-start(f32[3,32,32]{2,1,0:T(8,128)S(1)} %get-tuple-element.62), channel_id=1, source_target_pairs={{0,16},{1,17},{2,18},{3,19},{4,20},{5,21},{6,22},{7,23},{8,24},{9,... | collective-permute-start | bytes 36872 | tf_op jit(solution)/shard_map/ppermute | solution.py:490
  70.8 1.2 %collective-permute-start.7 = (f32[3,32,32]{2,1,0:T(8,128)S(1)}, f32[3,32,32]{2,1,0:T(8,128)S(1)}, u32[]{:S(2)}, u32[]{:S(2)}) collective-permute-start(f32[3,32,32]{2,1,0:T(8,128)S(1)} %get-tuple-element.63), channel_id=1, source_target_pairs={{0,17},{1,18},{2,19},{3,20},{4,21},{5,22},{6,23},{7,24},{8,25},{9,... | collective-permute-start | bytes 36872 | tf_op jit(solution)/shard_map/ppermute | solution.py:490
  72.0 0.7 collective-permute-start.8
  72.7 2.2 %collective-permute-start.9 = (f32[3,32,32]{2,1,0:T(8,128)S(1)}, f32[3,32,32]{2,1,0:T(8,128)S(1)}, u32[]{:S(2)}, u32[]{:S(2)}) collective-permute-start(f32[3,32,32]{2,1,0:T(8,128)S(1)} %get-tuple-element.65), channel_id=1, source_target_pairs={{0,113},{1,114},{2,115},{3,116},{4,117},{5,118},{6,119},{7,120},{8... | collective-permute-start | bytes 36872 | tf_op jit(solution)/shard_map/ppermute | solution.py:490
  74.9 1.5 %shard_map.164 = (bf16[8,256,512]{2,1,0:T(8,128)(2,1)S(1)}, f32[8,32,512]{2,1,0:T(8,128)S(1)}) custom-call(f32[4,32,128]{2,1,0:T(8,128)S(1)} %get-tuple-element.37.rows_ref, bf16[4,128,144]{2,1,0:T(8,128)(2,1)S(1)} %get-tuple-element.38.tz_ref), custom_call_target="tpu_custom_call" | custom-call | flops 268435456 | bytes 1048576 | tf_op jit(solution)/shard_map/pallas_call | solution.py:599
  76.5 3.0 %collective-permute-done.6.first_a = f32[3,32,32]{2,1,0:T(8,128)S(1)} collective-permute-done((f32[3,32,32]{2,1,0:T(8,128)S(1)}, f32[3,32,32]{2,1,0:T(8,128)S(1)}, u32[]{:S(2)}, u32[]{:S(2)}) %collective-permute-start.6) | collective-permute-done | bytes 12320 | tf_op jit(solution)/shard_map/ppermute | solution.py:490
  79.5 9.6 %collective-permute-done.7.first_b = f32[3,32,32]{2,1,0:T(8,128)S(1)} collective-permute-done((f32[3,32,32]{2,1,0:T(8,128)S(1)}, f32[3,32,32]{2,1,0:T(8,128)S(1)}, u32[]{:S(2)}, u32[]{:S(2)}) %collective-permute-start.7) | collective-permute-done | bytes 12320 | tf_op jit(solution)/shard_map/ppermute | solution.py:490
  89.1 0.9 shard_map.163
  90.0 6.1 %shard_map.165 = f32[3,128,32]{2,1,0:T(8,128)} custom-call(f32[128,1,2304]{2,1,0:T(1,128)} %all-to-all-done.2.in_ref, bf16[8,256,512]{2,1,0:T(8,128)(2,1)S(1)} %get-tuple-element.70.modes_ref, f32[8,32,512]{2,1,0:T(8,128)S(1)} %get-tuple-element.71.edges_ref, f32[1,128]{1,0:T(1,128)S(1)} %copy-done), custom_call_target="tpu_custom_call" | custom-call | tf_op jit(solution)/shard_map/pallas_call | solution.py:614
  (14 shorter events, 0.0 us)
Async XLA Ops:
  2.3 14.5 %collective-permute-start.2 = (f32[6,32,128]{2,1,0:T(8,128)S(1)}, f32[6,32,128]{2,1,0:T(8,128)S(1)}, u32[]{:S(2)}, u32[]{:S(2)}) collective-permute-start(f32[6,32,128]{2,1,0:T(8,128)S(1)} %get-tuple-element.41.refs_0_), channel_id=1, source_target_pairs={{0,15},{1,0},{2,1},{3,2},{4,3},{5,4},{6,5},{7,6},{8,7},{9,8},{10,9... | collective-permute-start | bytes 294920 | tf_op jit(solution)/shard_map/ppermute | solution.py:490
  9.4 7.4 %collective-permute-start.3 = (f32[6,32,32]{2,1,0:T(8,128)S(1)}, f32[6,32,32]{2,1,0:T(8,128)S(1)}, u32[]{:S(2)}, u32[]{:S(2)}) collective-permute-start(f32[6,32,32]{2,1,0:T(8,128)S(1)} %get-tuple-element.39), channel_id=1, source_target_pairs={{0,127},{1,112},{2,113},{3,114},{4,115},{5,116},{6,117},{7,118},{8... | collective-permute-start | bytes 73736 | tf_op jit(solution)/shard_map/ppermute | solution.py:490
  10.3 6.4 %collective-permute-start = (f32[6,32,32]{2,1,0:T(8,128)S(1)}, f32[6,32,32]{2,1,0:T(8,128)S(1)}, u32[]{:S(2)}, u32[]{:S(2)}) collective-permute-start(f32[6,32,32]{2,1,0:T(8,128)S(1)} %get-tuple-element.39), channel_id=1, source_target_pairs={{0,112},{1,113},{2,114},{3,115},{4,116},{5,117},{6,118},{7,119},{8... | collective-permute-start | bytes 73736 | tf_op jit(solution)/shard_map/ppermute | solution.py:490
  12.1 4.7 %collective-permute-start.4 = (f32[6,32,32]{2,1,0:T(8,128)S(1)}, f32[6,32,32]{2,1,0:T(8,128)S(1)}, u32[]{:S(2)}, u32[]{:S(2)}) collective-permute-start(f32[6,32,32]{2,1,0:T(8,128)S(1)} %get-tuple-element.40), channel_id=1, source_target_pairs={{0,31},{1,16},{2,17},{3,18},{4,19},{5,20},{6,21},{7,22},{8,23},{9,... | collective-permute-start | bytes 73736 | tf_op jit(solution)/shard_map/ppermute | solution.py:490
  12.1 4.7 %collective-permute-start.1 = (f32[6,32,32]{2,1,0:T(8,128)S(1)}, f32[6,32,32]{2,1,0:T(8,128)S(1)}, u32[]{:S(2)}, u32[]{:S(2)}) collective-permute-start(f32[6,32,32]{2,1,0:T(8,128)S(1)} %get-tuple-element.40), channel_id=1, source_target_pairs={{0,16},{1,17},{2,18},{3,19},{4,20},{5,21},{6,22},{7,23},{8,24},{9,... | collective-permute-start | bytes 73736 | tf_op jit(solution)/shard_map/ppermute | solution.py:490
  16.8 17.0 %all-to-all-start = ((f32[16,8,768]{2,1,0:T(8,128)}), f32[16,8,768]{2,1,0:T(8,128)S(1)}, u32[]{:S(2)}, u32[]{:S(2)}) async-start(f32[16,8,768]{2,1,0:T(8,128)} %shard_map.159), calls=%async_computation | async-start | bytes 786432 | tf_op jit(solution)/shard_map/all_to_all | solution.py:550
  34.6 15.6 %all-to-all-start.1 = ((f32[8,16,768]{2,1,0:T(8,128)}), f32[8,16,768]{2,1,0:T(8,128)S(1)}, u32[]{:S(2)}, u32[]{:S(2)}) async-start(f32[8,16,768]{2,1,0:T(8,128)} %copy.18), calls=%async_computation.1 | async-start | bytes 786432 | tf_op jit(solution)/shard_map/all_to_all | solution.py:558
  57.4 32.6 %all-to-all-start.2 = ((f32[128,1,2304]{2,1,0:T(1,128)}), f32[128,1,2304]{2,1,0:T(1,128)}, u32[]{:S(2)}, u32[]{:S(2)}) async-start(f32[128,1,2304]{2,1,0:T(1,128)} %shard_map.162), calls=%async_computation.2 | async-start | bytes 2359296 | tf_op jit(solution)/shard_map/all_to_all | solution.py:591
  67.5 22.5 %copy-start = (f32[1,128]{1,0:T(1,128)S(1)}, f32[1,128]{1,0:T(1,128)}, u32[]{:S(2)}) copy-start(f32[1,128]{1,0:T(1,128)} %constant.43.clone.swap_ref) | copy-start | bytes 1540
  67.5 21.6 %collective-permute-start.5 = (f32[3,32,128]{2,1,0:T(8,128)S(1)}, f32[3,32,128]{2,1,0:T(8,128)S(1)}, u32[]{:S(2)}, u32[]{:S(2)}) collective-permute-start(f32[3,32,128]{2,1,0:T(8,128)S(1)} %get-tuple-element.61), channel_id=1, source_target_pairs={{0,1},{1,2},{2,3},{3,4},{4,5},{5,6},{6,7},{7,8},{8,9},{9,10},{10,1... | collective-permute-start | bytes 147464 | tf_op jit(solution)/shard_map/ppermute | solution.py:490
  69.1 10.4 %collective-permute-start.6 = (f32[3,32,32]{2,1,0:T(8,128)S(1)}, f32[3,32,32]{2,1,0:T(8,128)S(1)}, u32[]{:S(2)}, u32[]{:S(2)}) collective-permute-start(f32[3,32,32]{2,1,0:T(8,128)S(1)} %get-tuple-element.62), channel_id=1, source_target_pairs={{0,16},{1,17},{2,18},{3,19},{4,20},{5,21},{6,22},{7,23},{8,24},{9,... | collective-permute-start | bytes 36872 | tf_op jit(solution)/shard_map/ppermute | solution.py:490
  70.8 18.3 %collective-permute-start.7 = (f32[3,32,32]{2,1,0:T(8,128)S(1)}, f32[3,32,32]{2,1,0:T(8,128)S(1)}, u32[]{:S(2)}, u32[]{:S(2)}) collective-permute-start(f32[3,32,32]{2,1,0:T(8,128)S(1)} %get-tuple-element.63), channel_id=1, source_target_pairs={{0,17},{1,18},{2,19},{3,20},{4,21},{5,22},{6,23},{7,24},{8,25},{9,... | collective-permute-start | bytes 36872 | tf_op jit(solution)/shard_map/ppermute | solution.py:490
  72.0 17.1 %collective-permute-start.8 = (f32[3,32,32]{2,1,0:T(8,128)S(1)}, f32[3,32,32]{2,1,0:T(8,128)S(1)}, u32[]{:S(2)}, u32[]{:S(2)}) collective-permute-start(f32[3,32,32]{2,1,0:T(8,128)S(1)} %get-tuple-element.64), channel_id=1, source_target_pairs={{0,112},{1,113},{2,114},{3,115},{4,116},{5,117},{6,118},{7,119},{8... | collective-permute-start | bytes 36872 | tf_op jit(solution)/shard_map/ppermute | solution.py:490
  72.7 16.4 %collective-permute-start.9 = (f32[3,32,32]{2,1,0:T(8,128)S(1)}, f32[3,32,32]{2,1,0:T(8,128)S(1)}, u32[]{:S(2)}, u32[]{:S(2)}) collective-permute-start(f32[3,32,32]{2,1,0:T(8,128)S(1)} %get-tuple-element.65), channel_id=1, source_target_pairs={{0,113},{1,114},{2,115},{3,116},{4,117},{5,118},{6,119},{7,120},{8... | collective-permute-start | bytes 36872 | tf_op jit(solution)/shard_map/ppermute | solution.py:490

commit v5 on v4

--- a/solution.py
+++ b/solution.py
@@ -208,7 +208,7 @@
     incoming[-1].wait()
 
 
-def spread_kernel(rows_ref, tz_ref, spread_out, total, packed, turned, sems):
+def spread_kernel(rows_ref, tz_ref, spread_out, total, packed, turned, sem):
     total[...] = jnp.zeros_like(total)
 
     def column(col, carry):
@@ -224,13 +224,7 @@
         packed[y * BX : (y + 1) * BX, :] = total[y, :BX, :]
     packed[BX * BY :, :] = jnp.zeros((BLOCK - BX * BY, LZ), F32)
     turned[...] = packed[...].T
-    outgoing = started(
-        *(
-            (turned.at[gx * DY : (gx + 1) * DY, :], spread_out.at[:, gx, :], sems.at[gx])
-            for gx in range(DX)
-        )
-    )
-    for copy in outgoing:
+    for copy in started((turned, spread_out.at[:, 0, :], sem)):
         copy.wait()
 
 
@@ -243,11 +237,13 @@
     lax.fori_loop(0, CX * CY, column, 0, unroll=2)
 
 
-def plane_kernel(plane_ref, lines, *refs):
+def plane_kernel(plane_ref, in_ref, *refs):
     sources, out_ref, held = refs[:6], refs[6], refs[7:13]
-    stacked, turned, sems = refs[13:]
+    lines, stacked, turned, sems = refs[13:]
     tx, ty, iy, ix, kx2, ky2 = held
+    (arrival,) = started((in_ref.at[:, 0, :], lines, sems.at[3]))
     constants = started(*((s, t, sems.at[4 + n]) for n, (s, t) in enumerate(zip(sources, held))))
+    arrival.wait()
     for y in range(BY):
         value = lines[:, y * BX : y * BX + KX]
         for gx in range(DX):
@@ -532,14 +528,14 @@
 
     spread = pl.pallas_call(
         spread_kernel,
-        out_shape=jax.ShapeDtypeStruct((DY, DX, BLOCK), F32),
+        out_shape=jax.ShapeDtypeStruct((LZ, 1, BLOCK), F32),
         in_specs=[VMEM] * 2,
         out_specs=ANY,
         scratch_shapes=[
             pltpu.VMEM((BY, 40, LZ), F32),
             pltpu.VMEM((BLOCK, LZ), F32),
             pltpu.VMEM((LZ, BLOCK), F32),
-            pltpu.SemaphoreType.DMA((DX,)),
+            pltpu.SemaphoreType.DMA,
         ],
         compiler_params=params(16),
     )(rows, tz)
@@ -547,55 +543,12 @@
         (spread, after, before, above, above_after, above_before)
     )
     blocks = (atoms, before, after, above, above_before, above_after)
-    lines = lax.all_to_all(spread, "gy", split_axis=0, concat_axis=0, tiled=True)
+    lines = lax.all_to_all(hbm(spread), ("gx", "gy"), split_axis=0, concat_axis=0, tiled=True)
     sums = pair_forces(
         blocks,
         [(0, 0, 0), (0, 0, 1)] + [(a, 1 - a, c) for a in (0, 1) for c in (-1, 0, 1)],
         single=1,
     )
-    lines, *sums = lax.optimization_barrier((lines, *sums))
-    lines = jnp.transpose(lines, (1, 0, 2))
-    lines = lax.all_to_all(lines, "gx", split_axis=0, concat_axis=0, tiled=True)
-    here, to_before, to_after, up, up_before, up_after = pair_forces(
-        blocks, [(a, 1, c) for a in (-1, 1) for c in (-1, 0, 1)], start=sums
-    )
-    lines, here, to_before, to_after, up, up_before, up_after = lax.optimization_barrier(
-        (lines, here, to_before, to_after, up, up_before, up_after)
-    )
-    lines = lines.reshape(DX * DY, BLOCK)
-    sides = (
-        send(up, 0, 1),
-        send(to_after, 1, 0),
-        send(up_after, 1, 1),
-        send(to_before, -1, 0),
-        send(up_before, -1, 1),
-    )
-
-    index = lax.axis_index("gx") * DY + lax.axis_index("gy")
-    plane = lax.dynamic_index_in_dim(jnp.asarray(tab["plane"]), index, 0, keepdims=False)
-    constants = [hbm(tab[name]) for name in ("tx", "ty", "iy", "ix", "kx2", "ky2")]
-    fields = pl.pallas_call(
-        plane_kernel,
-        out_shape=jax.ShapeDtypeStruct((DX * DY, 1, 3 * BLOCK), F32),
-        in_specs=[SMEM, VMEM] + [ANY] * 6,
-        out_specs=ANY,
-        scratch_shapes=[
-            *(pltpu.VMEM(tab[name].shape, BF16) for name in ("tx", "ty", "iy", "ix")),
-            *(pltpu.VMEM(tab[name].shape, F32) for name in ("kx2", "ky2")),
-            pltpu.VMEM((DX // 2, BY * DY, 128), F32),
-            pltpu.VMEM((3, DX * DY, BLOCK), F32),
-            pltpu.SemaphoreType.DMA((10,)),
-        ],
-        compiler_params=params(20),
-    )(plane, lines, *constants)
-    fields = lax.all_to_all(hbm(fields), ("gx", "gy"), split_axis=0, concat_axis=0, tiled=True)
-    pair_force = pl.pallas_call(
-        join_kernel,
-        out_shape=jax.ShapeDtypeStruct((3, CELLS, SLOTS), F32),
-        in_specs=[VMEM] * 6,
-        out_specs=VMEM,
-        compiler_params=params(4),
-    )(here, *sides)
     modes, edges = pl.pallas_call(
         weight_kernel,
         out_shape=(
@@ -607,10 +560,39 @@
         compiler_params=params(8),
         cost_estimate=pl.CostEstimate(flops=1 << 28, bytes_accessed=1 << 20, transcendentals=0),
     )(rows, tz)
-    fields, pair_force, modes, edges = lax.optimization_barrier(
-        (fields, pair_force, modes, edges)
-    )
-
+    lines, modes, edges, *sums = lax.optimization_barrier((lines, modes, edges, *sums))
+
+    index = lax.axis_index("gx") * DY + lax.axis_index("gy")
+    plane = lax.dynamic_index_in_dim(jnp.asarray(tab["plane"]), index, 0, keepdims=False)
+    constants = [hbm(tab[name]) for name in ("tx", "ty", "iy", "ix", "kx2", "ky2")]
+    fields = pl.pallas_call(
+        plane_kernel,
+        out_shape=jax.ShapeDtypeStruct((DX * DY, 1, 3 * BLOCK), F32),
+        in_specs=[SMEM] + [ANY] * 7,
+        out_specs=ANY,
+        scratch_shapes=[
+            *(pltpu.VMEM(tab[name].shape, BF16) for name in ("tx", "ty", "iy", "ix")),
+            *(pltpu.VMEM(tab[name].shape, F32) for name in ("kx2", "ky2")),
+            pltpu.VMEM((DX * DY, BLOCK), F32),
+            pltpu.VMEM((DX // 2, BY * DY, 128), F32),
+            pltpu.VMEM((3, DX * DY, BLOCK), F32),
+            pltpu.SemaphoreType.DMA((10,)),
+        ],
+        compiler_params=params(20),
+    )(plane, lines, *constants)
+    fields = lax.all_to_all(hbm(fields), ("gx", "gy"), split_axis=0, concat_axis=0, tiled=True)
+    here, to_before, to_after, up, up_before, up_after = pair_forces(
+        blocks, [(a, 1, c) for a in (-1, 1) for c in (-1, 0, 1)], start=sums
+    )
+    sides = (
+        send(up, 0, 1),
+        send(to_after, 1, 0),
+        send(up_after, 1, 1),
+        send(to_before, -1, 0),
+        send(up_before, -1, 1),
+    )
+
+    fields, here = lax.optimization_barrier((fields, here))
     mesh_force = pl.pallas_call(
         force_kernel,
         out_shape=jax.ShapeDtypeStruct((3, CELLS, SLOTS), F32),
@@ -625,6 +607,15 @@
         ],
         compiler_params=params(20),
     )(fields, modes, edges, tab["swap"])
+    mesh_force, here = lax.optimization_barrier((mesh_force, here))
+    pair_force = pl.pallas_call(
+        join_kernel,
+        out_shape=jax.ShapeDtypeStruct((3, CELLS, SLOTS), F32),
+        in_specs=[VMEM] * 6,
+        out_specs=VMEM,
+        compiler_params=params(4),
+    )(here, *sides)
+
     slot_first = lambda a: jnp.moveaxis(a.reshape(3, CX, CY, CZ, SLOTS), -1, 1)
     return slot_first(pair_force), slot_first(mesh_force)
 

time: 96.5 us -> 84 us (0.87)
  waiting for transfers between devices: 12.7 us -> 2.92 us
  starting transfers between devices: 38.1 us -> 36.1 us
    ppermute x10, waiting for transfers between devices: 12.7 us -> 0.04 us  [send(): return lax.ppermute(value, ('gx', 'gy'), route)]
    all_to_all x1, waiting for transfers between devices: 0.01 us -> 2.87 us  [body(): lax.all_to_all(hbm(fields), ('gx', 'gy'), split_axis=0, concat_axis=0, ti...]
    all_to_all x2 -> x1, starting transfers between devices: 10.7 us -> 8.81 us  [body(): lax.all_to_all(hbm(spread), ('gx', 'gy'), split_axis=0, concat_axis=0, ti...]
  transfers between devices with their start and end apart: 13 -> 12, of which waited for: 2 -> 1; matrix products, arithmetic and copies ran while one was open for 1% -> 1% of each run, Pallas kernels for 29% -> 41%
where the time goes in v5:
time: 84 us; the launch traced here: 83.7 us
  Pallas kernels  43.1 us (51%)
  starting transfers between devices  36.1 us (43%)
  waiting for transfers between devices  2.92 us (3%)
    pallas_call x2, Pallas kernels, pair_forces(): pl.pallas_call(functools.partial(pair_kernel, passes=tuple(passes), singl...  21.8 us
    ppermute x10, starting transfers between devices, send(): return lax.ppermute(value, ('gx', 'gy'), route)  17.1 us
    all_to_all x1, starting transfers between devices, body(): lax.all_to_all(hbm(fields), ('gx', 'gy'), split_axis=0, concat_axis=0, ti...  10.2 us
    all_to_all x1, starting transfers between devices, body(): lax.all_to_all(hbm(spread), ('gx', 'gy'), split_axis=0, concat_axis=0, ti...  8.81 us
    pallas_call x1, Pallas kernels, body(): pl.pallas_call(plane_kernel, out_shape=jax.ShapeDtypeStruct((DX * DY, 1,...  6.67 us
    pallas_call x1, Pallas kernels, body(): pl.pallas_call(force_kernel, out_shape=jax.ShapeDtypeStruct((3, CELLS, SL...  6.04 us
    pallas_call x1, Pallas kernels, body(): pl.pallas_call(spread_kernel, out_shape=jax.ShapeDtypeStruct((LZ, 1, BLOC...  4.6 us
    all_to_all x1, waiting for transfers between devices, body(): lax.all_to_all(hbm(fields), ('gx', 'gy'), split_axis=0, concat_axis=0, ti...  2.87 us
  transfers between devices with their start and end apart: 12, of which 1 were waited for; matrix products, arithmetic and copies ran while one was open for 1% of the time, Pallas kernels for 41%

profile of v5, /device:TPU:1, one launch (start us, length us, event | category | flops | bytes accessed | tf_op | source)
XLA Modules:
  0.0 83.7 jit_solution(15685374225605703065)
XLA Ops:
  0.6 1.6 %shard_map.158 = (f32[6,32,128]{2,1,0:T(8,128)S(1)}, f32[6,32,32]{2,1,0:T(8,128)S(1)}, f32[6,32,32]{2,1,0:T(8,128)S(1)}, f32[4,32,128]{2,1,0:T(8,128)S(1)}, bf16[4,128,144]{2,1,0:T(8,128)(2,1)S(1)}) custom-call(f32[3,128,32]{2,1,0:T(8,128)} %bitcast.18, f32[128,32]{1,0:T(8,128)} %bitcast.20, s32[128,32]{1,0:T(8,128)} %bitcast.21, s32[4,2,16]{2,1,0:T(2,128)} %refs_3_.2, ...), custom_call_target="tpu_custom_call" | custom-call | tf_op jit(solution)/shard_map/pallas_call | solution.py:493
  2.3 7.1 %collective-permute-start.2 = (f32[6,32,128]{2,1,0:T(8,128)S(1)}, f32[6,32,128]{2,1,0:T(8,128)S(1)}, u32[]{:S(2)}, u32[]{:S(2)}) collective-permute-start(f32[6,32,128]{2,1,0:T(8,128)S(1)} %get-tuple-element.36.refs_0_), channel_id=1, source_target_pairs={{0,15},{1,0},{2,1},{3,2},{4,3},{5,4},{6,5},{7,6},{8,7},{9,8},{10,9... | collective-permute-start | bytes 294920 | tf_op jit(solution)/shard_map/ppermute | solution.py:486
  9.4 1.0 %collective-permute-start.3 = (f32[6,32,32]{2,1,0:T(8,128)S(1)}, f32[6,32,32]{2,1,0:T(8,128)S(1)}, u32[]{:S(2)}, u32[]{:S(2)}) collective-permute-start(f32[6,32,32]{2,1,0:T(8,128)S(1)} %get-tuple-element.34), channel_id=1, source_target_pairs={{0,127},{1,112},{2,113},{3,114},{4,115},{5,116},{6,117},{7,118},{8... | collective-permute-start | bytes 73736 | tf_op jit(solution)/shard_map/ppermute | solution.py:486
  10.3 1.7 %collective-permute-start = (f32[6,32,32]{2,1,0:T(8,128)S(1)}, f32[6,32,32]{2,1,0:T(8,128)S(1)}, u32[]{:S(2)}, u32[]{:S(2)}) collective-permute-start(f32[6,32,32]{2,1,0:T(8,128)S(1)} %get-tuple-element.34), channel_id=1, source_target_pairs={{0,112},{1,113},{2,114},{3,115},{4,116},{5,117},{6,118},{7,119},{8... | collective-permute-start | bytes 73736 | tf_op jit(solution)/shard_map/ppermute | solution.py:486
  12.1 4.6 %shard_map.159 = f32[128,1,768]{2,1,0:T(1,128)} custom-call(f32[4,32,128]{2,1,0:T(8,128)S(1)} %get-tuple-element.32.rows_ref, bf16[4,128,144]{2,1,0:T(8,128)(2,1)S(1)} %get-tuple-element.33.tz_ref), custom_call_target="tpu_custom_call" | custom-call | tf_op jit(solution)/shard_map/pallas_call | solution.py:529
  16.7 0.0 collective-permute-done.4.refs_4_
  16.7 8.8 %all-to-all-start = ((f32[128,1,768]{2,1,0:T(1,128)}), f32[128,1,768]{2,1,0:T(1,128)}, u32[]{:S(2)}, u32[]{:S(2)}) async-start(f32[128,1,768]{2,1,0:T(1,128)} %shard_map.159), calls=%async_computation | async-start | bytes 786432 | tf_op jit(solution)/shard_map/all_to_all | solution.py:546
  25.6 1.5 %shard_map.160 = (bf16[8,256,512]{2,1,0:T(8,128)(2,1)S(1)}, f32[8,32,512]{2,1,0:T(8,128)S(1)}) custom-call(f32[4,32,128]{2,1,0:T(8,128)S(1)} %get-tuple-element.32.rows_ref, bf16[4,128,144]{2,1,0:T(8,128)(2,1)S(1)} %get-tuple-element.33.tz_ref), custom_call_target="tpu_custom_call" | custom-call | flops 268435456 | bytes 1048576 | tf_op jit(solution)/shard_map/pallas_call | solution.py:552
  27.1 0.7 dynamic-slice_bitcast_fusion.plane_ref
  27.8 12.0 %shard_map.161 = (f32[3,32,256]{2,1,0:T(8,128)S(1)}, f32[3,32,256]{2,1,0:T(8,128)S(1)}) custom-call(f32[6,32,128]{2,1,0:T(8,128)S(1)} %get-tuple-element.36.refs_0_, f32[6,32,32]{2,1,0:T(8,128)S(1)} %collective-permute-done.1.refs_1_, f32[6,32,32]{2,1,0:T(8,128)S(1)} %collective-permute-done.refs_2_, f32[6,32,128]{2,1,0:T(8,128)S(1)} %collective-permute-done.2.refs_3_, ...), custom_call_target="tpu_custom_call" | custom-call | flops 73400320 | bytes 1048576 | tf_op jit(solution)/shard_map/pallas_call | solution.py:447
  39.8 6.7 %shard_map.162 = f32[128,1,2304]{2,1,0:T(1,128)} custom-call(f32[2]{0:T(128)S(1)} %dynamic-slice_bitcast_fusion.plane_ref, f32[128,1,768]{2,1,0:T(1,128)} %all-to-all-done.in_ref, bf16[1536,256]{1,0:T(8,128)(2,1)} %constant.37.clone.refs_0_, bf16[256,960]{1,0:T(8,128)(2,1)} %constant.38.clone.refs_1_, bf16[640,768]{1,0:T(8,128)(2,1)} %constant.39.clone.refs_2_, ...), custom_call_target="tpu_custom_call" | custom-call | tf_op jit(solution)/shard_map/pallas_call | solution.py:568
  46.5 0.0 copy-start
  46.5 10.2 %all-to-all-start.1 = ((f32[128,1,2304]{2,1,0:T(1,128)}), f32[128,1,2304]{2,1,0:T(1,128)}, u32[]{:S(2)}, u32[]{:S(2)}) async-start(f32[128,1,2304]{2,1,0:T(1,128)} %shard_map.162), calls=%async_computation.1 | async-start | bytes 2359296 | tf_op jit(solution)/shard_map/all_to_all | solution.py:583
  56.7 9.8 %shard_map.163 = (f32[3,32,128]{2,1,0:T(8,128)S(1)}, f32[3,32,32]{2,1,0:T(8,128)}, f32[3,32,32]{2,1,0:T(8,128)}, f32[3,32,128]{2,1,0:T(8,128)S(1)}, f32[3,32,32]{2,1,0:T(8,128)}, /*index=5*/f32[3,32,32]{2,1,0:T(8,128)}) custom-call(f32[6,32,128]{2,1,0:T(8,128)S(1)} %get-tuple-element.36.refs_0_, f32[6,32,32]{2,1,0:T(8,128)S(1)} %collective-permute-done.1.refs_1_, ...), custom_call_target="tpu_custom_call" | custom-call | flops 55050240 | bytes 1048576 | tf_op jit(solution)/shard_map/pallas_call | solution.py:447
  66.5 1.5 %collective-permute-start.5 = (f32[3,32,128]{2,1,0:T(8,128)S(1)}, f32[3,32,128]{2,1,0:T(8,128)S(1)}, u32[]{:S(2)}, u32[]{:S(2)}) collective-permute-start(f32[3,32,128]{2,1,0:T(8,128)S(1)} %get-tuple-element.56), channel_id=1, source_target_pairs={{0,1},{1,2},{2,3},{3,4},{4,5},{5,6},{6,7},{7,8},{8,9},{9,10},{10,1... | collective-permute-start | bytes 147464 | tf_op jit(solution)/shard_map/ppermute | solution.py:486
  68.0 1.7 %collective-permute-start.6 = (f32[3,32,32]{2,1,0:T(8,128)}, f32[3,32,32]{2,1,0:T(8,128)S(1)}, u32[]{:S(2)}, u32[]{:S(2)}) collective-permute-start(f32[3,32,32]{2,1,0:T(8,128)} %get-tuple-element.57), channel_id=1, source_target_pairs={{0,16},{1,17},{2,18},{3,19},{4,20},{5,21},{6,22},{7,23},{8,24},{9,... | collective-permute-start | bytes 36872 | tf_op jit(solution)/shard_map/ppermute | solution.py:486
  69.7 1.2 %collective-permute-start.7 = (f32[3,32,32]{2,1,0:T(8,128)}, f32[3,32,32]{2,1,0:T(8,128)S(1)}, u32[]{:S(2)}, u32[]{:S(2)}) collective-permute-start(f32[3,32,32]{2,1,0:T(8,128)} %get-tuple-element.58), channel_id=1, source_target_pairs={{0,17},{1,18},{2,19},{3,20},{4,21},{5,22},{6,23},{7,24},{8,25},{9,... | collective-permute-start | bytes 36872 | tf_op jit(solution)/shard_map/ppermute | solution.py:486
  70.9 0.7 collective-permute-start.8
  71.6 2.2 %collective-permute-start.9 = (f32[3,32,32]{2,1,0:T(8,128)}, f32[3,32,32]{2,1,0:T(8,128)S(1)}, u32[]{:S(2)}, u32[]{:S(2)}) collective-permute-start(f32[3,32,32]{2,1,0:T(8,128)} %get-tuple-element.60), channel_id=1, source_target_pairs={{0,113},{1,114},{2,115},{3,116},{4,117},{5,118},{6,119},{7,120},{8... | collective-permute-start | bytes 36872 | tf_op jit(solution)/shard_map/ppermute | solution.py:486
  73.8 2.9 %all-to-all-done.1.in_ref = f32[128,1,2304]{2,1,0:T(1,128)} async-done(((f32[128,1,2304]{2,1,0:T(1,128)}), f32[128,1,2304]{2,1,0:T(1,128)}, u32[]{:S(2)}, u32[]{:S(2)}) %all-to-all-start.1) | async-done | bytes 1179680 | tf_op jit(solution)/shard_map/all_to_all | solution.py:583
  76.7 6.0 %shard_map.164 = f32[3,128,32]{2,1,0:T(8,128)} custom-call(f32[128,1,2304]{2,1,0:T(1,128)} %all-to-all-done.1.in_ref, bf16[8,256,512]{2,1,0:T(8,128)(2,1)S(1)} %get-tuple-element.52.modes_ref, f32[8,32,512]{2,1,0:T(8,128)S(1)} %get-tuple-element.53.edges_ref, f32[1,128]{1,0:T(1,128)S(1)} %copy-done), custom_call_target="tpu_custom_call" | custom-call | tf_op jit(solution)/shard_map/pallas_call | solution.py:596
  82.7 0.0 collective-permute-done.7.first_b
  82.8 0.0 collective-permute-done.8.last_a
  82.8 0.9 %shard_map.165 = f32[3,128,32]{2,1,0:T(8,128)} custom-call(f32[3,32,128]{2,1,0:T(8,128)S(1)} %get-tuple-element.55.here_ref, f32[3,32,128]{2,1,0:T(8,128)S(1)} %collective-permute-done.5.down_ref, f32[3,32,32]{2,1,0:T(8,128)S(1)} %collective-permute-done.6.first_a, f32[3,32,32]{2,1,0:T(8,128)S(1)} %collective-permute-done.7.first_b, ...), custom_call_target="tpu_custom_call" | custom-call | tf_op jit(solution)/shard_map/pallas_call | solution.py:611
  (11 shorter events, 0.0 us)
Async XLA Ops:
  2.3 14.5 %collective-permute-start.2 = (f32[6,32,128]{2,1,0:T(8,128)S(1)}, f32[6,32,128]{2,1,0:T(8,128)S(1)}, u32[]{:S(2)}, u32[]{:S(2)}) collective-permute-start(f32[6,32,128]{2,1,0:T(8,128)S(1)} %get-tuple-element.36.refs_0_), channel_id=1, source_target_pairs={{0,15},{1,0},{2,1},{3,2},{4,3},{5,4},{6,5},{7,6},{8,7},{9,8},{10,9... | collective-permute-start | bytes 294920 | tf_op jit(solution)/shard_map/ppermute | solution.py:486
  9.4 7.3 %collective-permute-start.3 = (f32[6,32,32]{2,1,0:T(8,128)S(1)}, f32[6,32,32]{2,1,0:T(8,128)S(1)}, u32[]{:S(2)}, u32[]{:S(2)}) collective-permute-start(f32[6,32,32]{2,1,0:T(8,128)S(1)} %get-tuple-element.34), channel_id=1, source_target_pairs={{0,127},{1,112},{2,113},{3,114},{4,115},{5,116},{6,117},{7,118},{8... | collective-permute-start | bytes 73736 | tf_op jit(solution)/shard_map/ppermute | solution.py:486
  10.3 6.4 %collective-permute-start = (f32[6,32,32]{2,1,0:T(8,128)S(1)}, f32[6,32,32]{2,1,0:T(8,128)S(1)}, u32[]{:S(2)}, u32[]{:S(2)}) collective-permute-start(f32[6,32,32]{2,1,0:T(8,128)S(1)} %get-tuple-element.34), channel_id=1, source_target_pairs={{0,112},{1,113},{2,114},{3,115},{4,116},{5,117},{6,118},{7,119},{8... | collective-permute-start | bytes 73736 | tf_op jit(solution)/shard_map/ppermute | solution.py:486
  12.1 4.7 %collective-permute-start.4 = (f32[6,32,32]{2,1,0:T(8,128)S(1)}, f32[6,32,32]{2,1,0:T(8,128)S(1)}, u32[]{:S(2)}, u32[]{:S(2)}) collective-permute-start(f32[6,32,32]{2,1,0:T(8,128)S(1)} %get-tuple-element.35), channel_id=1, source_target_pairs={{0,31},{1,16},{2,17},{3,18},{4,19},{5,20},{6,21},{7,22},{8,23},{9,... | collective-permute-start | bytes 73736 | tf_op jit(solution)/shard_map/ppermute | solution.py:486
  12.1 4.7 %collective-permute-start.1 = (f32[6,32,32]{2,1,0:T(8,128)S(1)}, f32[6,32,32]{2,1,0:T(8,128)S(1)}, u32[]{:S(2)}, u32[]{:S(2)}) collective-permute-start(f32[6,32,32]{2,1,0:T(8,128)S(1)} %get-tuple-element.35), channel_id=1, source_target_pairs={{0,16},{1,17},{2,18},{3,19},{4,20},{5,21},{6,22},{7,23},{8,24},{9,... | collective-permute-start | bytes 73736 | tf_op jit(solution)/shard_map/ppermute | solution.py:486
  16.7 23.1 %all-to-all-start = ((f32[128,1,768]{2,1,0:T(1,128)}), f32[128,1,768]{2,1,0:T(1,128)}, u32[]{:S(2)}, u32[]{:S(2)}) async-start(f32[128,1,768]{2,1,0:T(1,128)} %shard_map.159), calls=%async_computation | async-start | bytes 786432 | tf_op jit(solution)/shard_map/all_to_all | solution.py:546
  46.5 30.2 %copy-start = (f32[1,128]{1,0:T(1,128)S(1)}, f32[1,128]{1,0:T(1,128)}, u32[]{:S(2)}) copy-start(f32[1,128]{1,0:T(1,128)} %constant.43.clone.swap_ref) | copy-start | bytes 1540
  46.5 30.2 %all-to-all-start.1 = ((f32[128,1,2304]{2,1,0:T(1,128)}), f32[128,1,2304]{2,1,0:T(1,128)}, u32[]{:S(2)}, u32[]{:S(2)}) async-start(f32[128,1,2304]{2,1,0:T(1,128)} %shard_map.162), calls=%async_computation.1 | async-start | bytes 2359296 | tf_op jit(solution)/shard_map/all_to_all | solution.py:583
  66.5 16.3 %collective-permute-start.5 = (f32[3,32,128]{2,1,0:T(8,128)S(1)}, f32[3,32,128]{2,1,0:T(8,128)S(1)}, u32[]{:S(2)}, u32[]{:S(2)}) collective-permute-start(f32[3,32,128]{2,1,0:T(8,128)S(1)} %get-tuple-element.56), channel_id=1, source_target_pairs={{0,1},{1,2},{2,3},{3,4},{4,5},{5,6},{6,7},{7,8},{8,9},{9,10},{10,1... | collective-permute-start | bytes 147464 | tf_op jit(solution)/shard_map/ppermute | solution.py:486
  68.0 14.7 %collective-permute-start.6 = (f32[3,32,32]{2,1,0:T(8,128)}, f32[3,32,32]{2,1,0:T(8,128)S(1)}, u32[]{:S(2)}, u32[]{:S(2)}) collective-permute-start(f32[3,32,32]{2,1,0:T(8,128)} %get-tuple-element.57), channel_id=1, source_target_pairs={{0,16},{1,17},{2,18},{3,19},{4,20},{5,21},{6,22},{7,23},{8,24},{9,... | collective-permute-start | bytes 36872 | tf_op jit(solution)/shard_map/ppermute | solution.py:486
  69.7 13.0 %collective-permute-start.7 = (f32[3,32,32]{2,1,0:T(8,128)}, f32[3,32,32]{2,1,0:T(8,128)S(1)}, u32[]{:S(2)}, u32[]{:S(2)}) collective-permute-start(f32[3,32,32]{2,1,0:T(8,128)} %get-tuple-element.58), channel_id=1, source_target_pairs={{0,17},{1,18},{2,19},{3,20},{4,21},{5,22},{6,23},{7,24},{8,25},{9,... | collective-permute-start | bytes 36872 | tf_op jit(solution)/shard_map/ppermute | solution.py:486
  70.9 11.9 %collective-permute-start.8 = (f32[3,32,32]{2,1,0:T(8,128)}, f32[3,32,32]{2,1,0:T(8,128)S(1)}, u32[]{:S(2)}, u32[]{:S(2)}) collective-permute-start(f32[3,32,32]{2,1,0:T(8,128)} %get-tuple-element.59), channel_id=1, source_target_pairs={{0,112},{1,113},{2,114},{3,115},{4,116},{5,117},{6,118},{7,119},{8... | collective-permute-start | bytes 36872 | tf_op jit(solution)/shard_map/ppermute | solution.py:486
  71.6 11.2 %collective-permute-start.9 = (f32[3,32,32]{2,1,0:T(8,128)}, f32[3,32,32]{2,1,0:T(8,128)S(1)}, u32[]{:S(2)}, u32[]{:S(2)}) collective-permute-start(f32[3,32,32]{2,1,0:T(8,128)} %get-tuple-element.60), channel_id=1, source_target_pairs={{0,113},{1,114},{2,115},{3,116},{4,117},{5,118},{6,119},{7,120},{8... | collective-permute-start | bytes 36872 | tf_op jit(solution)/shard_map/ppermute | solution.py:486

commit v6 on v5

--- a/solution.py
+++ b/solution.py
@@ -31,7 +31,6 @@
 FAR = CUT * LENGTH * LENGTH
 SCALES = (LENGTH, LENGTH, LENGTH, 1.0, 1.0 / math.sqrt(8.0 * FAR * LENGTH), 0.5 * LENGTH)
 VMEM = pl.BlockSpec(memory_space=pltpu.VMEM)
-SMEM = pl.BlockSpec(memory_space=pltpu.SMEM)
 ANY = pl.BlockSpec(memory_space=pl.ANY)
 
 
@@ -107,7 +106,8 @@
     kx2 = ((2.0 * np.pi * mx / LX) ** 2).astype(np.float32)[None, :]
     ky2 = ((2.0 * np.pi * my / LY) ** 2).astype(np.float32)[:, None]
     kz = 2.0 * np.pi * mz / LZ
-    plane = np.stack([kz * kz, 4.0 * np.pi * damping(mz, LZ) * norms(mz, LZ)], 1)
+    plane = np.zeros((8, LZ))
+    plane[6:] = kz * kz, 4.0 * np.pi * damping(mz, LZ) * norms(mz, LZ)
     half = LZ // 2
     swap = 2.0 * np.pi * np.arange(half) / LZ
     swap = np.concatenate([-swap, swap]).astype(np.float32)[None, :]
@@ -208,7 +208,8 @@
     incoming[-1].wait()
 
 
-def spread_kernel(rows_ref, tz_ref, spread_out, total, packed, turned, sem):
+def spread_kernel(rows_ref, tz_ref, plane_ref, spread_out, total, packed, turned, sems):
+    (plane,) = started((plane_ref, packed.at[BLOCK - 8 :, :], sems.at[0]))
     total[...] = jnp.zeros_like(total)
 
     def column(col, carry):
@@ -219,12 +220,13 @@
         total[pl.ds(y, 12), pl.ds(x, 16), :] += part.reshape(12, 16, LZ)
         return carry
 
-    lax.fori_loop(0, CX * CY, column, 0, unroll=2)
+    lax.fori_loop(0, CX * CY, column, 0, unroll=4)
     for y in range(BY):
         packed[y * BX : (y + 1) * BX, :] = total[y, :BX, :]
-    packed[BX * BY :, :] = jnp.zeros((BLOCK - BX * BY, LZ), F32)
+    packed[BX * BY : BLOCK - 8, :] = jnp.zeros((BLOCK - 8 - BX * BY, LZ), F32)
+    plane.wait()
     turned[...] = packed[...].T
-    for copy in started((turned, spread_out.at[:, 0, :], sem)):
+    for copy in started((turned, spread_out.at[:, 0, :], sems.at[1])):
         copy.wait()
 
 
@@ -234,29 +236,35 @@
         modes_ref[col] = jnp.concatenate(halves(modes), axis=0)
         return carry
 
-    lax.fori_loop(0, CX * CY, column, 0, unroll=2)
-
-
-def plane_kernel(plane_ref, in_ref, *refs):
+    lax.fori_loop(0, CX * CY, column, 0, unroll=4)
+
+
+def plane_kernel(in_ref, *refs):
     sources, out_ref, held = refs[:6], refs[6], refs[7:13]
     lines, stacked, turned, sems = refs[13:]
     tx, ty, iy, ix, kx2, ky2 = held
     (arrival,) = started((in_ref.at[:, 0, :], lines, sems.at[3]))
     constants = started(*((s, t, sems.at[4 + n]) for n, (s, t) in enumerate(zip(sources, held))))
     arrival.wait()
+    kz2, gain = lines[:1, BLOCK - 2 : BLOCK - 1], lines[:1, BLOCK - 1 :]
     for y in range(BY):
         value = lines[:, y * BX : y * BX + KX]
         for gx in range(DX):
             at = KX * (gx % 2)
             stacked[gx // 2, y * DY : (y + 1) * DY, at : at + KX] = value[gx * DY : (gx + 1) * DY]
     pairs = jnp.concatenate([left_split(stacked[n]) for n in range(DX // 2)], axis=1)
-    for copy in constants:
+    constants[0].wait()
+    lines_y = right_split(dot(pairs, tx[...]))
+    constants[1].wait()
+    modes = dot(ty[...], lines_y)
+    for copy in constants[4:]:
         copy.wait()
-    modes = dot(ty[...], right_split(dot(pairs, tx[...])))
-    k2 = kx2[...] + jnp.concatenate([ky2[...], ky2[...]], axis=1) + plane_ref[0]
+    k2 = kx2[...] + jnp.concatenate([ky2[...], ky2[...]], axis=1) + kz2
     positive = k2 > 0.0
-    modes = jnp.where(positive, modes * (plane_ref[1] / jnp.where(positive, k2, 1.0)), 0.0)
+    modes = jnp.where(positive, modes * (gain / jnp.where(positive, k2, 1.0)), 0.0)
+    constants[2].wait()
     both = dot(iy[...], right_split(modes))
+    constants[3].wait()
     rows = BY * DY
     width = DX * BX
     plain = dot(left_split(both[:rows]), ix[...])
@@ -310,7 +318,7 @@
                 rows_out[d, pl.ds(col * 4 + zg, 1), :] = force[:, 128 * zg : 128 * (zg + 1)]
         return carry
 
-    lax.fori_loop(0, CX * CY, column, 0, unroll=2)
+    lax.fori_loop(0, CX * CY, column, 0, unroll=4)
     for d in range(3):
         value = rows_out[d]
         pieces = [value[:, s * SLOTS : (s + 1) * SLOTS][:, None, :] for s in range(4)]
@@ -440,7 +448,7 @@
             outs[at + 2][d] = total[:, COLUMNS + CELLS : 2 * COLUMNS + CELLS]
 
 
-def pair_forces(blocks, passes, single=0, start=(), unroll=4):
+def pair_forces(blocks, passes, single=0, start=(), unroll=8):
     rows = len(passes) * SLOTS
     pairs = rows * SLOTS * CELLS
     widths = (CELLS, COLUMNS, COLUMNS) * 2 if start else (256, 256)
@@ -529,16 +537,16 @@
     spread = pl.pallas_call(
         spread_kernel,
         out_shape=jax.ShapeDtypeStruct((LZ, 1, BLOCK), F32),
-        in_specs=[VMEM] * 2,
+        in_specs=[VMEM, VMEM, ANY],
         out_specs=ANY,
         scratch_shapes=[
             pltpu.VMEM((BY, 40, LZ), F32),
             pltpu.VMEM((BLOCK, LZ), F32),
             pltpu.VMEM((LZ, BLOCK), F32),
-            pltpu.SemaphoreType.DMA,
+            pltpu.SemaphoreType.DMA((2,)),
         ],
         compiler_params=params(16),
-    )(rows, tz)
+    )(rows, tz, hbm(tab["plane"]))
     spread, after, before, above, above_after, above_before = lax.optimization_barrier(
         (spread, after, before, above, above_after, above_before)
     )
@@ -549,6 +557,36 @@
         [(0, 0, 0), (0, 0, 1)] + [(a, 1 - a, c) for a in (0, 1) for c in (-1, 0, 1)],
         single=1,
     )
+    lines, *sums = lax.optimization_barrier((lines, *sums))
+
+    constants = [hbm(tab[name]) for name in ("tx", "ty", "iy", "ix", "kx2", "ky2")]
+    fields = pl.pallas_call(
+        plane_kernel,
+        out_shape=jax.ShapeDtypeStruct((DX * DY, 1, 3 * BLOCK), F32),
+        in_specs=[ANY] * 7,
+        out_specs=ANY,
+        scratch_shapes=[
+            *(pltpu.VMEM(tab[name].shape, BF16) for name in ("tx", "ty", "iy", "ix")),
+            *(pltpu.VMEM(tab[name].shape, F32) for name in ("kx2", "ky2")),
+            pltpu.VMEM((DX * DY, BLOCK), F32),
+            pltpu.VMEM((DX // 2, BY * DY, 128), F32),
+            pltpu.VMEM((3, DX * DY, BLOCK), F32),
+            pltpu.SemaphoreType.DMA((11,)),
+        ],
+        compiler_params=params(20),
+    )(lines, *constants)
+    fields = lax.all_to_all(hbm(fields), ("gx", "gy"), split_axis=0, concat_axis=0, tiled=True)
+    here, to_before, to_after, up, up_before, up_after = pair_forces(
+        blocks, [(a, 1, c) for a in (-1, 1) for c in (-1, 0, 1)], start=sums
+    )
+    sides = (
+        send(up, 0, 1),
+        send(to_after, 1, 0),
+        send(up_after, 1, 1),
+        send(to_before, -1, 0),
+        send(up_before, -1, 1),
+    )
+
     modes, edges = pl.pallas_call(
         weight_kernel,
         out_shape=(
@@ -560,39 +598,7 @@
         compiler_params=params(8),
         cost_estimate=pl.CostEstimate(flops=1 << 28, bytes_accessed=1 << 20, transcendentals=0),
     )(rows, tz)
-    lines, modes, edges, *sums = lax.optimization_barrier((lines, modes, edges, *sums))
-
-    index = lax.axis_index("gx") * DY + lax.axis_index("gy")
-    plane = lax.dynamic_index_in_dim(jnp.asarray(tab["plane"]), index, 0, keepdims=False)
-    constants = [hbm(tab[name]) for name in ("tx", "ty", "iy", "ix", "kx2", "ky2")]
-    fields = pl.pallas_call(
-        plane_kernel,
-        out_shape=jax.ShapeDtypeStruct((DX * DY, 1, 3 * BLOCK), F32),
-        in_specs=[SMEM] + [ANY] * 7,
-        out_specs=ANY,
-        scratch_shapes=[
-            *(pltpu.VMEM(tab[name].shape, BF16) for name in ("tx", "ty", "iy", "ix")),
-            *(pltpu.VMEM(tab[name].shape, F32) for name in ("kx2", "ky2")),
-            pltpu.VMEM((DX * DY, BLOCK), F32),
-            pltpu.VMEM((DX // 2, BY * DY, 128), F32),
-            pltpu.VMEM((3, DX * DY, BLOCK), F32),
-            pltpu.SemaphoreType.DMA((10,)),
-        ],
-        compiler_params=params(20),
-    )(plane, lines, *constants)
-    fields = lax.all_to_all(hbm(fields), ("gx", "gy"), split_axis=0, concat_axis=0, tiled=True)
-    here, to_before, to_after, up, up_before, up_after = pair_forces(
-        blocks, [(a, 1, c) for a in (-1, 1) for c in (-1, 0, 1)], start=sums
-    )
-    sides = (
-        send(up, 0, 1),
-        send(to_after, 1, 0),
-        send(up_after, 1, 1),
-        send(to_before, -1, 0),
-        send(up_before, -1, 1),
-    )
-
-    fields, here = lax.optimization_barrier((fields, here))
+    fields, here, modes, edges = lax.optimization_barrier((fields, here, modes, edges))
     mesh_force = pl.pallas_call(
         force_kernel,
         out_shape=jax.ShapeDtypeStruct((3, CELLS, SLOTS), F32),

time: 84 us -> 80.5 us (0.958)
  Pallas kernels: 43.1 us -> 39.7 us
  waiting for transfers between devices: 2.92 us -> 4.43 us
  starting transfers between devices: 36.1 us -> 34.6 us
    pallas_call x2, Pallas kernels: 21.8 us -> 20 us  [pair_forces(): pl.pallas_call(functools.partial(pair_kernel, passes=tuple(passes), singl...]
    all_to_all x1, waiting for transfers between devices: 0.01 us -> 1.2 us  [body(): lax.all_to_all(hbm(spread), ('gx', 'gy'), split_axis=0, concat_axis=0, ti...]
    all_to_all x1, starting transfers between devices: 10.2 us -> 8.98 us  [body(): lax.all_to_all(hbm(fields), ('gx', 'gy'), split_axis=0, concat_axis=0, ti...]
  transfers between devices with their start and end apart: 12 -> 12, of which waited for: 1 -> 3; matrix products, arithmetic and copies ran while one was open for 1% -> 0% of each run, Pallas kernels for 41% -> 39%
where the time goes in v6:
time: 80.5 us; the launch traced here: 80.3 us
  Pallas kernels  39.7 us (49%)
  starting transfers between devices  34.6 us (43%)
  waiting for transfers between devices  4.43 us (6%)
    pallas_call x2, Pallas kernels, pair_forces(): pl.pallas_call(functools.partial(pair_kernel, passes=tuple(passes), singl...  20 us
    ppermute x10, starting transfers between devices, send(): return lax.ppermute(value, ('gx', 'gy'), route)  17.2 us
    all_to_all x1, starting transfers between devices, body(): lax.all_to_all(hbm(fields), ('gx', 'gy'), split_axis=0, concat_axis=0, ti...  8.98 us
    all_to_all x1, starting transfers between devices, body(): lax.all_to_all(hbm(spread), ('gx', 'gy'), split_axis=0, concat_axis=0, ti...  8.41 us
    pallas_call x1, Pallas kernels, body(): pl.pallas_call(plane_kernel, out_shape=jax.ShapeDtypeStruct((DX * DY, 1,...  6.2 us
    pallas_call x1, Pallas kernels, body(): pl.pallas_call(force_kernel, out_shape=jax.ShapeDtypeStruct((3, CELLS, SL...  5.7 us
    pallas_call x1, Pallas kernels, body(): pl.pallas_call(spread_kernel, out_shape=jax.ShapeDtypeStruct((LZ, 1, BLOC...  4.16 us
    all_to_all x1, waiting for transfers between devices, body(): lax.all_to_all(hbm(fields), ('gx', 'gy'), split_axis=0, concat_axis=0, ti...  2.75 us
  transfers between devices with their start and end apart: 12, of which 3 were waited for; matrix products, arithmetic and copies ran while one was open for 0% of the time, Pallas kernels for 39%

profile of v6, /device:TPU:1, one launch (start us, length us, event | category | flops | bytes accessed | tf_op | source)
XLA Modules:
  0.0 80.3 jit_solution(13467579596675893195)
XLA Ops:
  0.6 1.6 %shard_map.158 = (f32[6,32,128]{2,1,0:T(8,128)S(1)}, f32[6,32,32]{2,1,0:T(8,128)S(1)}, f32[6,32,32]{2,1,0:T(8,128)S(1)}, f32[4,32,128]{2,1,0:T(8,128)S(1)}, bf16[4,128,144]{2,1,0:T(8,128)(2,1)S(1)}) custom-call(f32[3,128,32]{2,1,0:T(8,128)} %bitcast.16, f32[128,32]{1,0:T(8,128)} %bitcast.18, s32[128,32]{1,0:T(8,128)} %bitcast.19, s32[4,2,16]{2,1,0:T(2,128)} %refs_3_.2, ...), custom_call_target="tpu_custom_call" | custom-call | tf_op jit(solution)/shard_map/pallas_call | solution.py:501
  2.3 7.1 %collective-permute-start.2 = (f32[6,32,128]{2,1,0:T(8,128)S(1)}, f32[6,32,128]{2,1,0:T(8,128)S(1)}, u32[]{:S(2)}, u32[]{:S(2)}) collective-permute-start(f32[6,32,128]{2,1,0:T(8,128)S(1)} %get-tuple-element.36.refs_0_), channel_id=1, source_target_pairs={{0,15},{1,0},{2,1},{3,2},{4,3},{5,4},{6,5},{7,6},{8,7},{9,8},{10,9... | collective-permute-start | bytes 294920 | tf_op jit(solution)/shard_map/ppermute | solution.py:494
  9.4 1.0 %collective-permute-start.3 = (f32[6,32,32]{2,1,0:T(8,128)S(1)}, f32[6,32,32]{2,1,0:T(8,128)S(1)}, u32[]{:S(2)}, u32[]{:S(2)}) collective-permute-start(f32[6,32,32]{2,1,0:T(8,128)S(1)} %get-tuple-element.34), channel_id=1, source_target_pairs={{0,127},{1,112},{2,113},{3,114},{4,115},{5,116},{6,117},{7,118},{8... | collective-permute-start | bytes 73736 | tf_op jit(solution)/shard_map/ppermute | solution.py:494
  10.3 1.7 %collective-permute-start = (f32[6,32,32]{2,1,0:T(8,128)S(1)}, f32[6,32,32]{2,1,0:T(8,128)S(1)}, u32[]{:S(2)}, u32[]{:S(2)}) collective-permute-start(f32[6,32,32]{2,1,0:T(8,128)S(1)} %get-tuple-element.34), channel_id=1, source_target_pairs={{0,112},{1,113},{2,114},{3,115},{4,116},{5,117},{6,118},{7,119},{8... | collective-permute-start | bytes 73736 | tf_op jit(solution)/shard_map/ppermute | solution.py:494
  12.1 0.0 collective-permute-start.4
  12.1 4.2 %shard_map.159 = f32[128,1,768]{2,1,0:T(1,128)} custom-call(f32[4,32,128]{2,1,0:T(8,128)S(1)} %get-tuple-element.32.rows_ref, bf16[4,128,144]{2,1,0:T(8,128)(2,1)S(1)} %get-tuple-element.33.tz_ref, f32[8,128]{1,0:T(8,128)} %constant.19.clone.plane_ref), custom_call_target="tpu_custom_call" | custom-call | tf_op jit(solution)/shard_map/pallas_call | solution.py:537
  16.3 0.5 collective-permute-done.4.refs_4_
  16.7 8.4 %all-to-all-start = ((f32[128,1,768]{2,1,0:T(1,128)}), f32[128,1,768]{2,1,0:T(1,128)S(1)}, u32[]{:S(2)}, u32[]{:S(2)}) async-start(f32[128,1,768]{2,1,0:T(1,128)} %shard_map.159), calls=%async_computation | async-start | bytes 786432 | tf_op jit(solution)/shard_map/all_to_all | solution.py:554
  25.2 11.4 %shard_map.160 = (f32[3,32,256]{2,1,0:T(8,128)S(1)}, f32[3,32,256]{2,1,0:T(8,128)S(1)}) custom-call(f32[6,32,128]{2,1,0:T(8,128)S(1)} %get-tuple-element.36.refs_0_, f32[6,32,32]{2,1,0:T(8,128)S(1)} %collective-permute-done.1.refs_1_, f32[6,32,32]{2,1,0:T(8,128)S(1)} %collective-permute-done.refs_2_, f32[6,32,128]{2,1,0:T(8,128)S(1)} %collective-permute-done.2.refs_3_, ...), custom_call_target="tpu_custom_call" | custom-call | flops 73400320 | bytes 1048576 | tf_op jit(solution)/shard_map/pallas_call | solution.py:455
  36.5 1.2 %all-to-all-done.in_ref = f32[128,1,768]{2,1,0:T(1,128)S(1)} async-done(((f32[128,1,768]{2,1,0:T(1,128)}), f32[128,1,768]{2,1,0:T(1,128)S(1)}, u32[]{:S(2)}, u32[]{:S(2)}) %all-to-all-start) | async-done | bytes 393248 | tf_op jit(solution)/shard_map/all_to_all | solution.py:554
  37.7 0.7 copy-done.1
  38.5 6.2 %shard_map.161 = f32[128,1,2304]{2,1,0:T(1,128)} custom-call(f32[128,1,768]{2,1,0:T(1,128)} %copy-done.1, bf16[1536,256]{1,0:T(8,128)(2,1)} %constant.20.clone.refs_0_, bf16[256,960]{1,0:T(8,128)(2,1)} %constant.21.clone.refs_1_, bf16[640,768]{1,0:T(8,128)(2,1)} %constant.22.clone.refs_2_, bf16[768,576]{1,0:T(8,128)(2,1)} %constant.23.clone.refs_3_, ...), custom_call_target="tpu_custom_call" | custom-call | tf_op jit(solution)/shard_map/pallas_call | solution.py:563
  44.7 9.0 %all-to-all-start.1 = ((f32[128,1,2304]{2,1,0:T(1,128)}), f32[128,1,2304]{2,1,0:T(1,128)}, u32[]{:S(2)}, u32[]{:S(2)}) async-start(f32[128,1,2304]{2,1,0:T(1,128)} %shard_map.161), calls=%async_computation.1 | async-start | bytes 2359296 | tf_op jit(solution)/shard_map/all_to_all | solution.py:578
  53.7 0.0 copy-start
  53.7 8.6 %shard_map.162 = (f32[3,32,128]{2,1,0:T(8,128)S(1)}, f32[3,32,32]{2,1,0:T(8,128)S(1)}, f32[3,32,32]{2,1,0:T(8,128)S(1)}, f32[3,32,128]{2,1,0:T(8,128)S(1)}, f32[...) custom-call(f32[6,32,128]{2,1,0:T(8,128)S(1)} %get-tuple-element.36.refs_0_, ...), custom_call_target="tpu_custom_call" | custom-call | flops 55050240 | bytes 1048576 | tf_op jit(solution)/shard_map/pallas_call | solution.py:455
  62.3 1.6 %collective-permute-start.5 = (f32[3,32,128]{2,1,0:T(8,128)S(1)}, f32[3,32,128]{2,1,0:T(8,128)S(1)}, u32[]{:S(2)}, u32[]{:S(2)}) collective-permute-start(f32[3,32,128]{2,1,0:T(8,128)S(1)} %get-tuple-element.56), channel_id=1, source_target_pairs={{0,1},{1,2},{2,3},{3,4},{4,5},{5,6},{6,7},{7,8},{8,9},{9,10},{10,1... | collective-permute-start | bytes 147464 | tf_op jit(solution)/shard_map/ppermute | solution.py:494
  63.9 1.7 %collective-permute-start.6 = (f32[3,32,32]{2,1,0:T(8,128)S(1)}, f32[3,32,32]{2,1,0:T(8,128)S(1)}, u32[]{:S(2)}, u32[]{:S(2)}) collective-permute-start(f32[3,32,32]{2,1,0:T(8,128)S(1)} %get-tuple-element.57), channel_id=1, source_target_pairs={{0,16},{1,17},{2,18},{3,19},{4,20},{5,21},{6,22},{7,23},{8,24},{9,... | collective-permute-start | bytes 36872 | tf_op jit(solution)/shard_map/ppermute | solution.py:494
  65.6 1.2 %collective-permute-start.7 = (f32[3,32,32]{2,1,0:T(8,128)S(1)}, f32[3,32,32]{2,1,0:T(8,128)S(1)}, u32[]{:S(2)}, u32[]{:S(2)}) collective-permute-start(f32[3,32,32]{2,1,0:T(8,128)S(1)} %get-tuple-element.58), channel_id=1, source_target_pairs={{0,17},{1,18},{2,19},{3,20},{4,21},{5,22},{6,23},{7,24},{8,25},{9,... | collective-permute-start | bytes 36872 | tf_op jit(solution)/shard_map/ppermute | solution.py:494
  66.8 0.7 collective-permute-start.8
  67.5 2.2 %collective-permute-start.9 = (f32[3,32,32]{2,1,0:T(8,128)S(1)}, f32[3,32,32]{2,1,0:T(8,128)S(1)}, u32[]{:S(2)}, u32[]{:S(2)}) collective-permute-start(f32[3,32,32]{2,1,0:T(8,128)S(1)} %get-tuple-element.60), channel_id=1, source_target_pairs={{0,113},{1,114},{2,115},{3,116},{4,117},{5,118},{6,119},{7,120},{8... | collective-permute-start | bytes 36872 | tf_op jit(solution)/shard_map/ppermute | solution.py:494
  69.7 1.2 %shard_map.163 = (bf16[8,256,512]{2,1,0:T(8,128)(2,1)S(1)}, f32[8,32,512]{2,1,0:T(8,128)S(1)}) custom-call(f32[4,32,128]{2,1,0:T(8,128)S(1)} %get-tuple-element.32.rows_ref, bf16[4,128,144]{2,1,0:T(8,128)(2,1)S(1)} %get-tuple-element.33.tz_ref), custom_call_target="tpu_custom_call" | custom-call | flops 268435456 | bytes 1048576 | tf_op jit(solution)/shard_map/pallas_call | solution.py:590
  70.9 2.8 %all-to-all-done.1.in_ref = f32[128,1,2304]{2,1,0:T(1,128)} async-done(((f32[128,1,2304]{2,1,0:T(1,128)}), f32[128,1,2304]{2,1,0:T(1,128)}, u32[]{:S(2)}, u32[]{:S(2)}) %all-to-all-start.1) | async-done | bytes 1179680 | tf_op jit(solution)/shard_map/all_to_all | solution.py:578
  73.6 5.7 %shard_map.164 = f32[3,128,32]{2,1,0:T(8,128)} custom-call(f32[128,1,2304]{2,1,0:T(1,128)} %all-to-all-done.1.in_ref, bf16[8,256,512]{2,1,0:T(8,128)(2,1)S(1)} %get-tuple-element.52.modes_ref, f32[8,32,512]{2,1,0:T(8,128)S(1)} %get-tuple-element.53.edges_ref, f32[1,128]{1,0:T(1,128)S(1)} %copy-done), custom_call_target="tpu_custom_call" | custom-call | tf_op jit(solution)/shard_map/pallas_call | solution.py:602
  79.4 0.9 %shard_map.165 = f32[3,128,32]{2,1,0:T(8,128)} custom-call(f32[3,32,128]{2,1,0:T(8,128)S(1)} %get-tuple-element.55.here_ref, f32[3,32,128]{2,1,0:T(8,128)S(1)} %collective-permute-done.5.down_ref, f32[3,32,32]{2,1,0:T(8,128)S(1)} %collective-permute-done.6.first_a, f32[3,32,32]{2,1,0:T(8,128)S(1)} %collective-permute-done.7.first_b, ...), custom_call_target="tpu_custom_call" | custom-call | tf_op jit(solution)/shard_map/pallas_call | solution.py:617
  (12 shorter events, 0.0 us)
Async XLA Ops:
  2.3 14.5 %collective-permute-start.2 = (f32[6,32,128]{2,1,0:T(8,128)S(1)}, f32[6,32,128]{2,1,0:T(8,128)S(1)}, u32[]{:S(2)}, u32[]{:S(2)}) collective-permute-start(f32[6,32,128]{2,1,0:T(8,128)S(1)} %get-tuple-element.36.refs_0_), channel_id=1, source_target_pairs={{0,15},{1,0},{2,1},{3,2},{4,3},{5,4},{6,5},{7,6},{8,7},{9,8},{10,9... | collective-permute-start | bytes 294920 | tf_op jit(solution)/shard_map/ppermute | solution.py:494
  9.4 6.9 %collective-permute-start.3 = (f32[6,32,32]{2,1,0:T(8,128)S(1)}, f32[6,32,32]{2,1,0:T(8,128)S(1)}, u32[]{:S(2)}, u32[]{:S(2)}) collective-permute-start(f32[6,32,32]{2,1,0:T(8,128)S(1)} %get-tuple-element.34), channel_id=1, source_target_pairs={{0,127},{1,112},{2,113},{3,114},{4,115},{5,116},{6,117},{7,118},{8... | collective-permute-start | bytes 73736 | tf_op jit(solution)/shard_map/ppermute | solution.py:494
  10.3 5.9 %collective-permute-start = (f32[6,32,32]{2,1,0:T(8,128)S(1)}, f32[6,32,32]{2,1,0:T(8,128)S(1)}, u32[]{:S(2)}, u32[]{:S(2)}) collective-permute-start(f32[6,32,32]{2,1,0:T(8,128)S(1)} %get-tuple-element.34), channel_id=1, source_target_pairs={{0,112},{1,113},{2,114},{3,115},{4,116},{5,117},{6,118},{7,119},{8... | collective-permute-start | bytes 73736 | tf_op jit(solution)/shard_map/ppermute | solution.py:494
  12.1 4.7 %collective-permute-start.4 = (f32[6,32,32]{2,1,0:T(8,128)S(1)}, f32[6,32,32]{2,1,0:T(8,128)S(1)}, u32[]{:S(2)}, u32[]{:S(2)}) collective-permute-start(f32[6,32,32]{2,1,0:T(8,128)S(1)} %get-tuple-element.35), channel_id=1, source_target_pairs={{0,31},{1,16},{2,17},{3,18},{4,19},{5,20},{6,21},{7,22},{8,23},{9,... | collective-permute-start | bytes 73736 | tf_op jit(solution)/shard_map/ppermute | solution.py:494
  12.1 4.7 %collective-permute-start.1 = (f32[6,32,32]{2,1,0:T(8,128)S(1)}, f32[6,32,32]{2,1,0:T(8,128)S(1)}, u32[]{:S(2)}, u32[]{:S(2)}) collective-permute-start(f32[6,32,32]{2,1,0:T(8,128)S(1)} %get-tuple-element.35), channel_id=1, source_target_pairs={{0,16},{1,17},{2,18},{3,19},{4,20},{5,21},{6,22},{7,23},{8,24},{9,... | collective-permute-start | bytes 73736 | tf_op jit(solution)/shard_map/ppermute | solution.py:494
  16.7 21.0 %all-to-all-start = ((f32[128,1,768]{2,1,0:T(1,128)}), f32[128,1,768]{2,1,0:T(1,128)S(1)}, u32[]{:S(2)}, u32[]{:S(2)}) async-start(f32[128,1,768]{2,1,0:T(1,128)} %shard_map.159), calls=%async_computation | async-start | bytes 786432 | tf_op jit(solution)/shard_map/all_to_all | solution.py:554
  37.7 0.7 copy-start.1
  44.7 28.9 %all-to-all-start.1 = ((f32[128,1,2304]{2,1,0:T(1,128)}), f32[128,1,2304]{2,1,0:T(1,128)}, u32[]{:S(2)}, u32[]{:S(2)}) async-start(f32[128,1,2304]{2,1,0:T(1,128)} %shard_map.161), calls=%async_computation.1 | async-start | bytes 2359296 | tf_op jit(solution)/shard_map/all_to_all | solution.py:578
  53.7 20.0 %copy-start = (f32[1,128]{1,0:T(1,128)S(1)}, f32[1,128]{1,0:T(1,128)}, u32[]{:S(2)}) copy-start(f32[1,128]{1,0:T(1,128)} %constant.26.clone.swap_ref) | copy-start | bytes 1540
  62.3 17.1 %collective-permute-start.5 = (f32[3,32,128]{2,1,0:T(8,128)S(1)}, f32[3,32,128]{2,1,0:T(8,128)S(1)}, u32[]{:S(2)}, u32[]{:S(2)}) collective-permute-start(f32[3,32,128]{2,1,0:T(8,128)S(1)} %get-tuple-element.56), channel_id=1, source_target_pairs={{0,1},{1,2},{2,3},{3,4},{4,5},{5,6},{6,7},{7,8},{8,9},{9,10},{10,1... | collective-permute-start | bytes 147464 | tf_op jit(solution)/shard_map/ppermute | solution.py:494
  63.9 15.4 %collective-permute-start.6 = (f32[3,32,32]{2,1,0:T(8,128)S(1)}, f32[3,32,32]{2,1,0:T(8,128)S(1)}, u32[]{:S(2)}, u32[]{:S(2)}) collective-permute-start(f32[3,32,32]{2,1,0:T(8,128)S(1)} %get-tuple-element.57), channel_id=1, source_target_pairs={{0,16},{1,17},{2,18},{3,19},{4,20},{5,21},{6,22},{7,23},{8,24},{9,... | collective-permute-start | bytes 36872 | tf_op jit(solution)/shard_map/ppermute | solution.py:494
  65.6 13.7 %collective-permute-start.7 = (f32[3,32,32]{2,1,0:T(8,128)S(1)}, f32[3,32,32]{2,1,0:T(8,128)S(1)}, u32[]{:S(2)}, u32[]{:S(2)}) collective-permute-start(f32[3,32,32]{2,1,0:T(8,128)S(1)} %get-tuple-element.58), channel_id=1, source_target_pairs={{0,17},{1,18},{2,19},{3,20},{4,21},{5,22},{6,23},{7,24},{8,25},{9,... | collective-permute-start | bytes 36872 | tf_op jit(solution)/shard_map/ppermute | solution.py:494
  66.8 12.6 %collective-permute-start.8 = (f32[3,32,32]{2,1,0:T(8,128)S(1)}, f32[3,32,32]{2,1,0:T(8,128)S(1)}, u32[]{:S(2)}, u32[]{:S(2)}) collective-permute-start(f32[3,32,32]{2,1,0:T(8,128)S(1)} %get-tuple-element.59), channel_id=1, source_target_pairs={{0,112},{1,113},{2,114},{3,115},{4,116},{5,117},{6,118},{7,119},{8... | collective-permute-start | bytes 36872 | tf_op jit(solution)/shard_map/ppermute | solution.py:494
  67.5 11.9 %collective-permute-start.9 = (f32[3,32,32]{2,1,0:T(8,128)S(1)}, f32[3,32,32]{2,1,0:T(8,128)S(1)}, u32[]{:S(2)}, u32[]{:S(2)}) collective-permute-start(f32[3,32,32]{2,1,0:T(8,128)S(1)} %get-tuple-element.60), channel_id=1, source_target_pairs={{0,113},{1,114},{2,115},{3,116},{4,117},{5,118},{6,119},{7,120},{8... | collective-permute-start | bytes 36872 | tf_op jit(solution)/shard_map/ppermute | solution.py:494

commit v7 on v6

--- a/solution.py
+++ b/solution.py
@@ -27,6 +27,7 @@
 GROUPS = CELLS // 4
 KZ = 48
 KX = 64
+KY = 384
 LENGTH = math.sqrt(GEWALD * GEWALD * math.log2(math.e))
 FAR = CUT * LENGTH * LENGTH
 SCALES = (LENGTH, LENGTH, LENGTH, 1.0, 1.0 / math.sqrt(8.0 * FAR * LENGTH), 0.5 * LENGTH)
@@ -47,11 +48,6 @@
 def left_parts(array):
     high, low = split(array)
     return np.concatenate([high, high, low], axis=-1)
-
-
-def right_parts(array):
-    high, low = split(array)
-    return np.concatenate([high, low, high], axis=-2)
 
 
 def basis(length):
@@ -103,8 +99,6 @@
     gain_y = damping(my, LY) * norms(my, LY)
     ty = wave(points, my, sy, LY) * gain_y[:, None]
     iy = np.concatenate([wave(points, my, sy, LY).T, wave_slope(points, my, sy, LY).T])
-    kx2 = ((2.0 * np.pi * mx / LX) ** 2).astype(np.float32)[None, :]
-    ky2 = ((2.0 * np.pi * my / LY) ** 2).astype(np.float32)[:, None]
     kz = 2.0 * np.pi * mz / LZ
     plane = np.zeros((8, LZ))
     plane[6:] = kz * kz, 4.0 * np.pi * damping(mz, LZ) * norms(mz, LZ)
@@ -113,12 +107,10 @@
     swap = np.concatenate([-swap, swap]).astype(np.float32)[None, :]
     return dict(
         tz=left_parts(tz),
-        tx=right_parts(tx).reshape(-1, LX),
-        ty=left_parts(ty),
-        iy=left_parts(iy),
-        ix=right_parts(np.concatenate([ix[0], ix[1]], axis=1)),
-        kx2=kx2,
-        ky2=np.broadcast_to(ky2, (LY, 128)).astype(np.float32),
+        tx=np.concatenate(split(tx), axis=1).reshape(-1, LX),
+        ty=np.concatenate(split(np.pad(ty, ((0, 0), (0, KY - BY * DY)))), axis=1),
+        iy=np.concatenate(split(iy), axis=1),
+        ix=np.concatenate(split(np.concatenate([ix[0], ix[1]], axis=1))),
         plane=plane.astype(np.float32),
         swap=swap,
     )
@@ -225,8 +217,12 @@
         packed[y * BX : (y + 1) * BX, :] = total[y, :BX, :]
     packed[BX * BY : BLOCK - 8, :] = jnp.zeros((BLOCK - 8 - BX * BY, LZ), F32)
     plane.wait()
-    turned[...] = packed[...].T
-    for copy in started((turned, spread_out.at[:, 0, :], sems.at[1])):
+    outgoing = []
+    for n in range(BLOCK // 128):
+        part = pl.ds(128 * n, 128)
+        turned[:, part] = packed[part, :].T
+        outgoing += started((turned.at[:, part], spread_out.at[:, 0, part], sems.at[1 + n]))
+    for copy in outgoing:
         copy.wait()
 
 
@@ -240,12 +236,14 @@
 
 
 def plane_kernel(in_ref, *refs):
-    sources, out_ref, held = refs[:6], refs[6], refs[7:13]
-    lines, stacked, turned, sems = refs[13:]
-    tx, ty, iy, ix, kx2, ky2 = held
+    sources, out_ref, held = refs[:4], refs[4], refs[5:9]
+    lines, stacked, turned, sems = refs[9:]
+    tx, ty, iy, ix = held
     (arrival,) = started((in_ref.at[:, 0, :], lines, sems.at[3]))
-    constants = started(*((s, t, sems.at[4 + n]) for n, (s, t) in enumerate(zip(sources, held))))
+    copies = [(s, t, sems.at[4 + n]) for n, (s, t) in enumerate(zip(sources, held))]
+    constants = started(*copies[:2])
     arrival.wait()
+    constants += started(*copies[2:])
     kz2, gain = lines[:1, BLOCK - 2 : BLOCK - 1], lines[:1, BLOCK - 1 :]
     for y in range(BY):
         value = lines[:, y * BX : y * BX + KX]
@@ -254,21 +252,33 @@
             stacked[gx // 2, y * DY : (y + 1) * DY, at : at + KX] = value[gx * DY : (gx + 1) * DY]
     pairs = jnp.concatenate([left_split(stacked[n]) for n in range(DX // 2)], axis=1)
     constants[0].wait()
-    lines_y = right_split(dot(pairs, tx[...]))
+    table = []
+    for n in range(DX // 2):
+        table += [tx[256 * n : 256 * (n + 1)], tx[256 * n : 256 * n + 128]]
+    high, low = halves(dot(pairs, jnp.concatenate(table, axis=0)))
+    empty = jnp.zeros((KY - BY * DY, LX), BF16)
     constants[1].wait()
-    modes = dot(ty[...], lines_y)
-    for copy in constants[4:]:
-        copy.wait()
-    k2 = kx2[...] + jnp.concatenate([ky2[...], ky2[...]], axis=1) + kz2
+    modes = dot(
+        jnp.concatenate([ty[:, :KY], ty[:, :KY], ty[:, KY:]], axis=1),
+        jnp.concatenate([high, empty, low, empty, high, empty], axis=0),
+    )
+    k2 = kz2
+    for axis, length in ((0, LY), (1, LX)):
+        mode = lax.broadcasted_iota(jnp.int32, (LY, LX), axis)
+        mode = jnp.where(mode > length // 2, mode - length // 2, mode).astype(F32)
+        k = mode * (2.0 * math.pi / length)
+        k2 = k2 + k * k
     positive = k2 > 0.0
     modes = jnp.where(positive, modes * (gain / jnp.where(positive, k2, 1.0)), 0.0)
     constants[2].wait()
-    both = dot(iy[...], right_split(modes))
+    table = [iy[:, :LY], iy[:, :LY], iy[:, LY:]]
+    both = dot(jnp.concatenate(table, axis=1), right_split(modes))
     constants[3].wait()
     rows = BY * DY
     width = DX * BX
-    plain = dot(left_split(both[:rows]), ix[...])
-    slope = dot(left_split(both[rows:]), ix[:, :width])
+    table = jnp.concatenate([ix[...], ix[:LX]], axis=0)
+    plain = dot(left_split(both[:rows]), table)
+    slope = dot(left_split(both[rows:]), table[:, :width])
     fields = (plain[:, width:], slope, plain[:, :width])
     outgoing = []
     for d in range(3):
@@ -278,9 +288,14 @@
             for y in range(BY):
                 lane = y * BX
                 turned[d, gx * DY : (gx + 1) * DY, lane : lane + BX] = piece[y * DY : (y + 1) * DY]
-        outgoing += started(
-            (turned.at[d], out_ref.at[:, 0, d * BLOCK : (d + 1) * BLOCK], sems.at[d])
-        )
+            part = pl.ds(gx * DY, DY)
+            outgoing += started(
+                (
+                    turned.at[d, part],
+                    out_ref.at[part, 0, d * BLOCK : (d + 1) * BLOCK],
+                    sems.at[10 + d * DX + gx],
+                )
+            )
     for copy in outgoing:
         copy.wait()
 
@@ -543,7 +558,7 @@
             pltpu.VMEM((BY, 40, LZ), F32),
             pltpu.VMEM((BLOCK, LZ), F32),
             pltpu.VMEM((LZ, BLOCK), F32),
-            pltpu.SemaphoreType.DMA((2,)),
+            pltpu.SemaphoreType.DMA((1 + BLOCK // 128,)),
         ],
         compiler_params=params(16),
     )(rows, tz, hbm(tab["plane"]))
@@ -554,30 +569,29 @@
     lines = lax.all_to_all(hbm(spread), ("gx", "gy"), split_axis=0, concat_axis=0, tiled=True)
     sums = pair_forces(
         blocks,
-        [(0, 0, 0), (0, 0, 1)] + [(a, 1 - a, c) for a in (0, 1) for c in (-1, 0, 1)],
+        [(0, 0, 0), (0, 0, 1), (1, 0, -1), (1, 0, 0), (1, 0, 1), (0, 1, -1), (0, 1, 0)],
         single=1,
     )
     lines, *sums = lax.optimization_barrier((lines, *sums))
 
-    constants = [hbm(tab[name]) for name in ("tx", "ty", "iy", "ix", "kx2", "ky2")]
+    constants = [hbm(tab[name]) for name in ("tx", "ty", "iy", "ix")]
     fields = pl.pallas_call(
         plane_kernel,
         out_shape=jax.ShapeDtypeStruct((DX * DY, 1, 3 * BLOCK), F32),
-        in_specs=[ANY] * 7,
+        in_specs=[ANY] * 5,
         out_specs=ANY,
         scratch_shapes=[
             *(pltpu.VMEM(tab[name].shape, BF16) for name in ("tx", "ty", "iy", "ix")),
-            *(pltpu.VMEM(tab[name].shape, F32) for name in ("kx2", "ky2")),
             pltpu.VMEM((DX * DY, BLOCK), F32),
             pltpu.VMEM((DX // 2, BY * DY, 128), F32),
             pltpu.VMEM((3, DX * DY, BLOCK), F32),
-            pltpu.SemaphoreType.DMA((11,)),
+            pltpu.SemaphoreType.DMA((10 + 3 * DX,)),
         ],
         compiler_params=params(20),
     )(lines, *constants)
     fields = lax.all_to_all(hbm(fields), ("gx", "gy"), split_axis=0, concat_axis=0, tiled=True)
     here, to_before, to_after, up, up_before, up_after = pair_forces(
-        blocks, [(a, 1, c) for a in (-1, 1) for c in (-1, 0, 1)], start=sums
+        blocks, [(0, 1, 1)] + [(a, 1, c) for a in (-1, 1) for c in (-1, 0, 1)], start=sums
     )
     sides = (
         send(up, 0, 1),

time: 80.5 us -> 79.3 us (0.985)
  starting transfers between devices: 34.6 us -> 33.2 us
  Pallas kernels: 39.7 us -> 40.6 us
    all_to_all x1, waiting for transfers between devices: 2.75 us -> 1.06 us  [body(): lax.all_to_all(hbm(fields), ('gx', 'gy'), split_axis=0, concat_axis=0, ti...]
    all_to_all x1, waiting for transfers between devices: 1.2 us -> 2.59 us  [body(): lax.all_to_all(hbm(spread), ('gx', 'gy'), split_axis=0, concat_axis=0, ti...]
    all_to_all x1, starting transfers between devices: 8.98 us -> 7.59 us  [body(): lax.all_to_all(hbm(fields), ('gx', 'gy'), split_axis=0, concat_axis=0, ti...]
  transfers between devices with their start and end apart: 12 -> 12, of which waited for: 3 -> 3; matrix products, arithmetic and copies ran while one was open for 0% -> 0% of each run, Pallas kernels for 39% -> 40%
where the time goes in v7:
time: 79.3 us; the launch traced here: 79.1 us
  Pallas kernels  40.6 us (51%)
  starting transfers between devices  33.2 us (42%)
  waiting for transfers between devices  3.74 us (5%)
    pallas_call x2, Pallas kernels, pair_forces(): pl.pallas_call(functools.partial(pair_kernel, passes=tuple(passes), singl...  20.3 us
    ppermute x10, starting transfers between devices, send(): return lax.ppermute(value, ('gx', 'gy'), route)  17.2 us
    all_to_all x1, starting transfers between devices, body(): lax.all_to_all(hbm(spread), ('gx', 'gy'), split_axis=0, concat_axis=0, ti...  8.41 us
    all_to_all x1, starting transfers between devices, body(): lax.all_to_all(hbm(fields), ('gx', 'gy'), split_axis=0, concat_axis=0, ti...  7.59 us
    pallas_call x1, Pallas kernels, body(): pl.pallas_call(plane_kernel, out_shape=jax.ShapeDtypeStruct((DX * DY, 1,...  6.43 us
    pallas_call x1, Pallas kernels, body(): pl.pallas_call(force_kernel, out_shape=jax.ShapeDtypeStruct((3, CELLS, SL...  5.69 us
    pallas_call x1, Pallas kernels, body(): pl.pallas_call(spread_kernel, out_shape=jax.ShapeDtypeStruct((LZ, 1, BLOC...  4.55 us
    all_to_all x1, waiting for transfers between devices, body(): lax.all_to_all(hbm(spread), ('gx', 'gy'), split_axis=0, concat_axis=0, ti...  2.59 us
  transfers between devices with their start and end apart: 12, of which 3 were waited for; matrix products, arithmetic and copies ran while one was open for 0% of the time, Pallas kernels for 40%

profile of v7, /device:TPU:1, one launch (start us, length us, event | category | flops | bytes accessed | tf_op | source)
XLA Modules:
  0.0 79.1 jit_solution(4723777325864681005)
XLA Ops:
  0.6 1.6 %shard_map.140 = (f32[6,32,128]{2,1,0:T(8,128)S(1)}, f32[6,32,32]{2,1,0:T(8,128)S(1)}, f32[6,32,32]{2,1,0:T(8,128)S(1)}, f32[4,32,128]{2,1,0:T(8,128)S(1)}, bf16[4,128,144]{2,1,0:T(8,128)(2,1)S(1)}) custom-call(f32[3,128,32]{2,1,0:T(8,128)} %bitcast.16, f32[128,32]{1,0:T(8,128)} %bitcast.18, s32[128,32]{1,0:T(8,128)} %bitcast.19, s32[4,2,16]{2,1,0:T(2,128)} %refs_3_.2, ...), custom_call_target="tpu_custom_call" | custom-call | tf_op jit(solution)/shard_map/pallas_call | solution.py:516
  2.3 7.1 %collective-permute-start.2 = (f32[6,32,128]{2,1,0:T(8,128)S(1)}, f32[6,32,128]{2,1,0:T(8,128)S(1)}, u32[]{:S(2)}, u32[]{:S(2)}) collective-permute-start(f32[6,32,128]{2,1,0:T(8,128)S(1)} %get-tuple-element.36.refs_0_), channel_id=1, source_target_pairs={{0,15},{1,0},{2,1},{3,2},{4,3},{5,4},{6,5},{7,6},{8,7},{9,8},{10,9... | collective-permute-start | bytes 294920 | tf_op jit(solution)/shard_map/ppermute | solution.py:509
  9.4 1.0 %collective-permute-start.3 = (f32[6,32,32]{2,1,0:T(8,128)S(1)}, f32[6,32,32]{2,1,0:T(8,128)S(1)}, u32[]{:S(2)}, u32[]{:S(2)}) collective-permute-start(f32[6,32,32]{2,1,0:T(8,128)S(1)} %get-tuple-element.34), channel_id=1, source_target_pairs={{0,127},{1,112},{2,113},{3,114},{4,115},{5,116},{6,117},{7,118},{8... | collective-permute-start | bytes 73736 | tf_op jit(solution)/shard_map/ppermute | solution.py:509
  10.3 1.7 %collective-permute-start = (f32[6,32,32]{2,1,0:T(8,128)S(1)}, f32[6,32,32]{2,1,0:T(8,128)S(1)}, u32[]{:S(2)}, u32[]{:S(2)}) collective-permute-start(f32[6,32,32]{2,1,0:T(8,128)S(1)} %get-tuple-element.34), channel_id=1, source_target_pairs={{0,112},{1,113},{2,114},{3,115},{4,116},{5,117},{6,118},{7,119},{8... | collective-permute-start | bytes 73736 | tf_op jit(solution)/shard_map/ppermute | solution.py:509
  12.1 0.0 collective-permute-start.4
  12.1 4.5 %shard_map.141 = f32[128,1,768]{2,1,0:T(1,128)} custom-call(f32[4,32,128]{2,1,0:T(8,128)S(1)} %get-tuple-element.32.rows_ref, bf16[4,128,144]{2,1,0:T(8,128)(2,1)S(1)} %get-tuple-element.33.tz_ref, f32[8,128]{1,0:T(8,128)} %constant.15.clone.plane_ref), custom_call_target="tpu_custom_call" | custom-call | tf_op jit(solution)/shard_map/pallas_call | solution.py:552
  16.7 0.1 collective-permute-done.4.refs_4_
  16.7 8.4 %all-to-all-start = ((f32[128,1,768]{2,1,0:T(1,128)}), f32[128,1,768]{2,1,0:T(1,128)S(1)}, u32[]{:S(2)}, u32[]{:S(2)}) async-start(f32[128,1,768]{2,1,0:T(1,128)} %shard_map.141), calls=%async_computation | async-start | bytes 786432 | tf_op jit(solution)/shard_map/all_to_all | solution.py:569
  25.2 10.0 %shard_map.142 = (f32[3,32,256]{2,1,0:T(8,128)S(1)}, f32[3,32,256]{2,1,0:T(8,128)S(1)}) custom-call(f32[6,32,128]{2,1,0:T(8,128)S(1)} %get-tuple-element.36.refs_0_, f32[6,32,32]{2,1,0:T(8,128)S(1)} %collective-permute-done.1.refs_1_, f32[6,32,32]{2,1,0:T(8,128)S(1)} %collective-permute-done.refs_2_, f32[6,32,128]{2,1,0:T(8,128)S(1)} %collective-permute-done.2.refs_3_, ...), custom_call_target="tpu_custom_call" | custom-call | flops 64225280 | bytes 1048576 | tf_op jit(solution)/shard_map/pallas_call | solution.py:470
  35.1 2.6 %all-to-all-done.in_ref = f32[128,1,768]{2,1,0:T(1,128)S(1)} async-done(((f32[128,1,768]{2,1,0:T(1,128)}), f32[128,1,768]{2,1,0:T(1,128)S(1)}, u32[]{:S(2)}, u32[]{:S(2)}) %all-to-all-start) | async-done | bytes 393248 | tf_op jit(solution)/shard_map/all_to_all | solution.py:569
  37.7 0.7 copy-done.1
  38.5 6.4 %shard_map.143 = f32[128,1,2304]{2,1,0:T(1,128)} custom-call(f32[128,1,768]{2,1,0:T(1,128)} %copy-done.1, bf16[1024,256]{1,0:T(8,128)(2,1)} %constant.16.clone.refs_0_, bf16[256,768]{1,0:T(8,128)(2,1)} %constant.17.clone.refs_1_, bf16[640,512]{1,0:T(8,128)(2,1)} %constant.18.clone.refs_2_, bf16[512,576]{1,0:T(8,128)(2,1)} %constant.19.clone.refs_3_), custom_call_target="tpu_custom_call" | custom-call | tf_op jit(solution)/shard_map/pallas_call | solution.py:578
  44.9 7.6 %all-to-all-start.1 = ((f32[128,1,2304]{2,1,0:T(1,128)}), f32[128,1,2304]{2,1,0:T(1,128)}, u32[]{:S(2)}, u32[]{:S(2)}) async-start(f32[128,1,2304]{2,1,0:T(1,128)} %shard_map.143), calls=%async_computation.1 | async-start | bytes 2359296 | tf_op jit(solution)/shard_map/all_to_all | solution.py:592
  52.5 0.0 copy-start
  52.5 10.3 %shard_map.144 = (f32[3,32,128]{2,1,0:T(8,128)S(1)}, f32[3,32,32]{2,1,0:T(8,128)S(1)}, f32[3,32,32]{2,1,0:T(8,128)S(1)}, f32[3,32,128]{2,1,0:T(8,128)S(1)}, f32[...) custom-call(f32[6,32,128]{2,1,0:T(8,128)S(1)} %get-tuple-element.36.refs_0_, ...), custom_call_target="tpu_custom_call" | custom-call | flops 64225280 | bytes 1048576 | tf_op jit(solution)/shard_map/pallas_call | solution.py:470
  62.8 1.6 %collective-permute-start.5 = (f32[3,32,128]{2,1,0:T(8,128)S(1)}, f32[3,32,128]{2,1,0:T(8,128)S(1)}, u32[]{:S(2)}, u32[]{:S(2)}) collective-permute-start(f32[3,32,128]{2,1,0:T(8,128)S(1)} %get-tuple-element.56), channel_id=1, source_target_pairs={{0,1},{1,2},{2,3},{3,4},{4,5},{5,6},{6,7},{7,8},{8,9},{9,10},{10,1... | collective-permute-start | bytes 147464 | tf_op jit(solution)/shard_map/ppermute | solution.py:509
  64.4 1.7 %collective-permute-start.6 = (f32[3,32,32]{2,1,0:T(8,128)S(1)}, f32[3,32,32]{2,1,0:T(8,128)S(1)}, u32[]{:S(2)}, u32[]{:S(2)}) collective-permute-start(f32[3,32,32]{2,1,0:T(8,128)S(1)} %get-tuple-element.57), channel_id=1, source_target_pairs={{0,16},{1,17},{2,18},{3,19},{4,20},{5,21},{6,22},{7,23},{8,24},{9,... | collective-permute-start | bytes 36872 | tf_op jit(solution)/shard_map/ppermute | solution.py:509
  66.1 1.2 %collective-permute-start.7 = (f32[3,32,32]{2,1,0:T(8,128)S(1)}, f32[3,32,32]{2,1,0:T(8,128)S(1)}, u32[]{:S(2)}, u32[]{:S(2)}) collective-permute-start(f32[3,32,32]{2,1,0:T(8,128)S(1)} %get-tuple-element.58), channel_id=1, source_target_pairs={{0,17},{1,18},{2,19},{3,20},{4,21},{5,22},{6,23},{7,24},{8,25},{9,... | collective-permute-start | bytes 36872 | tf_op jit(solution)/shard_map/ppermute | solution.py:509
  67.3 0.7 collective-permute-start.8
  68.0 2.2 %collective-permute-start.9 = (f32[3,32,32]{2,1,0:T(8,128)S(1)}, f32[3,32,32]{2,1,0:T(8,128)S(1)}, u32[]{:S(2)}, u32[]{:S(2)}) collective-permute-start(f32[3,32,32]{2,1,0:T(8,128)S(1)} %get-tuple-element.60), channel_id=1, source_target_pairs={{0,113},{1,114},{2,115},{3,116},{4,117},{5,118},{6,119},{7,120},{8... | collective-permute-start | bytes 36872 | tf_op jit(solution)/shard_map/ppermute | solution.py:509
  70.2 1.1 %shard_map.145 = (bf16[8,256,512]{2,1,0:T(8,128)(2,1)S(1)}, f32[8,32,512]{2,1,0:T(8,128)S(1)}) custom-call(f32[4,32,128]{2,1,0:T(8,128)S(1)} %get-tuple-element.32.rows_ref, bf16[4,128,144]{2,1,0:T(8,128)(2,1)S(1)} %get-tuple-element.33.tz_ref), custom_call_target="tpu_custom_call" | custom-call | flops 268435456 | bytes 1048576 | tf_op jit(solution)/shard_map/pallas_call | solution.py:604
  71.4 1.1 %all-to-all-done.1.in_ref = f32[128,1,2304]{2,1,0:T(1,128)} async-done(((f32[128,1,2304]{2,1,0:T(1,128)}), f32[128,1,2304]{2,1,0:T(1,128)}, u32[]{:S(2)}, u32[]{:S(2)}) %all-to-all-start.1) | async-done | bytes 1179680 | tf_op jit(solution)/shard_map/all_to_all | solution.py:592
  72.4 5.7 %shard_map.146 = f32[3,128,32]{2,1,0:T(8,128)} custom-call(f32[128,1,2304]{2,1,0:T(1,128)} %all-to-all-done.1.in_ref, bf16[8,256,512]{2,1,0:T(8,128)(2,1)S(1)} %get-tuple-element.52.modes_ref, f32[8,32,512]{2,1,0:T(8,128)S(1)} %get-tuple-element.53.edges_ref, f32[1,128]{1,0:T(1,128)S(1)} %copy-done), custom_call_target="tpu_custom_call" | custom-call | tf_op jit(solution)/shard_map/pallas_call | solution.py:616
  78.2 0.9 %shard_map.147 = f32[3,128,32]{2,1,0:T(8,128)} custom-call(f32[3,32,128]{2,1,0:T(8,128)S(1)} %get-tuple-element.55.here_ref, f32[3,32,128]{2,1,0:T(8,128)S(1)} %collective-permute-done.5.down_ref, f32[3,32,32]{2,1,0:T(8,128)S(1)} %collective-permute-done.6.first_a, f32[3,32,32]{2,1,0:T(8,128)S(1)} %collective-permute-done.7.first_b, ...), custom_call_target="tpu_custom_call" | custom-call | tf_op jit(solution)/shard_map/pallas_call | solution.py:631
  (12 shorter events, 0.0 us)
Async XLA Ops:
  2.3 14.5 %collective-permute-start.2 = (f32[6,32,128]{2,1,0:T(8,128)S(1)}, f32[6,32,128]{2,1,0:T(8,128)S(1)}, u32[]{:S(2)}, u32[]{:S(2)}) collective-permute-start(f32[6,32,128]{2,1,0:T(8,128)S(1)} %get-tuple-element.36.refs_0_), channel_id=1, source_target_pairs={{0,15},{1,0},{2,1},{3,2},{4,3},{5,4},{6,5},{7,6},{8,7},{9,8},{10,9... | collective-permute-start | bytes 294920 | tf_op jit(solution)/shard_map/ppermute | solution.py:509
  9.4 7.3 %collective-permute-start.3 = (f32[6,32,32]{2,1,0:T(8,128)S(1)}, f32[6,32,32]{2,1,0:T(8,128)S(1)}, u32[]{:S(2)}, u32[]{:S(2)}) collective-permute-start(f32[6,32,32]{2,1,0:T(8,128)S(1)} %get-tuple-element.34), channel_id=1, source_target_pairs={{0,127},{1,112},{2,113},{3,114},{4,115},{5,116},{6,117},{7,118},{8... | collective-permute-start | bytes 73736 | tf_op jit(solution)/shard_map/ppermute | solution.py:509
  10.3 6.3 %collective-permute-start = (f32[6,32,32]{2,1,0:T(8,128)S(1)}, f32[6,32,32]{2,1,0:T(8,128)S(1)}, u32[]{:S(2)}, u32[]{:S(2)}) collective-permute-start(f32[6,32,32]{2,1,0:T(8,128)S(1)} %get-tuple-element.34), channel_id=1, source_target_pairs={{0,112},{1,113},{2,114},{3,115},{4,116},{5,117},{6,118},{7,119},{8... | collective-permute-start | bytes 73736 | tf_op jit(solution)/shard_map/ppermute | solution.py:509
  12.1 4.7 %collective-permute-start.4 = (f32[6,32,32]{2,1,0:T(8,128)S(1)}, f32[6,32,32]{2,1,0:T(8,128)S(1)}, u32[]{:S(2)}, u32[]{:S(2)}) collective-permute-start(f32[6,32,32]{2,1,0:T(8,128)S(1)} %get-tuple-element.35), channel_id=1, source_target_pairs={{0,31},{1,16},{2,17},{3,18},{4,19},{5,20},{6,21},{7,22},{8,23},{9,... | collective-permute-start | bytes 73736 | tf_op jit(solution)/shard_map/ppermute | solution.py:509
  12.1 4.7 %collective-permute-start.1 = (f32[6,32,32]{2,1,0:T(8,128)S(1)}, f32[6,32,32]{2,1,0:T(8,128)S(1)}, u32[]{:S(2)}, u32[]{:S(2)}) collective-permute-start(f32[6,32,32]{2,1,0:T(8,128)S(1)} %get-tuple-element.35), channel_id=1, source_target_pairs={{0,16},{1,17},{2,18},{3,19},{4,20},{5,21},{6,22},{7,23},{8,24},{9,... | collective-permute-start | bytes 73736 | tf_op jit(solution)/shard_map/ppermute | solution.py:509
  16.7 21.0 %all-to-all-start = ((f32[128,1,768]{2,1,0:T(1,128)}), f32[128,1,768]{2,1,0:T(1,128)S(1)}, u32[]{:S(2)}, u32[]{:S(2)}) async-start(f32[128,1,768]{2,1,0:T(1,128)} %shard_map.141), calls=%async_computation | async-start | bytes 786432 | tf_op jit(solution)/shard_map/all_to_all | solution.py:569
  37.7 0.7 copy-start.1
  44.9 27.5 %all-to-all-start.1 = ((f32[128,1,2304]{2,1,0:T(1,128)}), f32[128,1,2304]{2,1,0:T(1,128)}, u32[]{:S(2)}, u32[]{:S(2)}) async-start(f32[128,1,2304]{2,1,0:T(1,128)} %shard_map.143), calls=%async_computation.1 | async-start | bytes 2359296 | tf_op jit(solution)/shard_map/all_to_all | solution.py:592
  52.5 19.9 %copy-start = (f32[1,128]{1,0:T(1,128)S(1)}, f32[1,128]{1,0:T(1,128)}, u32[]{:S(2)}) copy-start(f32[1,128]{1,0:T(1,128)} %constant.20.clone.swap_ref) | copy-start | bytes 1540
  62.8 15.4 %collective-permute-start.5 = (f32[3,32,128]{2,1,0:T(8,128)S(1)}, f32[3,32,128]{2,1,0:T(8,128)S(1)}, u32[]{:S(2)}, u32[]{:S(2)}) collective-permute-start(f32[3,32,128]{2,1,0:T(8,128)S(1)} %get-tuple-element.56), channel_id=1, source_target_pairs={{0,1},{1,2},{2,3},{3,4},{4,5},{5,6},{6,7},{7,8},{8,9},{9,10},{10,1... | collective-permute-start | bytes 147464 | tf_op jit(solution)/shard_map/ppermute | solution.py:509
  64.4 13.7 %collective-permute-start.6 = (f32[3,32,32]{2,1,0:T(8,128)S(1)}, f32[3,32,32]{2,1,0:T(8,128)S(1)}, u32[]{:S(2)}, u32[]{:S(2)}) collective-permute-start(f32[3,32,32]{2,1,0:T(8,128)S(1)} %get-tuple-element.57), channel_id=1, source_target_pairs={{0,16},{1,17},{2,18},{3,19},{4,20},{5,21},{6,22},{7,23},{8,24},{9,... | collective-permute-start | bytes 36872 | tf_op jit(solution)/shard_map/ppermute | solution.py:509
  66.1 12.0 %collective-permute-start.7 = (f32[3,32,32]{2,1,0:T(8,128)S(1)}, f32[3,32,32]{2,1,0:T(8,128)S(1)}, u32[]{:S(2)}, u32[]{:S(2)}) collective-permute-start(f32[3,32,32]{2,1,0:T(8,128)S(1)} %get-tuple-element.58), channel_id=1, source_target_pairs={{0,17},{1,18},{2,19},{3,20},{4,21},{5,22},{6,23},{7,24},{8,25},{9,... | collective-permute-start | bytes 36872 | tf_op jit(solution)/shard_map/ppermute | solution.py:509
  67.3 10.9 %collective-permute-start.8 = (f32[3,32,32]{2,1,0:T(8,128)S(1)}, f32[3,32,32]{2,1,0:T(8,128)S(1)}, u32[]{:S(2)}, u32[]{:S(2)}) collective-permute-start(f32[3,32,32]{2,1,0:T(8,128)S(1)} %get-tuple-element.59), channel_id=1, source_target_pairs={{0,112},{1,113},{2,114},{3,115},{4,116},{5,117},{6,118},{7,119},{8... | collective-permute-start | bytes 36872 | tf_op jit(solution)/shard_map/ppermute | solution.py:509
  68.0 10.2 %collective-permute-start.9 = (f32[3,32,32]{2,1,0:T(8,128)S(1)}, f32[3,32,32]{2,1,0:T(8,128)S(1)}, u32[]{:S(2)}, u32[]{:S(2)}) collective-permute-start(f32[3,32,32]{2,1,0:T(8,128)S(1)} %get-tuple-element.60), channel_id=1, source_target_pairs={{0,113},{1,114},{2,115},{3,116},{4,117},{5,118},{6,119},{7,120},{8... | collective-permute-start | bytes 36872 | tf_op jit(solution)/shard_map/ppermute | solution.py:509

commit v8 on v7

--- a/solution.py
+++ b/solution.py
@@ -212,17 +212,13 @@
         total[pl.ds(y, 12), pl.ds(x, 16), :] += part.reshape(12, 16, LZ)
         return carry
 
-    lax.fori_loop(0, CX * CY, column, 0, unroll=4)
+    lax.fori_loop(0, CX * CY, column, 0, unroll=8)
     for y in range(BY):
         packed[y * BX : (y + 1) * BX, :] = total[y, :BX, :]
     packed[BX * BY : BLOCK - 8, :] = jnp.zeros((BLOCK - 8 - BX * BY, LZ), F32)
     plane.wait()
-    outgoing = []
-    for n in range(BLOCK // 128):
-        part = pl.ds(128 * n, 128)
-        turned[:, part] = packed[part, :].T
-        outgoing += started((turned.at[:, part], spread_out.at[:, 0, part], sems.at[1 + n]))
-    for copy in outgoing:
+    turned[...] = packed[...].T
+    for copy in started((turned, spread_out.at[:, 0, :], sems.at[1])):
         copy.wait()
 
 
@@ -232,7 +228,7 @@
         modes_ref[col] = jnp.concatenate(halves(modes), axis=0)
         return carry
 
-    lax.fori_loop(0, CX * CY, column, 0, unroll=4)
+    lax.fori_loop(0, CX * CY, column, 0, unroll=8)
 
 
 def plane_kernel(in_ref, *refs):
@@ -288,14 +284,9 @@
             for y in range(BY):
                 lane = y * BX
                 turned[d, gx * DY : (gx + 1) * DY, lane : lane + BX] = piece[y * DY : (y + 1) * DY]
-            part = pl.ds(gx * DY, DY)
-            outgoing += started(
-                (
-                    turned.at[d, part],
-                    out_ref.at[part, 0, d * BLOCK : (d + 1) * BLOCK],
-                    sems.at[10 + d * DX + gx],
-                )
-            )
+        outgoing += started(
+            (turned.at[d], out_ref.at[:, 0, d * BLOCK : (d + 1) * BLOCK], sems.at[d])
+        )
     for copy in outgoing:
         copy.wait()
 
@@ -333,7 +324,7 @@
                 rows_out[d, pl.ds(col * 4 + zg, 1), :] = force[:, 128 * zg : 128 * (zg + 1)]
         return carry
 
-    lax.fori_loop(0, CX * CY, column, 0, unroll=4)
+    lax.fori_loop(0, CX * CY, column, 0, unroll=8)
     for d in range(3):
         value = rows_out[d]
         pieces = [value[:, s * SLOTS : (s + 1) * SLOTS][:, None, :] for s in range(4)]
@@ -558,7 +549,7 @@
             pltpu.VMEM((BY, 40, LZ), F32),
             pltpu.VMEM((BLOCK, LZ), F32),
             pltpu.VMEM((LZ, BLOCK), F32),
-            pltpu.SemaphoreType.DMA((1 + BLOCK // 128,)),
+            pltpu.SemaphoreType.DMA((2,)),
         ],
         compiler_params=params(16),
     )(rows, tz, hbm(tab["plane"]))
@@ -585,7 +576,7 @@
             pltpu.VMEM((DX * DY, BLOCK), F32),
             pltpu.VMEM((DX // 2, BY * DY, 128), F32),
             pltpu.VMEM((3, DX * DY, BLOCK), F32),
-            pltpu.SemaphoreType.DMA((10 + 3 * DX,)),
+            pltpu.SemaphoreType.DMA((8,)),
         ],
         compiler_params=params(20),
     )(lines, *constants)

time: 79.3 us -> 78.3 us (0.987)
  Pallas kernels: 40.6 us -> 38.7 us
    pallas_call x1, Pallas kernels: 4.55 us -> 3.7 us  [body(): pl.pallas_call(spread_kernel, out_shape=jax.ShapeDtypeStruct((LZ, 1, BLOC...]
    ppermute x10, waiting for transfers between devices: 0.09 us -> 0.94 us  [send(): return lax.ppermute(value, ('gx', 'gy'), route)]
  transfers between devices with their start and end apart: 12 -> 12, of which waited for: 3 -> 3; matrix products, arithmetic and copies ran while one was open for 0% -> 0% of each run, Pallas kernels for 40% -> 39%
where the time goes in v8:
time: 78.3 us; the launch traced here: 78 us
  Pallas kernels  38.7 us (49%)
  starting transfers between devices  33.2 us (42%)
  waiting for transfers between devices  4.51 us (6%)
    pallas_call x2, Pallas kernels, pair_forces(): pl.pallas_call(functools.partial(pair_kernel, passes=tuple(passes), singl...  20.3 us
    ppermute x10, starting transfers between devices, send(): return lax.ppermute(value, ('gx', 'gy'), route)  17.2 us
    all_to_all x1, starting transfers between devices, body(): lax.all_to_all(hbm(spread), ('gx', 'gy'), split_axis=0, concat_axis=0, ti...  8.41 us
    all_to_all x1, starting transfers between devices, body(): lax.all_to_all(hbm(fields), ('gx', 'gy'), split_axis=0, concat_axis=0, ti...  7.6 us
    pallas_call x1, Pallas kernels, body(): pl.pallas_call(plane_kernel, out_shape=jax.ShapeDtypeStruct((DX * DY, 1,...  6.07 us
    pallas_call x1, Pallas kernels, body(): pl.pallas_call(force_kernel, out_shape=jax.ShapeDtypeStruct((3, CELLS, SL...  4.98 us
    pallas_call x1, Pallas kernels, body(): pl.pallas_call(spread_kernel, out_shape=jax.ShapeDtypeStruct((LZ, 1, BLOC...  3.7 us
    all_to_all x1, waiting for transfers between devices, body(): lax.all_to_all(hbm(spread), ('gx', 'gy'), split_axis=0, concat_axis=0, ti...  2.59 us
  transfers between devices with their start and end apart: 12, of which 3 were waited for; matrix products, arithmetic and copies ran while one was open for 0% of the time, Pallas kernels for 39%

profile of v8, /device:TPU:1, one launch (start us, length us, event | category | flops | bytes accessed | tf_op | source)
XLA Modules:
  0.0 78.0 jit_solution(225795932358554418)
XLA Ops:
  0.6 1.6 %shard_map.140 = (f32[6,32,128]{2,1,0:T(8,128)S(1)}, f32[6,32,32]{2,1,0:T(8,128)S(1)}, f32[6,32,32]{2,1,0:T(8,128)S(1)}, f32[4,32,128]{2,1,0:T(8,128)S(1)}, bf16[4,128,144]{2,1,0:T(8,128)(2,1)S(1)}) custom-call(f32[3,128,32]{2,1,0:T(8,128)} %bitcast.16, f32[128,32]{1,0:T(8,128)} %bitcast.18, s32[128,32]{1,0:T(8,128)} %bitcast.19, s32[4,2,16]{2,1,0:T(2,128)} %refs_3_.2, ...), custom_call_target="tpu_custom_call" | custom-call | tf_op jit(solution)/shard_map/pallas_call | solution.py:507
  2.3 7.1 %collective-permute-start.2 = (f32[6,32,128]{2,1,0:T(8,128)S(1)}, f32[6,32,128]{2,1,0:T(8,128)S(1)}, u32[]{:S(2)}, u32[]{:S(2)}) collective-permute-start(f32[6,32,128]{2,1,0:T(8,128)S(1)} %get-tuple-element.36.refs_0_), channel_id=1, source_target_pairs={{0,15},{1,0},{2,1},{3,2},{4,3},{5,4},{6,5},{7,6},{8,7},{9,8},{10,9... | collective-permute-start | bytes 294920 | tf_op jit(solution)/shard_map/ppermute | solution.py:500
  9.4 1.0 %collective-permute-start.3 = (f32[6,32,32]{2,1,0:T(8,128)S(1)}, f32[6,32,32]{2,1,0:T(8,128)S(1)}, u32[]{:S(2)}, u32[]{:S(2)}) collective-permute-start(f32[6,32,32]{2,1,0:T(8,128)S(1)} %get-tuple-element.34), channel_id=1, source_target_pairs={{0,127},{1,112},{2,113},{3,114},{4,115},{5,116},{6,117},{7,118},{8... | collective-permute-start | bytes 73736 | tf_op jit(solution)/shard_map/ppermute | solution.py:500
  10.3 1.7 %collective-permute-start = (f32[6,32,32]{2,1,0:T(8,128)S(1)}, f32[6,32,32]{2,1,0:T(8,128)S(1)}, u32[]{:S(2)}, u32[]{:S(2)}) collective-permute-start(f32[6,32,32]{2,1,0:T(8,128)S(1)} %get-tuple-element.34), channel_id=1, source_target_pairs={{0,112},{1,113},{2,114},{3,115},{4,116},{5,117},{6,118},{7,119},{8... | collective-permute-start | bytes 73736 | tf_op jit(solution)/shard_map/ppermute | solution.py:500
  12.1 0.0 collective-permute-start.4
  12.1 3.7 %shard_map.141 = f32[128,1,768]{2,1,0:T(1,128)} custom-call(f32[4,32,128]{2,1,0:T(8,128)S(1)} %get-tuple-element.32.rows_ref, bf16[4,128,144]{2,1,0:T(8,128)(2,1)S(1)} %get-tuple-element.33.tz_ref, f32[8,128]{1,0:T(8,128)} %constant.15.clone.plane_ref), custom_call_target="tpu_custom_call" | custom-call | tf_op jit(solution)/shard_map/pallas_call | solution.py:543
  15.8 0.9 %collective-permute-done.4.refs_4_ = f32[6,32,32]{2,1,0:T(8,128)S(1)} collective-permute-done((f32[6,32,32]{2,1,0:T(8,128)S(1)}, f32[6,32,32]{2,1,0:T(8,128)S(1)}, u32[]{:S(2)}, u32[]{:S(2)}) %collective-permute-start.4) | collective-permute-done | bytes 24608 | tf_op jit(solution)/shard_map/ppermute | solution.py:500
  16.7 8.4 %all-to-all-start = ((f32[128,1,768]{2,1,0:T(1,128)}), f32[128,1,768]{2,1,0:T(1,128)S(1)}, u32[]{:S(2)}, u32[]{:S(2)}) async-start(f32[128,1,768]{2,1,0:T(1,128)} %shard_map.141), calls=%async_computation | async-start | bytes 786432 | tf_op jit(solution)/shard_map/all_to_all | solution.py:560
  25.2 10.0 %shard_map.142 = (f32[3,32,256]{2,1,0:T(8,128)S(1)}, f32[3,32,256]{2,1,0:T(8,128)S(1)}) custom-call(f32[6,32,128]{2,1,0:T(8,128)S(1)} %get-tuple-element.36.refs_0_, f32[6,32,32]{2,1,0:T(8,128)S(1)} %collective-permute-done.1.refs_1_, f32[6,32,32]{2,1,0:T(8,128)S(1)} %collective-permute-done.refs_2_, f32[6,32,128]{2,1,0:T(8,128)S(1)} %collective-permute-done.2.refs_3_, ...), custom_call_target="tpu_custom_call" | custom-call | flops 64225280 | bytes 1048576 | tf_op jit(solution)/shard_map/pallas_call | solution.py:461
  35.1 2.6 %all-to-all-done.in_ref = f32[128,1,768]{2,1,0:T(1,128)S(1)} async-done(((f32[128,1,768]{2,1,0:T(1,128)}), f32[128,1,768]{2,1,0:T(1,128)S(1)}, u32[]{:S(2)}, u32[]{:S(2)}) %all-to-all-start) | async-done | bytes 393248 | tf_op jit(solution)/shard_map/all_to_all | solution.py:560
  37.7 0.7 copy-done.1
  38.5 6.1 %shard_map.143 = f32[128,1,2304]{2,1,0:T(1,128)} custom-call(f32[128,1,768]{2,1,0:T(1,128)} %copy-done.1, bf16[1024,256]{1,0:T(8,128)(2,1)} %constant.16.clone.refs_0_, bf16[256,768]{1,0:T(8,128)(2,1)} %constant.17.clone.refs_1_, bf16[640,512]{1,0:T(8,128)(2,1)} %constant.18.clone.refs_2_, bf16[512,576]{1,0:T(8,128)(2,1)} %constant.19.clone.refs_3_), custom_call_target="tpu_custom_call" | custom-call | tf_op jit(solution)/shard_map/pallas_call | solution.py:569
  44.5 7.6 %all-to-all-start.1 = ((f32[128,1,2304]{2,1,0:T(1,128)}), f32[128,1,2304]{2,1,0:T(1,128)}, u32[]{:S(2)}, u32[]{:S(2)}) async-start(f32[128,1,2304]{2,1,0:T(1,128)} %shard_map.143), calls=%async_computation.1 | async-start | bytes 2359296 | tf_op jit(solution)/shard_map/all_to_all | solution.py:583
  52.1 0.0 copy-start
  52.2 10.3 %shard_map.144 = (f32[3,32,128]{2,1,0:T(8,128)S(1)}, f32[3,32,32]{2,1,0:T(8,128)S(1)}, f32[3,32,32]{2,1,0:T(8,128)S(1)}, f32[3,32,128]{2,1,0:T(8,128)S(1)}, f32[...) custom-call(f32[6,32,128]{2,1,0:T(8,128)S(1)} %get-tuple-element.36.refs_0_, ...), custom_call_target="tpu_custom_call" | custom-call | flops 64225280 | bytes 1048576 | tf_op jit(solution)/shard_map/pallas_call | solution.py:461
  62.5 1.6 %collective-permute-start.5 = (f32[3,32,128]{2,1,0:T(8,128)S(1)}, f32[3,32,128]{2,1,0:T(8,128)S(1)}, u32[]{:S(2)}, u32[]{:S(2)}) collective-permute-start(f32[3,32,128]{2,1,0:T(8,128)S(1)} %get-tuple-element.56), channel_id=1, source_target_pairs={{0,1},{1,2},{2,3},{3,4},{4,5},{5,6},{6,7},{7,8},{8,9},{9,10},{10,1... | collective-permute-start | bytes 147464 | tf_op jit(solution)/shard_map/ppermute | solution.py:500
  64.0 1.7 %collective-permute-start.6 = (f32[3,32,32]{2,1,0:T(8,128)S(1)}, f32[3,32,32]{2,1,0:T(8,128)S(1)}, u32[]{:S(2)}, u32[]{:S(2)}) collective-permute-start(f32[3,32,32]{2,1,0:T(8,128)S(1)} %get-tuple-element.57), channel_id=1, source_target_pairs={{0,16},{1,17},{2,18},{3,19},{4,20},{5,21},{6,22},{7,23},{8,24},{9,... | collective-permute-start | bytes 36872 | tf_op jit(solution)/shard_map/ppermute | solution.py:500
  65.8 1.2 %collective-permute-start.7 = (f32[3,32,32]{2,1,0:T(8,128)S(1)}, f32[3,32,32]{2,1,0:T(8,128)S(1)}, u32[]{:S(2)}, u32[]{:S(2)}) collective-permute-start(f32[3,32,32]{2,1,0:T(8,128)S(1)} %get-tuple-element.58), channel_id=1, source_target_pairs={{0,17},{1,18},{2,19},{3,20},{4,21},{5,22},{6,23},{7,24},{8,25},{9,... | collective-permute-start | bytes 36872 | tf_op jit(solution)/shard_map/ppermute | solution.py:500
  66.9 0.7 collective-permute-start.8
  67.6 2.2 %collective-permute-start.9 = (f32[3,32,32]{2,1,0:T(8,128)S(1)}, f32[3,32,32]{2,1,0:T(8,128)S(1)}, u32[]{:S(2)}, u32[]{:S(2)}) collective-permute-start(f32[3,32,32]{2,1,0:T(8,128)S(1)} %get-tuple-element.60), channel_id=1, source_target_pairs={{0,113},{1,114},{2,115},{3,116},{4,117},{5,118},{6,119},{7,120},{8... | collective-permute-start | bytes 36872 | tf_op jit(solution)/shard_map/ppermute | solution.py:500
  69.9 1.2 %shard_map.145 = (bf16[8,256,512]{2,1,0:T(8,128)(2,1)S(1)}, f32[8,32,512]{2,1,0:T(8,128)S(1)}) custom-call(f32[4,32,128]{2,1,0:T(8,128)S(1)} %get-tuple-element.32.rows_ref, bf16[4,128,144]{2,1,0:T(8,128)(2,1)S(1)} %get-tuple-element.33.tz_ref), custom_call_target="tpu_custom_call" | custom-call | flops 268435456 | bytes 1048576 | tf_op jit(solution)/shard_map/pallas_call | solution.py:595
  71.1 1.0 %all-to-all-done.1.in_ref = f32[128,1,2304]{2,1,0:T(1,128)} async-done(((f32[128,1,2304]{2,1,0:T(1,128)}), f32[128,1,2304]{2,1,0:T(1,128)}, u32[]{:S(2)}, u32[]{:S(2)}) %all-to-all-start.1) | async-done | bytes 1179680 | tf_op jit(solution)/shard_map/all_to_all | solution.py:583
  72.1 5.0 %shard_map.146 = f32[3,128,32]{2,1,0:T(8,128)} custom-call(f32[128,1,2304]{2,1,0:T(1,128)} %all-to-all-done.1.in_ref, bf16[8,256,512]{2,1,0:T(8,128)(2,1)S(1)} %get-tuple-element.52.modes_ref, f32[8,32,512]{2,1,0:T(8,128)S(1)} %get-tuple-element.53.edges_ref, f32[1,128]{1,0:T(1,128)S(1)} %copy-done), custom_call_target="tpu_custom_call" | custom-call | tf_op jit(solution)/shard_map/pallas_call | solution.py:607
  77.1 0.9 %shard_map.147 = f32[3,128,32]{2,1,0:T(8,128)} custom-call(f32[3,32,128]{2,1,0:T(8,128)S(1)} %get-tuple-element.55.here_ref, f32[3,32,128]{2,1,0:T(8,128)S(1)} %collective-permute-done.5.down_ref, f32[3,32,32]{2,1,0:T(8,128)S(1)} %collective-permute-done.6.first_a, f32[3,32,32]{2,1,0:T(8,128)S(1)} %collective-permute-done.7.first_b, ...), custom_call_target="tpu_custom_call" | custom-call | tf_op jit(solution)/shard_map/pallas_call | solution.py:622
  (12 shorter events, 0.0 us)
Async XLA Ops:
  2.3 14.5 %collective-permute-start.2 = (f32[6,32,128]{2,1,0:T(8,128)S(1)}, f32[6,32,128]{2,1,0:T(8,128)S(1)}, u32[]{:S(2)}, u32[]{:S(2)}) collective-permute-start(f32[6,32,128]{2,1,0:T(8,128)S(1)} %get-tuple-element.36.refs_0_), channel_id=1, source_target_pairs={{0,15},{1,0},{2,1},{3,2},{4,3},{5,4},{6,5},{7,6},{8,7},{9,8},{10,9... | collective-permute-start | bytes 294920 | tf_op jit(solution)/shard_map/ppermute | solution.py:500
  9.4 6.4 %collective-permute-start.3 = (f32[6,32,32]{2,1,0:T(8,128)S(1)}, f32[6,32,32]{2,1,0:T(8,128)S(1)}, u32[]{:S(2)}, u32[]{:S(2)}) collective-permute-start(f32[6,32,32]{2,1,0:T(8,128)S(1)} %get-tuple-element.34), channel_id=1, source_target_pairs={{0,127},{1,112},{2,113},{3,114},{4,115},{5,116},{6,117},{7,118},{8... | collective-permute-start | bytes 73736 | tf_op jit(solution)/shard_map/ppermute | solution.py:500
  10.3 5.5 %collective-permute-start = (f32[6,32,32]{2,1,0:T(8,128)S(1)}, f32[6,32,32]{2,1,0:T(8,128)S(1)}, u32[]{:S(2)}, u32[]{:S(2)}) collective-permute-start(f32[6,32,32]{2,1,0:T(8,128)S(1)} %get-tuple-element.34), channel_id=1, source_target_pairs={{0,112},{1,113},{2,114},{3,115},{4,116},{5,117},{6,118},{7,119},{8... | collective-permute-start | bytes 73736 | tf_op jit(solution)/shard_map/ppermute | solution.py:500
  12.1 4.7 %collective-permute-start.4 = (f32[6,32,32]{2,1,0:T(8,128)S(1)}, f32[6,32,32]{2,1,0:T(8,128)S(1)}, u32[]{:S(2)}, u32[]{:S(2)}) collective-permute-start(f32[6,32,32]{2,1,0:T(8,128)S(1)} %get-tuple-element.35), channel_id=1, source_target_pairs={{0,31},{1,16},{2,17},{3,18},{4,19},{5,20},{6,21},{7,22},{8,23},{9,... | collective-permute-start | bytes 73736 | tf_op jit(solution)/shard_map/ppermute | solution.py:500
  12.1 4.7 %collective-permute-start.1 = (f32[6,32,32]{2,1,0:T(8,128)S(1)}, f32[6,32,32]{2,1,0:T(8,128)S(1)}, u32[]{:S(2)}, u32[]{:S(2)}) collective-permute-start(f32[6,32,32]{2,1,0:T(8,128)S(1)} %get-tuple-element.35), channel_id=1, source_target_pairs={{0,16},{1,17},{2,18},{3,19},{4,20},{5,21},{6,22},{7,23},{8,24},{9,... | collective-permute-start | bytes 73736 | tf_op jit(solution)/shard_map/ppermute | solution.py:500
  16.7 21.0 %all-to-all-start = ((f32[128,1,768]{2,1,0:T(1,128)}), f32[128,1,768]{2,1,0:T(1,128)S(1)}, u32[]{:S(2)}, u32[]{:S(2)}) async-start(f32[128,1,768]{2,1,0:T(1,128)} %shard_map.141), calls=%async_computation | async-start | bytes 786432 | tf_op jit(solution)/shard_map/all_to_all | solution.py:560
  37.7 0.7 copy-start.1
  44.5 27.5 %all-to-all-start.1 = ((f32[128,1,2304]{2,1,0:T(1,128)}), f32[128,1,2304]{2,1,0:T(1,128)}, u32[]{:S(2)}, u32[]{:S(2)}) async-start(f32[128,1,2304]{2,1,0:T(1,128)} %shard_map.143), calls=%async_computation.1 | async-start | bytes 2359296 | tf_op jit(solution)/shard_map/all_to_all | solution.py:583
  52.1 19.9 %copy-start = (f32[1,128]{1,0:T(1,128)S(1)}, f32[1,128]{1,0:T(1,128)}, u32[]{:S(2)}) copy-start(f32[1,128]{1,0:T(1,128)} %constant.20.clone.swap_ref) | copy-start | bytes 1540
  62.5 14.6 %collective-permute-start.5 = (f32[3,32,128]{2,1,0:T(8,128)S(1)}, f32[3,32,128]{2,1,0:T(8,128)S(1)}, u32[]{:S(2)}, u32[]{:S(2)}) collective-permute-start(f32[3,32,128]{2,1,0:T(8,128)S(1)} %get-tuple-element.56), channel_id=1, source_target_pairs={{0,1},{1,2},{2,3},{3,4},{4,5},{5,6},{6,7},{7,8},{8,9},{9,10},{10,1... | collective-permute-start | bytes 147464 | tf_op jit(solution)/shard_map/ppermute | solution.py:500
  64.0 13.0 %collective-permute-start.6 = (f32[3,32,32]{2,1,0:T(8,128)S(1)}, f32[3,32,32]{2,1,0:T(8,128)S(1)}, u32[]{:S(2)}, u32[]{:S(2)}) collective-permute-start(f32[3,32,32]{2,1,0:T(8,128)S(1)} %get-tuple-element.57), channel_id=1, source_target_pairs={{0,16},{1,17},{2,18},{3,19},{4,20},{5,21},{6,22},{7,23},{8,24},{9,... | collective-permute-start | bytes 36872 | tf_op jit(solution)/shard_map/ppermute | solution.py:500
  65.8 11.3 %collective-permute-start.7 = (f32[3,32,32]{2,1,0:T(8,128)S(1)}, f32[3,32,32]{2,1,0:T(8,128)S(1)}, u32[]{:S(2)}, u32[]{:S(2)}) collective-permute-start(f32[3,32,32]{2,1,0:T(8,128)S(1)} %get-tuple-element.58), channel_id=1, source_target_pairs={{0,17},{1,18},{2,19},{3,20},{4,21},{5,22},{6,23},{7,24},{8,25},{9,... | collective-permute-start | bytes 36872 | tf_op jit(solution)/shard_map/ppermute | solution.py:500
  66.9 10.1 %collective-permute-start.8 = (f32[3,32,32]{2,1,0:T(8,128)S(1)}, f32[3,32,32]{2,1,0:T(8,128)S(1)}, u32[]{:S(2)}, u32[]{:S(2)}) collective-permute-start(f32[3,32,32]{2,1,0:T(8,128)S(1)} %get-tuple-element.59), channel_id=1, source_target_pairs={{0,112},{1,113},{2,114},{3,115},{4,116},{5,117},{6,118},{7,119},{8... | collective-permute-start | bytes 36872 | tf_op jit(solution)/shard_map/ppermute | solution.py:500
  67.6 9.5 %collective-permute-start.9 = (f32[3,32,32]{2,1,0:T(8,128)S(1)}, f32[3,32,32]{2,1,0:T(8,128)S(1)}, u32[]{:S(2)}, u32[]{:S(2)}) collective-permute-start(f32[3,32,32]{2,1,0:T(8,128)S(1)} %get-tuple-element.60), channel_id=1, source_target_pairs={{0,113},{1,114},{2,115},{3,116},{4,117},{5,118},{6,119},{7,120},{8... | collective-permute-start | bytes 36872 | tf_op jit(solution)/shard_map/ppermute | solution.py:500

commit v9 on v8

--- a/solution.py
+++ b/solution.py
@@ -454,7 +454,7 @@
             outs[at + 2][d] = total[:, COLUMNS + CELLS : 2 * COLUMNS + CELLS]
 
 
-def pair_forces(blocks, passes, single=0, start=(), unroll=8):
+def pair_forces(blocks, passes, single=0, start=(), unroll=16):
     rows = len(passes) * SLOTS
     pairs = rows * SLOTS * CELLS
     widths = (CELLS, COLUMNS, COLUMNS) * 2 if start else (256, 256)

time: 78.3 us -> 78.2 us (level)
  transfers between devices with their start and end apart: 12 -> 12, of which waited for: 3 -> 3; matrix products, arithmetic and copies ran while one was open for 0% -> 0% of each run, Pallas kernels for 39% -> 38%
where the time goes in v9:
time: 78.2 us; the launch traced here: 77.9 us
  Pallas kernels  38.2 us (49%)
  starting transfers between devices  33 us (42%)
  waiting for transfers between devices  5.21 us (7%)
    pallas_call x2, Pallas kernels, pair_forces(): pl.pallas_call(functools.partial(pair_kernel, passes=tuple(passes), singl...  19.7 us
    ppermute x10, starting transfers between devices, send(): return lax.ppermute(value, ('gx', 'gy'), route)  17.2 us
    all_to_all x1, starting transfers between devices, body(): lax.all_to_all(hbm(spread), ('gx', 'gy'), split_axis=0, concat_axis=0, ti...  8.41 us
    all_to_all x1, starting transfers between devices, body(): lax.all_to_all(hbm(fields), ('gx', 'gy'), split_axis=0, concat_axis=0, ti...  7.34 us
    pallas_call x1, Pallas kernels, body(): pl.pallas_call(plane_kernel, out_shape=jax.ShapeDtypeStruct((DX * DY, 1,...  6.07 us
    pallas_call x1, Pallas kernels, body(): pl.pallas_call(force_kernel, out_shape=jax.ShapeDtypeStruct((3, CELLS, SL...  4.98 us
    pallas_call x1, Pallas kernels, body(): pl.pallas_call(spread_kernel, out_shape=jax.ShapeDtypeStruct((LZ, 1, BLOC...  3.7 us
    all_to_all x1, waiting for transfers between devices, body(): lax.all_to_all(hbm(spread), ('gx', 'gy'), split_axis=0, concat_axis=0, ti...  2.85 us
  transfers between devices with their start and end apart: 12, of which 3 were waited for; matrix products, arithmetic and copies ran while one was open for 0% of the time, Pallas kernels for 38%

profile of v9, /device:TPU:1, one launch (start us, length us, event | category | flops | bytes accessed | tf_op | source)
XLA Modules:
  0.0 77.9 jit_solution(1497416938904464135)
XLA Ops:
  0.6 1.6 %shard_map.140 = (f32[6,32,128]{2,1,0:T(8,128)S(1)}, f32[6,32,32]{2,1,0:T(8,128)S(1)}, f32[6,32,32]{2,1,0:T(8,128)S(1)}, f32[4,32,128]{2,1,0:T(8,128)S(1)}, bf16[4,128,144]{2,1,0:T(8,128)(2,1)S(1)}) custom-call(f32[3,128,32]{2,1,0:T(8,128)} %bitcast.16, f32[128,32]{1,0:T(8,128)} %bitcast.18, s32[128,32]{1,0:T(8,128)} %bitcast.19, s32[4,2,16]{2,1,0:T(2,128)} %refs_3_.2, ...), custom_call_target="tpu_custom_call" | custom-call | tf_op jit(solution)/shard_map/pallas_call | solution.py:507
  2.3 7.1 %collective-permute-start.2 = (f32[6,32,128]{2,1,0:T(8,128)S(1)}, f32[6,32,128]{2,1,0:T(8,128)S(1)}, u32[]{:S(2)}, u32[]{:S(2)}) collective-permute-start(f32[6,32,128]{2,1,0:T(8,128)S(1)} %get-tuple-element.36.refs_0_), channel_id=1, source_target_pairs={{0,15},{1,0},{2,1},{3,2},{4,3},{5,4},{6,5},{7,6},{8,7},{9,8},{10,9... | collective-permute-start | bytes 294920 | tf_op jit(solution)/shard_map/ppermute | solution.py:500
  9.4 1.0 %collective-permute-start.3 = (f32[6,32,32]{2,1,0:T(8,128)S(1)}, f32[6,32,32]{2,1,0:T(8,128)S(1)}, u32[]{:S(2)}, u32[]{:S(2)}) collective-permute-start(f32[6,32,32]{2,1,0:T(8,128)S(1)} %get-tuple-element.34), channel_id=1, source_target_pairs={{0,127},{1,112},{2,113},{3,114},{4,115},{5,116},{6,117},{7,118},{8... | collective-permute-start | bytes 73736 | tf_op jit(solution)/shard_map/ppermute | solution.py:500
  10.3 1.7 %collective-permute-start = (f32[6,32,32]{2,1,0:T(8,128)S(1)}, f32[6,32,32]{2,1,0:T(8,128)S(1)}, u32[]{:S(2)}, u32[]{:S(2)}) collective-permute-start(f32[6,32,32]{2,1,0:T(8,128)S(1)} %get-tuple-element.34), channel_id=1, source_target_pairs={{0,112},{1,113},{2,114},{3,115},{4,116},{5,117},{6,118},{7,119},{8... | collective-permute-start | bytes 73736 | tf_op jit(solution)/shard_map/ppermute | solution.py:500
  12.1 3.7 %shard_map.141 = f32[128,1,768]{2,1,0:T(1,128)} custom-call(f32[4,32,128]{2,1,0:T(8,128)S(1)} %get-tuple-element.32.rows_ref, bf16[4,128,144]{2,1,0:T(8,128)(2,1)S(1)} %get-tuple-element.33.tz_ref, f32[8,128]{1,0:T(8,128)} %constant.15.clone.plane_ref), custom_call_target="tpu_custom_call" | custom-call | tf_op jit(solution)/shard_map/pallas_call | solution.py:543
  15.8 0.0 collective-permute-done.refs_2_
  15.8 0.9 %collective-permute-done.4.refs_4_ = f32[6,32,32]{2,1,0:T(8,128)S(1)} collective-permute-done((f32[6,32,32]{2,1,0:T(8,128)S(1)}, f32[6,32,32]{2,1,0:T(8,128)S(1)}, u32[]{:S(2)}, u32[]{:S(2)}) %collective-permute-start.4) | collective-permute-done | bytes 24608 | tf_op jit(solution)/shard_map/ppermute | solution.py:500
  16.7 8.4 %all-to-all-start = ((f32[128,1,768]{2,1,0:T(1,128)}), f32[128,1,768]{2,1,0:T(1,128)S(1)}, u32[]{:S(2)}, u32[]{:S(2)}) async-start(f32[128,1,768]{2,1,0:T(1,128)} %shard_map.141), calls=%async_computation | async-start | bytes 786432 | tf_op jit(solution)/shard_map/all_to_all | solution.py:560
  25.2 9.7 %shard_map.142 = (f32[3,32,256]{2,1,0:T(8,128)S(1)}, f32[3,32,256]{2,1,0:T(8,128)S(1)}) custom-call(f32[6,32,128]{2,1,0:T(8,128)S(1)} %get-tuple-element.36.refs_0_, f32[6,32,32]{2,1,0:T(8,128)S(1)} %collective-permute-done.1.refs_1_, f32[6,32,32]{2,1,0:T(8,128)S(1)} %collective-permute-done.refs_2_, f32[6,32,128]{2,1,0:T(8,128)S(1)} %collective-permute-done.2.refs_3_, ...), custom_call_target="tpu_custom_call" | custom-call | flops 64225280 | bytes 1048576 | tf_op jit(solution)/shard_map/pallas_call | solution.py:461
  34.9 2.8 %all-to-all-done.in_ref = f32[128,1,768]{2,1,0:T(1,128)S(1)} async-done(((f32[128,1,768]{2,1,0:T(1,128)}), f32[128,1,768]{2,1,0:T(1,128)S(1)}, u32[]{:S(2)}, u32[]{:S(2)}) %all-to-all-start) | async-done | bytes 393248 | tf_op jit(solution)/shard_map/all_to_all | solution.py:560
  37.7 0.7 copy-done.1
  38.5 6.1 %shard_map.143 = f32[128,1,2304]{2,1,0:T(1,128)} custom-call(f32[128,1,768]{2,1,0:T(1,128)} %copy-done.1, bf16[1024,256]{1,0:T(8,128)(2,1)} %constant.16.clone.refs_0_, bf16[256,768]{1,0:T(8,128)(2,1)} %constant.17.clone.refs_1_, bf16[640,512]{1,0:T(8,128)(2,1)} %constant.18.clone.refs_2_, bf16[512,576]{1,0:T(8,128)(2,1)} %constant.19.clone.refs_3_), custom_call_target="tpu_custom_call" | custom-call | tf_op jit(solution)/shard_map/pallas_call | solution.py:569
  44.5 7.3 %all-to-all-start.1 = ((f32[128,1,2304]{2,1,0:T(1,128)}), f32[128,1,2304]{2,1,0:T(1,128)}, u32[]{:S(2)}, u32[]{:S(2)}) async-start(f32[128,1,2304]{2,1,0:T(1,128)} %shard_map.143), calls=%async_computation.1 | async-start | bytes 2359296 | tf_op jit(solution)/shard_map/all_to_all | solution.py:583
  51.9 0.0 copy-start
  51.9 10.0 %shard_map.144 = (f32[3,32,128]{2,1,0:T(8,128)S(1)}, f32[3,32,32]{2,1,0:T(8,128)S(1)}, f32[3,32,32]{2,1,0:T(8,128)S(1)}, f32[3,32,128]{2,1,0:T(8,128)S(1)}, f32[...) custom-call(f32[6,32,128]{2,1,0:T(8,128)S(1)} %get-tuple-element.36.refs_0_, ...), custom_call_target="tpu_custom_call" | custom-call | flops 64225280 | bytes 1048576 | tf_op jit(solution)/shard_map/pallas_call | solution.py:461
  61.9 1.6 %collective-permute-start.5 = (f32[3,32,128]{2,1,0:T(8,128)S(1)}, f32[3,32,128]{2,1,0:T(8,128)S(1)}, u32[]{:S(2)}, u32[]{:S(2)}) collective-permute-start(f32[3,32,128]{2,1,0:T(8,128)S(1)} %get-tuple-element.56), channel_id=1, source_target_pairs={{0,1},{1,2},{2,3},{3,4},{4,5},{5,6},{6,7},{7,8},{8,9},{9,10},{10,1... | collective-permute-start | bytes 147464 | tf_op jit(solution)/shard_map/ppermute | solution.py:500
  63.5 1.7 %collective-permute-start.6 = (f32[3,32,32]{2,1,0:T(8,128)S(1)}, f32[3,32,32]{2,1,0:T(8,128)S(1)}, u32[]{:S(2)}, u32[]{:S(2)}) collective-permute-start(f32[3,32,32]{2,1,0:T(8,128)S(1)} %get-tuple-element.57), channel_id=1, source_target_pairs={{0,16},{1,17},{2,18},{3,19},{4,20},{5,21},{6,22},{7,23},{8,24},{9,... | collective-permute-start | bytes 36872 | tf_op jit(solution)/shard_map/ppermute | solution.py:500
  65.2 1.2 %collective-permute-start.7 = (f32[3,32,32]{2,1,0:T(8,128)S(1)}, f32[3,32,32]{2,1,0:T(8,128)S(1)}, u32[]{:S(2)}, u32[]{:S(2)}) collective-permute-start(f32[3,32,32]{2,1,0:T(8,128)S(1)} %get-tuple-element.58), channel_id=1, source_target_pairs={{0,17},{1,18},{2,19},{3,20},{4,21},{5,22},{6,23},{7,24},{8,25},{9,... | collective-permute-start | bytes 36872 | tf_op jit(solution)/shard_map/ppermute | solution.py:500
  66.4 0.7 collective-permute-start.8
  67.1 2.2 %collective-permute-start.9 = (f32[3,32,32]{2,1,0:T(8,128)S(1)}, f32[3,32,32]{2,1,0:T(8,128)S(1)}, u32[]{:S(2)}, u32[]{:S(2)}) collective-permute-start(f32[3,32,32]{2,1,0:T(8,128)S(1)} %get-tuple-element.60), channel_id=1, source_target_pairs={{0,113},{1,114},{2,115},{3,116},{4,117},{5,118},{6,119},{7,120},{8... | collective-permute-start | bytes 36872 | tf_op jit(solution)/shard_map/ppermute | solution.py:500
  69.3 1.2 %shard_map.145 = (bf16[8,256,512]{2,1,0:T(8,128)(2,1)S(1)}, f32[8,32,512]{2,1,0:T(8,128)S(1)}) custom-call(f32[4,32,128]{2,1,0:T(8,128)S(1)} %get-tuple-element.32.rows_ref, bf16[4,128,144]{2,1,0:T(8,128)(2,1)S(1)} %get-tuple-element.33.tz_ref), custom_call_target="tpu_custom_call" | custom-call | flops 268435456 | bytes 1048576 | tf_op jit(solution)/shard_map/pallas_call | solution.py:595
  70.5 1.4 %all-to-all-done.1.in_ref = f32[128,1,2304]{2,1,0:T(1,128)} async-done(((f32[128,1,2304]{2,1,0:T(1,128)}), f32[128,1,2304]{2,1,0:T(1,128)}, u32[]{:S(2)}, u32[]{:S(2)}) %all-to-all-start.1) | async-done | bytes 1179680 | tf_op jit(solution)/shard_map/all_to_all | solution.py:583
  72.0 5.0 %shard_map.146 = f32[3,128,32]{2,1,0:T(8,128)} custom-call(f32[128,1,2304]{2,1,0:T(1,128)} %all-to-all-done.1.in_ref, bf16[8,256,512]{2,1,0:T(8,128)(2,1)S(1)} %get-tuple-element.52.modes_ref, f32[8,32,512]{2,1,0:T(8,128)S(1)} %get-tuple-element.53.edges_ref, f32[1,128]{1,0:T(1,128)S(1)} %copy-done), custom_call_target="tpu_custom_call" | custom-call | tf_op jit(solution)/shard_map/pallas_call | solution.py:607
  77.0 0.9 %shard_map.147 = f32[3,128,32]{2,1,0:T(8,128)} custom-call(f32[3,32,128]{2,1,0:T(8,128)S(1)} %get-tuple-element.55.here_ref, f32[3,32,128]{2,1,0:T(8,128)S(1)} %collective-permute-done.5.down_ref, f32[3,32,32]{2,1,0:T(8,128)S(1)} %collective-permute-done.6.first_a, f32[3,32,32]{2,1,0:T(8,128)S(1)} %collective-permute-done.7.first_b, ...), custom_call_target="tpu_custom_call" | custom-call | tf_op jit(solution)/shard_map/pallas_call | solution.py:622
  (12 shorter events, 0.0 us)
Async XLA Ops:
  2.3 14.5 %collective-permute-start.2 = (f32[6,32,128]{2,1,0:T(8,128)S(1)}, f32[6,32,128]{2,1,0:T(8,128)S(1)}, u32[]{:S(2)}, u32[]{:S(2)}) collective-permute-start(f32[6,32,128]{2,1,0:T(8,128)S(1)} %get-tuple-element.36.refs_0_), channel_id=1, source_target_pairs={{0,15},{1,0},{2,1},{3,2},{4,3},{5,4},{6,5},{7,6},{8,7},{9,8},{10,9... | collective-permute-start | bytes 294920 | tf_op jit(solution)/shard_map/ppermute | solution.py:500
  9.4 6.4 %collective-permute-start.3 = (f32[6,32,32]{2,1,0:T(8,128)S(1)}, f32[6,32,32]{2,1,0:T(8,128)S(1)}, u32[]{:S(2)}, u32[]{:S(2)}) collective-permute-start(f32[6,32,32]{2,1,0:T(8,128)S(1)} %get-tuple-element.34), channel_id=1, source_target_pairs={{0,127},{1,112},{2,113},{3,114},{4,115},{5,116},{6,117},{7,118},{8... | collective-permute-start | bytes 73736 | tf_op jit(solution)/shard_map/ppermute | solution.py:500
  10.3 5.5 %collective-permute-start = (f32[6,32,32]{2,1,0:T(8,128)S(1)}, f32[6,32,32]{2,1,0:T(8,128)S(1)}, u32[]{:S(2)}, u32[]{:S(2)}) collective-permute-start(f32[6,32,32]{2,1,0:T(8,128)S(1)} %get-tuple-element.34), channel_id=1, source_target_pairs={{0,112},{1,113},{2,114},{3,115},{4,116},{5,117},{6,118},{7,119},{8... | collective-permute-start | bytes 73736 | tf_op jit(solution)/shard_map/ppermute | solution.py:500
  12.1 4.7 %collective-permute-start.4 = (f32[6,32,32]{2,1,0:T(8,128)S(1)}, f32[6,32,32]{2,1,0:T(8,128)S(1)}, u32[]{:S(2)}, u32[]{:S(2)}) collective-permute-start(f32[6,32,32]{2,1,0:T(8,128)S(1)} %get-tuple-element.35), channel_id=1, source_target_pairs={{0,31},{1,16},{2,17},{3,18},{4,19},{5,20},{6,21},{7,22},{8,23},{9,... | collective-permute-start | bytes 73736 | tf_op jit(solution)/shard_map/ppermute | solution.py:500
  12.1 4.7 %collective-permute-start.1 = (f32[6,32,32]{2,1,0:T(8,128)S(1)}, f32[6,32,32]{2,1,0:T(8,128)S(1)}, u32[]{:S(2)}, u32[]{:S(2)}) collective-permute-start(f32[6,32,32]{2,1,0:T(8,128)S(1)} %get-tuple-element.35), channel_id=1, source_target_pairs={{0,16},{1,17},{2,18},{3,19},{4,20},{5,21},{6,22},{7,23},{8,24},{9,... | collective-permute-start | bytes 73736 | tf_op jit(solution)/shard_map/ppermute | solution.py:500
  16.7 21.0 %all-to-all-start = ((f32[128,1,768]{2,1,0:T(1,128)}), f32[128,1,768]{2,1,0:T(1,128)S(1)}, u32[]{:S(2)}, u32[]{:S(2)}) async-start(f32[128,1,768]{2,1,0:T(1,128)} %shard_map.141), calls=%async_computation | async-start | bytes 786432 | tf_op jit(solution)/shard_map/all_to_all | solution.py:560
  37.7 0.7 copy-start.1
  44.5 27.4 %all-to-all-start.1 = ((f32[128,1,2304]{2,1,0:T(1,128)}), f32[128,1,2304]{2,1,0:T(1,128)}, u32[]{:S(2)}, u32[]{:S(2)}) async-start(f32[128,1,2304]{2,1,0:T(1,128)} %shard_map.143), calls=%async_computation.1 | async-start | bytes 2359296 | tf_op jit(solution)/shard_map/all_to_all | solution.py:583
  51.9 20.1 %copy-start = (f32[1,128]{1,0:T(1,128)S(1)}, f32[1,128]{1,0:T(1,128)}, u32[]{:S(2)}) copy-start(f32[1,128]{1,0:T(1,128)} %constant.20.clone.swap_ref) | copy-start | bytes 1540
  61.9 15.1 %collective-permute-start.5 = (f32[3,32,128]{2,1,0:T(8,128)S(1)}, f32[3,32,128]{2,1,0:T(8,128)S(1)}, u32[]{:S(2)}, u32[]{:S(2)}) collective-permute-start(f32[3,32,128]{2,1,0:T(8,128)S(1)} %get-tuple-element.56), channel_id=1, source_target_pairs={{0,1},{1,2},{2,3},{3,4},{4,5},{5,6},{6,7},{7,8},{8,9},{9,10},{10,1... | collective-permute-start | bytes 147464 | tf_op jit(solution)/shard_map/ppermute | solution.py:500
  63.5 13.5 %collective-permute-start.6 = (f32[3,32,32]{2,1,0:T(8,128)S(1)}, f32[3,32,32]{2,1,0:T(8,128)S(1)}, u32[]{:S(2)}, u32[]{:S(2)}) collective-permute-start(f32[3,32,32]{2,1,0:T(8,128)S(1)} %get-tuple-element.57), channel_id=1, source_target_pairs={{0,16},{1,17},{2,18},{3,19},{4,20},{5,21},{6,22},{7,23},{8,24},{9,... | collective-permute-start | bytes 36872 | tf_op jit(solution)/shard_map/ppermute | solution.py:500
  65.2 11.7 %collective-permute-start.7 = (f32[3,32,32]{2,1,0:T(8,128)S(1)}, f32[3,32,32]{2,1,0:T(8,128)S(1)}, u32[]{:S(2)}, u32[]{:S(2)}) collective-permute-start(f32[3,32,32]{2,1,0:T(8,128)S(1)} %get-tuple-element.58), channel_id=1, source_target_pairs={{0,17},{1,18},{2,19},{3,20},{4,21},{5,22},{6,23},{7,24},{8,25},{9,... | collective-permute-start | bytes 36872 | tf_op jit(solution)/shard_map/ppermute | solution.py:500
  66.4 10.6 %collective-permute-start.8 = (f32[3,32,32]{2,1,0:T(8,128)S(1)}, f32[3,32,32]{2,1,0:T(8,128)S(1)}, u32[]{:S(2)}, u32[]{:S(2)}) collective-permute-start(f32[3,32,32]{2,1,0:T(8,128)S(1)} %get-tuple-element.59), channel_id=1, source_target_pairs={{0,112},{1,113},{2,114},{3,115},{4,116},{5,117},{6,118},{7,119},{8... | collective-permute-start | bytes 36872 | tf_op jit(solution)/shard_map/ppermute | solution.py:500
  67.1 9.9 %collective-permute-start.9 = (f32[3,32,32]{2,1,0:T(8,128)S(1)}, f32[3,32,32]{2,1,0:T(8,128)S(1)}, u32[]{:S(2)}, u32[]{:S(2)}) collective-permute-start(f32[3,32,32]{2,1,0:T(8,128)S(1)} %get-tuple-element.60), channel_id=1, source_target_pairs={{0,113},{1,114},{2,115},{3,116},{4,117},{5,118},{6,119},{7,120},{8... | collective-permute-start | bytes 36872 | tf_op jit(solution)/shard_map/ppermute | solution.py:500

commit v10 on v9

--- a/solution.py
+++ b/solution.py
@@ -563,7 +563,18 @@
         [(0, 0, 0), (0, 0, 1), (1, 0, -1), (1, 0, 0), (1, 0, 1), (0, 1, -1), (0, 1, 0)],
         single=1,
     )
-    lines, *sums = lax.optimization_barrier((lines, *sums))
+    modes, edges = pl.pallas_call(
+        weight_kernel,
+        out_shape=(
+            jax.ShapeDtypeStruct((CX * CY, 2 * LZ, 512), BF16),
+            jax.ShapeDtypeStruct((CX * CY, 32, 512), F32),
+        ),
+        in_specs=[VMEM] * 2,
+        out_specs=(VMEM, VMEM),
+        compiler_params=params(8),
+        cost_estimate=pl.CostEstimate(flops=1 << 28, bytes_accessed=1 << 20, transcendentals=0),
+    )(rows, tz)
+    lines, modes, edges, *sums = lax.optimization_barrier((lines, modes, edges, *sums))
 
     constants = [hbm(tab[name]) for name in ("tx", "ty", "iy", "ix")]
     fields = pl.pallas_call(
@@ -592,18 +603,7 @@
         send(up_before, -1, 1),
     )
 
-    modes, edges = pl.pallas_call(
-        weight_kernel,
-        out_shape=(
-            jax.ShapeDtypeStruct((CX * CY, 2 * LZ, 512), BF16),
-            jax.ShapeDtypeStruct((CX * CY, 32, 512), F32),
-        ),
-        in_specs=[VMEM] * 2,
-        out_specs=(VMEM, VMEM),
-        compiler_params=params(8),
-        cost_estimate=pl.CostEstimate(flops=1 << 28, bytes_accessed=1 << 20, transcendentals=0),
-    )(rows, tz)
-    fields, here, modes, edges = lax.optimization_barrier((fields, here, modes, edges))
+    fields, here = lax.optimization_barrier((fields, here))
     mesh_force = pl.pallas_call(
         force_kernel,
         out_shape=jax.ShapeDtypeStruct((3, CELLS, SLOTS), F32),

time: 78.2 us -> 78.8 us (level)
  starting transfers between devices: 33 us -> 34.8 us
  waiting for transfers between devices: 5.21 us -> 4.13 us
    all_to_all x1, waiting for transfers between devices: 2.85 us -> 1.32 us  [body(): lax.all_to_all(hbm(spread), ('gx', 'gy'), split_axis=0, concat_axis=0, ti...]
    all_to_all x1, starting transfers between devices: 7.34 us -> 8.86 us  [body(): lax.all_to_all(hbm(fields), ('gx', 'gy'), split_axis=0, concat_axis=0, ti...]
  transfers between devices with their start and end apart: 12 -> 12, of which waited for: 3 -> 3; matrix products, arithmetic and copies ran while one was open for 0% -> 0% of each run, Pallas kernels for 38% -> 39%
where the time goes in v10:
time: 78.8 us; the launch traced here: 78.5 us
  Pallas kernels  38.8 us (49%)
  starting transfers between devices  34.8 us (44%)
  waiting for transfers between devices  4.13 us (5%)
    pallas_call x2, Pallas kernels, pair_forces(): pl.pallas_call(functools.partial(pair_kernel, passes=tuple(passes), singl...  20.3 us
    ppermute x10, starting transfers between devices, send(): return lax.ppermute(value, ('gx', 'gy'), route)  17.1 us
    all_to_all x1, starting transfers between devices, body(): lax.all_to_all(hbm(fields), ('gx', 'gy'), split_axis=0, concat_axis=0, ti...  8.86 us
    all_to_all x1, starting transfers between devices, body(): lax.all_to_all(hbm(spread), ('gx', 'gy'), split_axis=0, concat_axis=0, ti...  8.81 us
    pallas_call x1, Pallas kernels, body(): pl.pallas_call(plane_kernel, out_shape=jax.ShapeDtypeStruct((DX * DY, 1,...  6.05 us
    pallas_call x1, Pallas kernels, body(): pl.pallas_call(force_kernel, out_shape=jax.ShapeDtypeStruct((3, CELLS, SL...  4.98 us
    pallas_call x1, Pallas kernels, body(): pl.pallas_call(spread_kernel, out_shape=jax.ShapeDtypeStruct((LZ, 1, BLOC...  3.71 us
    all_to_all x1, waiting for transfers between devices, body(): lax.all_to_all(hbm(fields), ('gx', 'gy'), split_axis=0, concat_axis=0, ti...  1.88 us
  transfers between devices with their start and end apart: 12, of which 3 were waited for; matrix products, arithmetic and copies ran while one was open for 0% of the time, Pallas kernels for 39%

profile of v10, /device:TPU:1, one launch (start us, length us, event | category | flops | bytes accessed | tf_op | source)
XLA Modules:
  0.0 78.5 jit_solution(5030947070839346406)
XLA Ops:
  0.6 1.6 %shard_map.140 = (f32[6,32,128]{2,1,0:T(8,128)S(1)}, f32[6,32,32]{2,1,0:T(8,128)S(1)}, f32[6,32,32]{2,1,0:T(8,128)S(1)}, f32[4,32,128]{2,1,0:T(8,128)S(1)}, bf16[4,128,144]{2,1,0:T(8,128)(2,1)S(1)}) custom-call(f32[3,128,32]{2,1,0:T(8,128)} %bitcast.16, f32[128,32]{1,0:T(8,128)} %bitcast.18, s32[128,32]{1,0:T(8,128)} %bitcast.19, s32[4,2,16]{2,1,0:T(2,128)} %refs_3_.2, ...), custom_call_target="tpu_custom_call" | custom-call | tf_op jit(solution)/shard_map/pallas_call | solution.py:507
  2.3 7.1 %collective-permute-start.2 = (f32[6,32,128]{2,1,0:T(8,128)S(1)}, f32[6,32,128]{2,1,0:T(8,128)S(1)}, u32[]{:S(2)}, u32[]{:S(2)}) collective-permute-start(f32[6,32,128]{2,1,0:T(8,128)S(1)} %get-tuple-element.36.refs_0_), channel_id=1, source_target_pairs={{0,15},{1,0},{2,1},{3,2},{4,3},{5,4},{6,5},{7,6},{8,7},{9,8},{10,9... | collective-permute-start | bytes 294920 | tf_op jit(solution)/shard_map/ppermute | solution.py:500
  9.4 1.0 %collective-permute-start.3 = (f32[6,32,32]{2,1,0:T(8,128)S(1)}, f32[6,32,32]{2,1,0:T(8,128)S(1)}, u32[]{:S(2)}, u32[]{:S(2)}) collective-permute-start(f32[6,32,32]{2,1,0:T(8,128)S(1)} %get-tuple-element.34), channel_id=1, source_target_pairs={{0,127},{1,112},{2,113},{3,114},{4,115},{5,116},{6,117},{7,118},{8... | collective-permute-start | bytes 73736 | tf_op jit(solution)/shard_map/ppermute | solution.py:500
  10.3 1.7 %collective-permute-start = (f32[6,32,32]{2,1,0:T(8,128)S(1)}, f32[6,32,32]{2,1,0:T(8,128)S(1)}, u32[]{:S(2)}, u32[]{:S(2)}) collective-permute-start(f32[6,32,32]{2,1,0:T(8,128)S(1)} %get-tuple-element.34), channel_id=1, source_target_pairs={{0,112},{1,113},{2,114},{3,115},{4,116},{5,117},{6,118},{7,119},{8... | collective-permute-start | bytes 73736 | tf_op jit(solution)/shard_map/ppermute | solution.py:500
  12.1 0.0 collective-permute-start.4
  12.1 0.0 collective-permute-start.1
  12.1 3.7 %shard_map.141 = f32[128,1,768]{2,1,0:T(1,128)} custom-call(f32[4,32,128]{2,1,0:T(8,128)S(1)} %get-tuple-element.32.rows_ref, bf16[4,128,144]{2,1,0:T(8,128)(2,1)S(1)} %get-tuple-element.33.tz_ref, f32[8,128]{1,0:T(8,128)} %constant.15.clone.plane_ref), custom_call_target="tpu_custom_call" | custom-call | tf_op jit(solution)/shard_map/pallas_call | solution.py:543
  15.8 0.9 %collective-permute-done.4.refs_4_ = f32[6,32,32]{2,1,0:T(8,128)S(1)} collective-permute-done((f32[6,32,32]{2,1,0:T(8,128)S(1)}, f32[6,32,32]{2,1,0:T(8,128)S(1)}, u32[]{:S(2)}, u32[]{:S(2)}) %collective-permute-start.4) | collective-permute-done | bytes 24608 | tf_op jit(solution)/shard_map/ppermute | solution.py:500
  16.7 8.8 %all-to-all-start = ((f32[128,1,768]{2,1,0:T(1,128)}), f32[128,1,768]{2,1,0:T(1,128)}, u32[]{:S(2)}, u32[]{:S(2)}) async-start(f32[128,1,768]{2,1,0:T(1,128)} %shard_map.141), calls=%async_computation | async-start | bytes 786432 | tf_op jit(solution)/shard_map/all_to_all | solution.py:560
  25.6 1.2 %shard_map.142 = (bf16[8,256,512]{2,1,0:T(8,128)(2,1)S(1)}, f32[8,32,512]{2,1,0:T(8,128)S(1)}) custom-call(f32[4,32,128]{2,1,0:T(8,128)S(1)} %get-tuple-element.32.rows_ref, bf16[4,128,144]{2,1,0:T(8,128)(2,1)S(1)} %get-tuple-element.33.tz_ref), custom_call_target="tpu_custom_call" | custom-call | flops 268435456 | bytes 1048576 | tf_op jit(solution)/shard_map/pallas_call | solution.py:566
  26.8 9.7 %shard_map.143 = (f32[3,32,256]{2,1,0:T(8,128)S(1)}, f32[3,32,256]{2,1,0:T(8,128)S(1)}) custom-call(f32[6,32,128]{2,1,0:T(8,128)S(1)} %get-tuple-element.36.refs_0_, f32[6,32,32]{2,1,0:T(8,128)S(1)} %collective-permute-done.1.refs_1_, f32[6,32,32]{2,1,0:T(8,128)S(1)} %collective-permute-done.refs_2_, f32[6,32,128]{2,1,0:T(8,128)S(1)} %collective-permute-done.2.refs_3_, ...), custom_call_target="tpu_custom_call" | custom-call | flops 64225280 | bytes 1048576 | tf_op jit(solution)/shard_map/pallas_call | solution.py:461
  36.5 1.3 %all-to-all-done.in_ref = f32[128,1,768]{2,1,0:T(1,128)} async-done(((f32[128,1,768]{2,1,0:T(1,128)}), f32[128,1,768]{2,1,0:T(1,128)}, u32[]{:S(2)}, u32[]{:S(2)}) %all-to-all-start) | async-done | bytes 393248 | tf_op jit(solution)/shard_map/all_to_all | solution.py:560
  37.8 6.1 %shard_map.144 = f32[128,1,2304]{2,1,0:T(1,128)} custom-call(f32[128,1,768]{2,1,0:T(1,128)} %all-to-all-done.in_ref, bf16[1024,256]{1,0:T(8,128)(2,1)} %constant.16.clone.refs_0_, bf16[256,768]{1,0:T(8,128)(2,1)} %constant.17.clone.refs_1_, bf16[640,512]{1,0:T(8,128)(2,1)} %constant.18.clone.refs_2_, bf16[512,576]{1,0:T(8,128)(2,1)} %constant.19.clone.refs_3_), custom_call_target="tpu_custom_call" | custom-call | tf_op jit(solution)/shard_map/pallas_call | solution.py:580
  43.9 0.0 copy-start
  43.9 8.9 %all-to-all-start.1 = ((f32[128,1,2304]{2,1,0:T(1,128)}), f32[128,1,2304]{2,1,0:T(1,128)}, u32[]{:S(2)}, u32[]{:S(2)}) async-start(f32[128,1,2304]{2,1,0:T(1,128)} %shard_map.144), calls=%async_computation.1 | async-start | bytes 2359296 | tf_op jit(solution)/shard_map/all_to_all | solution.py:594
  52.8 10.6 %shard_map.145 = (f32[3,32,128]{2,1,0:T(8,128)S(1)}, f32[3,32,32]{2,1,0:T(8,128)}, f32[3,32,32]{2,1,0:T(8,128)}, f32[3,32,128]{2,1,0:T(8,128)S(1)}, f32[3,32,32]{2,1,0:T(8,128)}, /*index=5*/f32[3,32,32]{2,1,0:T(8,128)}) custom-call(f32[6,32,128]{2,1,0:T(8,128)S(1)} %get-tuple-element.36.refs_0_, f32[6,32,32]{2,1,0:T(8,128)S(1)} %collective-permute-done.1.refs_1_, ...), custom_call_target="tpu_custom_call" | custom-call | flops 64225280 | bytes 1048576 | tf_op jit(solution)/shard_map/pallas_call | solution.py:461
  63.4 1.5 %collective-permute-start.5 = (f32[3,32,128]{2,1,0:T(8,128)S(1)}, f32[3,32,128]{2,1,0:T(8,128)S(1)}, u32[]{:S(2)}, u32[]{:S(2)}) collective-permute-start(f32[3,32,128]{2,1,0:T(8,128)S(1)} %get-tuple-element.56), channel_id=1, source_target_pairs={{0,1},{1,2},{2,3},{3,4},{4,5},{5,6},{6,7},{7,8},{8,9},{9,10},{10,1... | collective-permute-start | bytes 147464 | tf_op jit(solution)/shard_map/ppermute | solution.py:500
  64.9 1.7 %collective-permute-start.6 = (f32[3,32,32]{2,1,0:T(8,128)}, f32[3,32,32]{2,1,0:T(8,128)S(1)}, u32[]{:S(2)}, u32[]{:S(2)}) collective-permute-start(f32[3,32,32]{2,1,0:T(8,128)} %get-tuple-element.57), channel_id=1, source_target_pairs={{0,16},{1,17},{2,18},{3,19},{4,20},{5,21},{6,22},{7,23},{8,24},{9,... | collective-permute-start | bytes 36872 | tf_op jit(solution)/shard_map/ppermute | solution.py:500
  66.6 1.2 %collective-permute-start.7 = (f32[3,32,32]{2,1,0:T(8,128)}, f32[3,32,32]{2,1,0:T(8,128)S(1)}, u32[]{:S(2)}, u32[]{:S(2)}) collective-permute-start(f32[3,32,32]{2,1,0:T(8,128)} %get-tuple-element.58), channel_id=1, source_target_pairs={{0,17},{1,18},{2,19},{3,20},{4,21},{5,22},{6,23},{7,24},{8,25},{9,... | collective-permute-start | bytes 36872 | tf_op jit(solution)/shard_map/ppermute | solution.py:500
  67.8 0.7 collective-permute-start.8
  68.5 2.2 %collective-permute-start.9 = (f32[3,32,32]{2,1,0:T(8,128)}, f32[3,32,32]{2,1,0:T(8,128)S(1)}, u32[]{:S(2)}, u32[]{:S(2)}) collective-permute-start(f32[3,32,32]{2,1,0:T(8,128)} %get-tuple-element.60), channel_id=1, source_target_pairs={{0,113},{1,114},{2,115},{3,116},{4,117},{5,118},{6,119},{7,120},{8... | collective-permute-start | bytes 36872 | tf_op jit(solution)/shard_map/ppermute | solution.py:500
  70.7 1.9 %all-to-all-done.1.in_ref = f32[128,1,2304]{2,1,0:T(1,128)} async-done(((f32[128,1,2304]{2,1,0:T(1,128)}), f32[128,1,2304]{2,1,0:T(1,128)}, u32[]{:S(2)}, u32[]{:S(2)}) %all-to-all-start.1) | async-done | bytes 1179680 | tf_op jit(solution)/shard_map/all_to_all | solution.py:594
  72.6 5.0 %shard_map.146 = f32[3,128,32]{2,1,0:T(8,128)} custom-call(f32[128,1,2304]{2,1,0:T(1,128)} %all-to-all-done.1.in_ref, bf16[8,256,512]{2,1,0:T(8,128)(2,1)S(1)} %get-tuple-element.52.modes_ref, f32[8,32,512]{2,1,0:T(8,128)S(1)} %get-tuple-element.53.edges_ref, f32[1,128]{1,0:T(1,128)S(1)} %copy-done), custom_call_target="tpu_custom_call" | custom-call | tf_op jit(solution)/shard_map/pallas_call | solution.py:607
  77.7 0.9 %shard_map.147 = f32[3,128,32]{2,1,0:T(8,128)} custom-call(f32[3,32,128]{2,1,0:T(8,128)S(1)} %get-tuple-element.55.here_ref, f32[3,32,128]{2,1,0:T(8,128)S(1)} %collective-permute-done.5.down_ref, f32[3,32,32]{2,1,0:T(8,128)S(1)} %collective-permute-done.6.first_a, f32[3,32,32]{2,1,0:T(8,128)S(1)} %collective-permute-done.7.first_b, ...), custom_call_target="tpu_custom_call" | custom-call | tf_op jit(solution)/shard_map/pallas_call | solution.py:622
  (10 shorter events, 0.0 us)
Async XLA Ops:
  2.3 14.5 %collective-permute-start.2 = (f32[6,32,128]{2,1,0:T(8,128)S(1)}, f32[6,32,128]{2,1,0:T(8,128)S(1)}, u32[]{:S(2)}, u32[]{:S(2)}) collective-permute-start(f32[6,32,128]{2,1,0:T(8,128)S(1)} %get-tuple-element.36.refs_0_), channel_id=1, source_target_pairs={{0,15},{1,0},{2,1},{3,2},{4,3},{5,4},{6,5},{7,6},{8,7},{9,8},{10,9... | collective-permute-start | bytes 294920 | tf_op jit(solution)/shard_map/ppermute | solution.py:500
  9.4 6.4 %collective-permute-start.3 = (f32[6,32,32]{2,1,0:T(8,128)S(1)}, f32[6,32,32]{2,1,0:T(8,128)S(1)}, u32[]{:S(2)}, u32[]{:S(2)}) collective-permute-start(f32[6,32,32]{2,1,0:T(8,128)S(1)} %get-tuple-element.34), channel_id=1, source_target_pairs={{0,127},{1,112},{2,113},{3,114},{4,115},{5,116},{6,117},{7,118},{8... | collective-permute-start | bytes 73736 | tf_op jit(solution)/shard_map/ppermute | solution.py:500
  10.3 5.5 %collective-permute-start = (f32[6,32,32]{2,1,0:T(8,128)S(1)}, f32[6,32,32]{2,1,0:T(8,128)S(1)}, u32[]{:S(2)}, u32[]{:S(2)}) collective-permute-start(f32[6,32,32]{2,1,0:T(8,128)S(1)} %get-tuple-element.34), channel_id=1, source_target_pairs={{0,112},{1,113},{2,114},{3,115},{4,116},{5,117},{6,118},{7,119},{8... | collective-permute-start | bytes 73736 | tf_op jit(solution)/shard_map/ppermute | solution.py:500
  12.1 4.7 %collective-permute-start.4 = (f32[6,32,32]{2,1,0:T(8,128)S(1)}, f32[6,32,32]{2,1,0:T(8,128)S(1)}, u32[]{:S(2)}, u32[]{:S(2)}) collective-permute-start(f32[6,32,32]{2,1,0:T(8,128)S(1)} %get-tuple-element.35), channel_id=1, source_target_pairs={{0,31},{1,16},{2,17},{3,18},{4,19},{5,20},{6,21},{7,22},{8,23},{9,... | collective-permute-start | bytes 73736 | tf_op jit(solution)/shard_map/ppermute | solution.py:500
  12.1 4.7 %collective-permute-start.1 = (f32[6,32,32]{2,1,0:T(8,128)S(1)}, f32[6,32,32]{2,1,0:T(8,128)S(1)}, u32[]{:S(2)}, u32[]{:S(2)}) collective-permute-start(f32[6,32,32]{2,1,0:T(8,128)S(1)} %get-tuple-element.35), channel_id=1, source_target_pairs={{0,16},{1,17},{2,18},{3,19},{4,20},{5,21},{6,22},{7,23},{8,24},{9,... | collective-permute-start | bytes 73736 | tf_op jit(solution)/shard_map/ppermute | solution.py:500
  16.7 21.1 %all-to-all-start = ((f32[128,1,768]{2,1,0:T(1,128)}), f32[128,1,768]{2,1,0:T(1,128)}, u32[]{:S(2)}, u32[]{:S(2)}) async-start(f32[128,1,768]{2,1,0:T(1,128)} %shard_map.141), calls=%async_computation | async-start | bytes 786432 | tf_op jit(solution)/shard_map/all_to_all | solution.py:560
  43.9 28.7 %copy-start = (f32[1,128]{1,0:T(1,128)S(1)}, f32[1,128]{1,0:T(1,128)}, u32[]{:S(2)}) copy-start(f32[1,128]{1,0:T(1,128)} %constant.20.clone.swap_ref) | copy-start | bytes 1540
  43.9 28.7 %all-to-all-start.1 = ((f32[128,1,2304]{2,1,0:T(1,128)}), f32[128,1,2304]{2,1,0:T(1,128)}, u32[]{:S(2)}, u32[]{:S(2)}) async-start(f32[128,1,2304]{2,1,0:T(1,128)} %shard_map.144), calls=%async_computation.1 | async-start | bytes 2359296 | tf_op jit(solution)/shard_map/all_to_all | solution.py:594
  63.4 14.2 %collective-permute-start.5 = (f32[3,32,128]{2,1,0:T(8,128)S(1)}, f32[3,32,128]{2,1,0:T(8,128)S(1)}, u32[]{:S(2)}, u32[]{:S(2)}) collective-permute-start(f32[3,32,128]{2,1,0:T(8,128)S(1)} %get-tuple-element.56), channel_id=1, source_target_pairs={{0,1},{1,2},{2,3},{3,4},{4,5},{5,6},{6,7},{7,8},{8,9},{9,10},{10,1... | collective-permute-start | bytes 147464 | tf_op jit(solution)/shard_map/ppermute | solution.py:500
  64.9 12.7 %collective-permute-start.6 = (f32[3,32,32]{2,1,0:T(8,128)}, f32[3,32,32]{2,1,0:T(8,128)S(1)}, u32[]{:S(2)}, u32[]{:S(2)}) collective-permute-start(f32[3,32,32]{2,1,0:T(8,128)} %get-tuple-element.57), channel_id=1, source_target_pairs={{0,16},{1,17},{2,18},{3,19},{4,20},{5,21},{6,22},{7,23},{8,24},{9,... | collective-permute-start | bytes 36872 | tf_op jit(solution)/shard_map/ppermute | solution.py:500
  66.6 11.0 %collective-permute-start.7 = (f32[3,32,32]{2,1,0:T(8,128)}, f32[3,32,32]{2,1,0:T(8,128)S(1)}, u32[]{:S(2)}, u32[]{:S(2)}) collective-permute-start(f32[3,32,32]{2,1,0:T(8,128)} %get-tuple-element.58), channel_id=1, source_target_pairs={{0,17},{1,18},{2,19},{3,20},{4,21},{5,22},{6,23},{7,24},{8,25},{9,... | collective-permute-start | bytes 36872 | tf_op jit(solution)/shard_map/ppermute | solution.py:500
  67.8 9.8 %collective-permute-start.8 = (f32[3,32,32]{2,1,0:T(8,128)}, f32[3,32,32]{2,1,0:T(8,128)S(1)}, u32[]{:S(2)}, u32[]{:S(2)}) collective-permute-start(f32[3,32,32]{2,1,0:T(8,128)} %get-tuple-element.59), channel_id=1, source_target_pairs={{0,112},{1,113},{2,114},{3,115},{4,116},{5,117},{6,118},{7,119},{8... | collective-permute-start | bytes 36872 | tf_op jit(solution)/shard_map/ppermute | solution.py:500
  68.5 9.1 %collective-permute-start.9 = (f32[3,32,32]{2,1,0:T(8,128)}, f32[3,32,32]{2,1,0:T(8,128)S(1)}, u32[]{:S(2)}, u32[]{:S(2)}) collective-permute-start(f32[3,32,32]{2,1,0:T(8,128)} %get-tuple-element.60), channel_id=1, source_target_pairs={{0,113},{1,114},{2,115},{3,116},{4,117},{5,118},{6,119},{7,120},{8... | collective-permute-start | bytes 36872 | tf_op jit(solution)/shard_map/ppermute | solution.py:500
